TPU v7x, 256 devices: a whole 4x4x8 slice. The times are simulated.
256 devices in a mesh: gx: 8 (over z), gy: 32 (over x, y, core).
Axes of the slice: x: 4, y: 4, z: 8, core: 2. Of those that a mesh axis runs over, the one named last changes fastest.
Arguments:
- orbitals: float32 [2, 256, 512, 256], P(None, 'gx', 'gy'), may hold values from -6 to 6
- potential: float32 [256, 512, 256], P('gx', 'gy'), may hold values from -4 to 4
- projectors: float32 [8192, 9, 1024], P(('gx', 'gy')), may hold values from -3 to 3
- strengths: float32 [9], replicated, may hold values from 0.5 to 2
- atom_owner: int32 [5120], replicated, may hold values from 0 to 255, as said below
- slot_atom: int32 [8192], P(('gx', 'gy')), may hold values from 0 to 5120, as said below
- slot_offset: int32 [3, 8192], P(None, ('gx', 'gy')), may hold values from 0 to 240, as said below
Outputs:
- first_filter: float32 [2, 256, 512, 256], P(None, 'gx', 'gy')
- second_filter: float32 [2, 256, 512, 256], P(None, 'gx', 'gy')
Inputs may be any that keep to these rules, and one draw needn't show every extreme that they name: `atom_owner`: every tile owns 1 to 39 atoms, and some tile owns exactly 39. `slot_atom`: every live slot is linked; the first slots of a tile are live and the rest empty; at most 32 live slots a tile, and some tile has empty slots. `slot_offset`: A patch lies within its tile: the first entry is at most 24, the second at most 8, the third at most 240, which some slot reaches.
All inputs are finite; a program needn't handle non-finite values.
Results may differ from a plain program's by a relative error of at most 0.00012.
Values sent between devices are 32-bit elements; how exact they have to be, the bound alone decides.
No kernel may reach another device: no remote copies, remote signals or barrier semaphores. Data moves between devices by JAX's collectives and lax.ppermute only.
A program may use at most 64 MiB of HBM per device.

v0:
```python
import jax
import jax.numpy as jnp
from jax import lax
from jax.experimental import pallas as pl
from jax.experimental.pallas import tpu as pltpu
from jax.sharding import PartitionSpec as P

LAPLACE_COEFFS = (
    -5369.0 / 1800.0,
    12.0 / 7.0,
    -15.0 / 56.0,
    10.0 / 189.0,
    -1.0 / 112.0,
    2.0 / 1925.0,
    -1.0 / 16632.0,
)
SPACING = 0.4
CENTER = 45.0
HALF_WIDTH = 48.0
KINETIC = -0.5 / (SPACING * SPACING)
REACH = 6

ORB = 2
NPROJ = 9
LANES = 128
CX, CY, NZ = 32, 16, 256
SLOTS = 32
ATOMS = 5120
BLOCK = 40
WIDTH = 24
Y_ROWS = ORB * CX * 2 * 8
X_ROWS = ORB * REACH * 2 * CY

VMEM = pl.BlockSpec(memory_space=pltpu.VMEM)
SMEM = pl.BlockSpec(memory_space=pltpu.SMEM)
F32 = jnp.float32


def iota(shape, axis):
    return lax.broadcasted_iota(jnp.int32, shape, axis)


def swap_groups(x):
    row = iota((1, 8, LANES), 1)
    group = iota((1, 8, LANES), 2) // 16
    for d in (4, 2, 1):
        row_bit, group_bit = ((row & d) != 0, (group & d) != 0)
        later = pltpu.roll(pltpu.roll(x, 8 - d, 1), 16 * d, 2)
        if d == 4:
            other = later
        else:
            earlier = pltpu.roll(pltpu.roll(x, d, 1), LANES - 16 * d, 2)
            other = jnp.where(group_bit, later, earlier)
        x = jnp.where(row_bit == group_bit, x, other)
    return x


def corner(offset_ref, slot):
    z = offset_ref[2, slot]
    return offset_ref[0, slot], offset_ref[1, slot], z // LANES, z % LANES


def project(work, proj_ref, offset_ref, atom_ref, part):
    lane = iota((1, 8, LANES), 2)
    group_of_lane = lane // 16
    flat_lane = iota((8, LANES), 1)

    def group_step(g, carry):
        patches = [jnp.zeros((8, 8, LANES), F32) for _ in range(ORB)]
        for i in range(8):
            x, y, half, z = corner(offset_ref, g * 8 + i)
            shift = (16 * i + LANES - z) % LANES
            for o in range(ORB):
                near = work[o, pl.ds(x, 8), half, pl.ds(y, 8), :]
                far = work[o, pl.ds(x, 8), 1, pl.ds(y, 8), :]
                window = pltpu.roll(jnp.where(lane >= z, near, far), shift, 2)
                patches[o] = jnp.where(group_of_lane == i, window, patches[o])
        patches = [swap_groups(patch) for patch in patches]
        tile = jnp.zeros((8, LANES), F32)
        rows = pl.ds(pl.multiple_of(g * 8, 8), 8)
        for p in range(NPROJ):
            values = [proj_ref[p, rows, LANES * a : LANES * (a + 1)] for a in range(8)]
            for o in range(ORB):
                total = values[0] * patches[o][0]
                for a in range(1, 8):
                    total = total + values[a] * patches[o][a]
                summed = jnp.sum(total, axis=1, keepdims=True)
                tile = jnp.where(flat_lane == 2 * p + o, summed, tile)
        part[rows, :] = tile
        return carry

    lax.fori_loop(0, SLOTS // 8, group_step, 0)
    atoms = jnp.full((8, LANES), -2.0, F32)
    first = iota((8, LANES), 0) == 0
    for s in range(SLOTS):
        atoms = jnp.where(first & (flat_lane == s), atom_ref[s].astype(F32), atoms)
    part[SLOTS:BLOCK, :] = atoms


def pack(work, part, y_up, y_down, x_up, x_down):
    for o in range(ORB):
        rows = slice(o * CX * 16, (o + 1) * CX * 16)
        y_up[rows, :] = work[o, :, :, 8:16, :].reshape(CX * 16, LANES)
        y_down[rows, :] = work[o, :, :, 0:8, :].reshape(CX * 16, LANES)
        rows = slice(o * REACH * 32, (o + 1) * REACH * 32)
        x_up[rows, :] = work[o, CX - REACH : CX].reshape(REACH * 32, LANES)
        x_down[rows, :] = work[o, 0:REACH].reshape(REACH * 32, LANES)
    y_up[Y_ROWS:, :] = part[...]
    y_down[Y_ROWS:, :] = part[...]


def first_kernel(v, proj_ref, offset_ref, atom_ref, y_up, y_down, x_up, x_down, part, work):
    for half in range(2):
        work[:, :, half] = v[:, :, :, LANES * half : LANES * (half + 1)]
    project(work, proj_ref, offset_ref, atom_ref, part)
    pack(work, part, y_up, y_down, x_up, x_down)


def local_kernel(scale, subtract, *refs):
    if subtract:
        v, potential, before, after, orbital, out, pad, along_z = refs
    else:
        v, potential, before, after, out, pad, along_z = refs
    weights = [scale * KINETIC / HALF_WIDTH * w for w in LAPLACE_COEFFS]

    gap = jnp.abs(iota((NZ, NZ), 0) - iota((NZ, NZ), 1))
    band = jnp.zeros((NZ, NZ), F32)
    for r in range(1, REACH + 1):
        band = jnp.where(gap == r, weights[r], band)
    along_z[...] = jnp.dot(
        v[...].reshape(ORB * CX * CY, NZ),
        band,
        precision=lax.Precision.HIGHEST,
        preferred_element_type=F32,
    )

    for o in range(ORB):
        for x in range(REACH):
            pad[o, x, :, 8:24, :] = jnp.zeros((2, CY, LANES), F32)
            pad[o, x + REACH + CX, :, 8:24, :] = jnp.zeros((2, CY, LANES), F32)
        rows = slice(o * CX * 16, (o + 1) * CX * 16)
        pad[o, REACH : REACH + CX, :, 0:8, :] = before[rows, :].reshape(CX, 2, 8, LANES)
        pad[o, REACH : REACH + CX, :, 24:32, :] = after[rows, :].reshape(CX, 2, 8, LANES)
        for half in range(2):
            pad[o, REACH : REACH + CX, half, 8:24, :] = v[
                o, :, :, LANES * half : LANES * (half + 1)
            ]

    def step(n, carry):
        o, x = (n // CX, n % CX)
        for half in range(2):
            lanes = slice(LANES * half, LANES * (half + 1))
            for t in range(2):
                rows = slice(8 + 8 * t, 16 + 8 * t)
                here = pad[o, x + REACH, half, rows, :]
                factor = potential[x, 8 * t : 8 * t + 8, lanes] * (scale / HALF_WIDTH) + (
                    3.0 * weights[0] - scale * CENTER / HALF_WIDTH
                )
                total = factor * here
                depth = pl.ds(pl.multiple_of(n * CY + 8 * t, 8), 8)
                total = total + along_z[depth, lanes]
                for r in range(1, REACH + 1):
                    paired = (
                        pad[o, x + REACH + r, half, rows, :] + pad[o, x + REACH - r, half, rows, :]
                    )
                    paired = paired + (
                        pad[o, x + REACH, half, 8 + 8 * t + r : 16 + 8 * t + r, :]
                        + pad[o, x + REACH, half, 8 + 8 * t - r : 16 + 8 * t - r, :]
                    )
                    total = total + weights[r] * paired
                if subtract:
                    total = total - orbital[o, x, 8 * t : 8 * t + 8, lanes]
                out[o, x, half, 8 * t : 8 * t + 8, :] = total
        return carry

    lax.fori_loop(0, ORB * CX, step, 0)


def coefficients(tiles, atom_ref):
    row = iota((SLOTS, LANES), 0)
    own = jnp.full((SLOTS, LANES), -1.0, F32)
    for s in range(SLOTS):
        atom = jnp.where(atom_ref[s] < ATOMS, atom_ref[s], -1)
        own = jnp.where(row == s, atom.astype(F32), own)
    result = jnp.zeros((5 * SLOTS, 3 * LANES), F32)
    for tile, start in tiles:
        values = tile[start : start + SLOTS, :]
        high = values.astype(jnp.bfloat16)
        rest = values - high.astype(F32)
        middle = rest.astype(jnp.bfloat16)
        low = (rest - middle.astype(F32)).astype(jnp.bfloat16)
        same = [
            jnp.where(
                own[:, :SLOTS] == tile[start + SLOTS + k : start + SLOTS + k + 1, :SLOTS], 1.0, 0.0
            )
            for k in range(5)
        ]
        same = jnp.concatenate(same, axis=0).astype(jnp.bfloat16)
        result = result + jnp.dot(
            same, jnp.concatenate([high, middle, low], axis=1), preferred_element_type=F32
        )
    result = result[:, :LANES] + result[:, LANES : 2 * LANES] + result[:, 2 * LANES :]
    total = result[:SLOTS]
    for k in range(1, 5):
        total = total + pltpu.roll(result[SLOTS * k : SLOTS * (k + 1)], LANES - WIDTH * k, 1)
    return total


def finish(scale, local, before, after, two_up, two_down, own_block, proj_ref, strength_ref,
           offset_ref, atom_ref, work, table):
    weights = [scale * KINETIC / HALF_WIDTH * w for w in LAPLACE_COEFFS]
    table[...] = coefficients(
        ((own_block, 0), (before, X_ROWS), (after, X_ROWS), (two_up, 0), (two_down, 0)), atom_ref
    )
    work[:, REACH : CX - REACH] = local[:, REACH : CX - REACH]
    for o in range(ORB):
        for j in range(REACH):
            low = local[o, j]
            for i in range(j, REACH):
                rows = slice((o * REACH + i) * 32, (o * REACH + i + 1) * 32)
                low = low + weights[j + REACH - i] * before[rows, :].reshape(2, CY, LANES)
            work[o, j] = low
            high = local[o, CX - REACH + j]
            for i in range(j + 1):
                rows = slice((o * REACH + i) * 32, (o * REACH + i + 1) * 32)
                high = high + weights[REACH + i - j] * after[rows, :].reshape(2, CY, LANES)
            work[o, CX - REACH + j] = high

    lane = iota((1, 8, LANES), 2)

    def group_step(g, carry):
        rows = pl.ds(pl.multiple_of(g * 8, 8), 8)
        held = table[rows, :]
        added = [[None] * 8 for _ in range(ORB)]
        for p in range(NPROJ):
            strength = strength_ref[p] * (scale / HALF_WIDTH)
            spread = [
                jnp.broadcast_to(held[:, 2 * p + o : 2 * p + o + 1], (8, LANES)) * strength
                for o in range(ORB)
            ]
            for a in range(8):
                values = proj_ref[p, rows, LANES * a : LANES * (a + 1)]
                for o in range(ORB):
                    term = values * spread[o]
                    added[o][a] = term if p == 0 else added[o][a] + term
        patches = [swap_groups(jnp.stack(added[o])) for o in range(ORB)]
        for i in range(8):
            x, y, half, z = corner(offset_ref, g * 8 + i)
            shift = (z + LANES - 16 * i) % LANES
            moved = [pltpu.roll(patches[o], shift, 2) for o in range(ORB)]
            inside = (lane >= z) & (lane < z + 16)
            for o in range(ORB):
                place = (o, pl.ds(x, 8), half, pl.ds(y, 8), slice(None))
                work[place] = work[place] + jnp.where(inside, moved[o], 0.0)

            @pl.when(z > LANES - 16)
            def _():
                for o in range(ORB):
                    place = (o, pl.ds(x, 8), 1, pl.ds(y, 8), slice(None))
                    work[place] = work[place] + jnp.where(lane < z + 16 - LANES, moved[o], 0.0)

        return carry

    lax.fori_loop(0, SLOTS // 8, group_step, 0)


def unsplit(work, out):
    for half in range(2):
        out[:, :, :, LANES * half : LANES * (half + 1)] = work[:, :, half]


def middle_kernel(scale, local, before, after, two_up, two_down, own_block, proj_ref, strength_ref,
                  offset_ref, atom_ref, out, y_up, y_down, x_up, x_down, part, work, table):
    finish(scale, local, before, after, two_up, two_down, own_block, proj_ref, strength_ref,
           offset_ref, atom_ref, work, table)
    project(work, proj_ref, offset_ref, atom_ref, part)
    pack(work, part, y_up, y_down, x_up, x_down)
    unsplit(work, out)


def last_kernel(scale, local, before, after, two_up, two_down, own_block, proj_ref, strength_ref,
                offset_ref, atom_ref, out, work, table):
    finish(scale, local, before, after, two_up, two_down, own_block, proj_ref, strength_ref,
           offset_ref, atom_ref, work, table)
    unsplit(work, out)


def shaped(*shape):
    return jax.ShapeDtypeStruct(shape, F32)


PARAMS = pltpu.CompilerParams(vmem_limit_bytes=32 * 1024 * 1024)
FIELD = (ORB, CX, CY, NZ)
WORK = (ORB, CX, 2, CY, LANES)
SENT = (
    shaped(Y_ROWS + BLOCK, LANES),
    shaped(Y_ROWS + BLOCK, LANES),
    shaped(X_ROWS + BLOCK, LANES),
    shaped(X_ROWS + BLOCK, LANES),
    shaped(BLOCK, LANES),
)


def shift(value, axis, step):
    devices = lax.axis_size(axis)
    return lax.ppermute(value, axis, [(i, (i + step) % devices) for i in range(devices)])


def local_part(scale, field, potential, before, after, orbital):
    subtract = orbital is not None
    args = (field, potential, before, after) + ((orbital,) if subtract else ())

    def body(*refs):
        local_kernel(scale, subtract, *refs)

    return pl.pallas_call(
        body,
        out_shape=shaped(*WORK),
        in_specs=[VMEM] * len(args),
        out_specs=VMEM,
        scratch_shapes=[
            pltpu.VMEM((ORB, CX + 2 * REACH, 2, 32, LANES), F32),
            pltpu.VMEM((ORB * CX * CY, NZ), F32),
        ],
        compiler_params=PARAMS,
        name="local_part",
    )(*args)


def apply(scale, field, potential, sent, orbital, shared, last):
    y_up, y_down, x_up, x_down, part = sent
    projectors, strengths, offsets, atoms = shared
    y_before = shift(y_up, "gy", 1)
    y_after = shift(y_down, "gy", -1)
    y_two_before = shift(part, "gy", 2)
    y_two_after = shift(part, "gy", -2)
    tiles = (y_two_before, y_before[Y_ROWS:], part, y_after[Y_ROWS:], y_two_after)
    sums = jnp.concatenate(
        [tile[:SLOTS, :WIDTH] for tile in tiles] + [jnp.zeros((SLOTS, LANES - 5 * WIDTH), F32)],
        axis=1,
    )
    block = jnp.concatenate(
        [sums] + [tile[SLOTS : SLOTS + 1] for tile in tiles] + [tiles[0][SLOTS + 1 : SLOTS + 4]],
        axis=0,
    )
    x_up = lax.dynamic_update_slice(x_up, block, (X_ROWS, 0))
    x_down = lax.dynamic_update_slice(x_down, block, (X_ROWS, 0))
    x_before = shift(x_up, "gx", 1)
    x_after = shift(x_down, "gx", -1)
    x_two_before = shift(block, "gx", 2)
    x_two_after = shift(block, "gx", -2)
    local = local_part(scale, field, potential, y_before, y_after, orbital)
    kernel = last_kernel if last else middle_kernel

    def body(*refs):
        kernel(scale, *refs)

    return pl.pallas_call(
        body,
        out_shape=shaped(*FIELD) if last else (shaped(*FIELD),) + SENT,
        in_specs=[VMEM] * 7 + [SMEM] * 3,
        out_specs=VMEM if last else (VMEM,) * 6,
        scratch_shapes=[pltpu.VMEM(WORK, F32), pltpu.VMEM((SLOTS, LANES), F32)],
        compiler_params=PARAMS,
        name="last_part" if last else "middle_part",
    )(local, x_before, x_after, x_two_before, x_two_after, block, projectors, strengths, offsets, atoms)


def shards(orbitals, potential, projectors, strengths, atom_owner, slot_atom, slot_offset):
    projectors = jnp.transpose(projectors, (1, 0, 2))
    shared = (projectors, strengths, slot_offset, slot_atom)
    sent = pl.pallas_call(
        first_kernel,
        out_shape=SENT,
        in_specs=[VMEM, VMEM, SMEM, SMEM],
        out_specs=(VMEM,) * 5,
        scratch_shapes=[pltpu.VMEM(WORK, F32)],
        compiler_params=PARAMS,
        name="first_part",
    )(orbitals, projectors, slot_offset, slot_atom)
    first_filter, *sent = apply(1.0, orbitals, potential, sent, None, shared, False)
    second_filter = apply(2.0, first_filter, potential, sent, orbitals, shared, True)
    return (first_filter, second_filter)


def solution(mesh):
    return jax.shard_map(
        shards,
        mesh=mesh,
        in_specs=(
            P(None, "gx", "gy", None),
            P("gx", "gy", None),
            P(("gx", "gy"), None, None),
            P(),
            P(),
            P(("gx", "gy")),
            P(None, ("gx", "gy")),
        ),
        out_specs=(P(None, "gx", "gy", None), P(None, "gx", "gy", None)),
        check_vma=False,
    )
```

profile of v0, /device:TPU:30, one launch (start us, length us, event | category | flops | bytes accessed | tf_op | source)
XLA Modules:
  0.0 90.5 jit_solution(16329643522826408465)
XLA Ops:
  0.6 1.3 %copy-done = f32[32,9,1024]{2,0,1:T(8,128)S(1)} copy-done((f32[32,9,1024]{2,0,1:T(8,128)S(1)}, f32[32,9,1024]{2,0,1:T(8,128)}, u32[]{:S(2)}) %copy-start) | copy-done | bytes 1179672
  1.9 1.2 %copy-done.2 = f32[2,32,16,256]{3,2,1,0:T(8,128)S(1)} copy-done((f32[2,32,16,256]{3,2,1,0:T(8,128)S(1)}, f32[2,32,16,256]{3,2,1,0:T(8,128)}, u32[]{:S(2)}) %copy-start.2) | copy-done | bytes 1048600
  4.5 3.0 %first_part.1 = (f32[1064,128]{1,0:T(8,128)S(1)}, f32[1064,128]{1,0:T(8,128)S(1)}, f32[424,128]{1,0:T(8,128)S(1)}, f32[424,128]{1,0:T(8,128)S(1)}, f32[40,128]{1,0:T(8,128)S(1)}) custom-call(f32[2,32,16,256]{3,2,1,0:T(8,128)S(1)} %copy-done.2, f32[9,32,1024]{2,1,0:T(8,128)S(1)} %bitcast.1, s32[3,32]{1,0:T(4,128)S(1)} %copy-done.10, s32[32]{0:T(128)S(1)} %copy-done.12), custom_call_target="tpu_custom_call" | custom-call | tf_op jit(solution)/shard_map/first_part/pallas_call | solution.py:372
  8.1 1.7 %collective-permute-start.1 = (f32[1064,128]{1,0:T(8,128)S(1)}, f32[1064,128]{1,0:T(8,128)S(1)}, u32[]{:S(2)}, u32[]{:S(2)}) collective-permute-start(f32[1064,128]{1,0:T(8,128)S(1)} %get-tuple-element.14), channel_id=1, source_target_pairs={{0,31},{1,0},{2,1},{3,2},{4,3},{5,4},{6,5},{7,6},{8,7},{9,8},{10,9... | collective-permute-start | bytes 1634312 | tf_op jit(solution)/shard_map/ppermute | solution.py:306
  10.6 4.6 %collective-permute-start.2 = (f32[40,128]{1,0:T(8,128)S(1)}, f32[40,128]{1,0:T(8,128)S(1)}, u32[]{:S(2)}, u32[]{:S(2)}) collective-permute-start(f32[40,128]{1,0:T(8,128)S(1)} %get-tuple-element.16), channel_id=1, source_target_pairs={{0,2},{1,3},{2,4},{3,5},{4,6},{5,7},{6,8},{7,9},{8,10},{9,11},{10,... | collective-permute-start | bytes 61448 | tf_op jit(solution)/shard_map/ppermute | solution.py:306
  15.2 7.4 %collective-permute-done.3 = f32[40,128]{1,0:T(8,128)S(1)} collective-permute-done((f32[40,128]{1,0:T(8,128)S(1)}, f32[40,128]{1,0:T(8,128)S(1)}, u32[]{:S(2)}, u32[]{:S(2)}) %collective-permute-start.3) | collective-permute-done | bytes 20512 | tf_op jit(solution)/shard_map/ppermute | solution.py:306
  25.5 4.1 %collective-permute-start.5 = (f32[424,128]{1,0:T(8,128)}, f32[424,128]{1,0:T(8,128)S(1)}, u32[]{:S(2)}, u32[]{:S(2)}) collective-permute-start(f32[424,128]{1,0:T(8,128)} %get-tuple-element.26), channel_id=1, source_target_pairs={{0,224},{32,0},{64,32},{96,64},{128,96},{160,128},{192,160},{224,1... | collective-permute-start | bytes 651272 | tf_op jit(solution)/shard_map/ppermute | solution.py:306
  29.7 2.5 %collective-permute-start.7 = (f32[40,128]{1,0:T(8,128)S(1)}, f32[40,128]{1,0:T(8,128)S(1)}, u32[]{:S(2)}, u32[]{:S(2)}) collective-permute-start(f32[40,128]{1,0:T(8,128)S(1)} %concatenate.13.refs_5_), channel_id=1, source_target_pairs={{0,192},{32,224},{64,0},{96,32},{128,64},{160,96},{192,128},{224,1... | collective-permute-start | bytes 61448 | tf_op jit(solution)/shard_map/ppermute | solution.py:306
  32.7 1.0 %copy-done.7 = f32[1064,128]{1,0:T(8,128)S(1)} copy-done((f32[1064,128]{1,0:T(8,128)S(1)}, f32[1064,128]{1,0:T(8,128)}, u32[]{:S(2)}) %copy-start.7) | copy-done | bytes 544792
  33.8 3.8 %local_part.2.refs_0_ = f32[2,32,2,16,128]{4,3,2,1,0:T(8,128)S(1)} custom-call(f32[2,32,16,256]{3,2,1,0:T(8,128)S(1)} %copy-done.3, f32[32,16,256]{2,1,0:T(8,128)S(1)} %copy-done.4, f32[1064,128]{1,0:T(8,128)S(1)} %collective-permute-done.refs_2_, f32[1064,128]{1,0:T(8,128)S(1)} %copy-done.7), custom_call_target="tpu_custom_call" | custom-call | tf_op jit(solution)/shard_map/local_part/pallas_call | solution.py:316
  38.2 8.7 %middle_part.1 = (f32[2,32,16,256]{3,2,1,0:T(8,128)}, f32[1064,128]{1,0:T(8,128)S(1)}, f32[1064,128]{1,0:T(8,128)S(1)}, f32[424,128]{1,0:T(8,128)S(1)}, f32[424,128]{1,0:T(8,128)S(1)}, /*index=5*/f32[40,128]{1,0:T(8,128)S(1)}) custom-call(f32[2,32,2,16,128]{4,3,2,1,0:T(8,128)S(1)} %local_part.2.refs_0_, f32[424,128]{1,0:T(8,128)S(1)} %collective-permute-done.4.refs_1_, ...), custom_call_target="tpu_custom_call" | custom-call | tf_op jit(solution)/shard_map/middle_part/pallas_call | solution.py:358
  47.5 1.7 %collective-permute-start.9 = (f32[1064,128]{1,0:T(8,128)S(1)}, f32[1064,128]{1,0:T(8,128)S(1)}, u32[]{:S(2)}, u32[]{:S(2)}) collective-permute-start(f32[1064,128]{1,0:T(8,128)S(1)} %get-tuple-element.20), channel_id=1, source_target_pairs={{0,31},{1,0},{2,1},{3,2},{4,3},{5,4},{6,5},{7,6},{8,7},{9,8},{10,9... | collective-permute-start | bytes 1634312 | tf_op jit(solution)/shard_map/ppermute | solution.py:306
  49.3 5.3 %collective-permute-start.10 = (f32[40,128]{1,0:T(8,128)S(1)}, f32[40,128]{1,0:T(8,128)S(1)}, u32[]{:S(2)}, u32[]{:S(2)}) collective-permute-start(f32[40,128]{1,0:T(8,128)S(1)} %get-tuple-element.22), channel_id=1, source_target_pairs={{0,2},{1,3},{2,4},{3,5},{4,6},{5,7},{6,8},{7,9},{8,10},{9,11},{10,... | collective-permute-start | bytes 61448 | tf_op jit(solution)/shard_map/ppermute | solution.py:306
  54.6 6.9 %collective-permute-done.11 = f32[40,128]{1,0:T(8,128)S(1)} collective-permute-done((f32[40,128]{1,0:T(8,128)S(1)}, f32[40,128]{1,0:T(8,128)S(1)}, u32[]{:S(2)}, u32[]{:S(2)}) %collective-permute-start.11) | collective-permute-done | bytes 20512 | tf_op jit(solution)/shard_map/ppermute | solution.py:306
  65.9 1.5 %concatenate.14 = f32[32,128]{1,0:T(8,128)} concatenate(f32[32,24]{1,0:T(8,128)} %slice.109, f32[32,24]{1,0:T(8,128)} %slice.110, f32[32,24]{1,0:T(8,128)S(1)} %slice.91, f32[32,24]{1,0:T(8,128)} %slice.111, f32[32,24]{1,0:T(8,128)} %slice.112, f32[32,8]{1,0:T(8,128)} %copy-done.17), dimensions={1} | concatenate | bytes 32768 | tf_op jit(solution)/shard_map/concatenate | solution.py:338
  67.9 1.2 %slice.115 = f32[1,128]{1,0:T(1,128)} slice(f32[1064,128]{1,0:T(8,128)} %copy-done.8), slice={[1056:1057], [0:128]} | slice | bytes 1024 | tf_op jit(solution)/shard_map/slice | solution.py:343
  69.1 1.4 %concatenate.15.refs_5_ = f32[40,128]{1,0:T(8,128)S(1)} concatenate(f32[32,128]{1,0:T(8,128)} %concatenate.14, f32[1,128]{1,0:T(1,128)} %slice.113, f32[1,128]{1,0:T(1,128)} %slice.114, f32[1,128]{1,0:T(1,128)S(1)} %slice.96, f32[1,128]{1,0:T(1,128)} %slice.115, f32[1,128]{1,0:T(1,128)} %slice.116, f32[3,128]{1,0:T(4,128)S(1)} %slice.117), dimensions={0} | concatenate | bytes 40960 | tf_op jit(solution)/shard_map/concatenate | solution.py:342
  71.1 3.9 %collective-permute-start.13 = (f32[424,128]{1,0:T(8,128)}, f32[424,128]{1,0:T(8,128)S(1)}, u32[]{:S(2)}, u32[]{:S(2)}) collective-permute-start(f32[424,128]{1,0:T(8,128)} %get-tuple-element.24), channel_id=1, source_target_pairs={{0,224},{32,0},{64,32},{96,64},{128,96},{160,128},{192,160},{224,1... | collective-permute-start | bytes 651272 | tf_op jit(solution)/shard_map/ppermute | solution.py:306
  75.0 1.5 %collective-permute-start.15 = (f32[40,128]{1,0:T(8,128)S(1)}, f32[40,128]{1,0:T(8,128)S(1)}, u32[]{:S(2)}, u32[]{:S(2)}) collective-permute-start(f32[40,128]{1,0:T(8,128)S(1)} %concatenate.15.refs_5_), channel_id=1, source_target_pairs={{0,192},{32,224},{64,0},{96,32},{128,64},{160,96},{192,128},{224,1... | collective-permute-start | bytes 61448 | tf_op jit(solution)/shard_map/ppermute | solution.py:306
  76.5 1.5 %collective-permute-start.14 = (f32[40,128]{1,0:T(8,128)S(1)}, f32[40,128]{1,0:T(8,128)S(1)}, u32[]{:S(2)}, u32[]{:S(2)}) collective-permute-start(f32[40,128]{1,0:T(8,128)S(1)} %concatenate.15.refs_5_), channel_id=1, source_target_pairs={{0,64},{32,96},{64,128},{96,160},{128,192},{160,224},{192,0},{224,... | collective-permute-start | bytes 61448 | tf_op jit(solution)/shard_map/ppermute | solution.py:306
  77.9 1.2 %copy-done.5 = f32[2,32,16,256]{3,2,1,0:T(8,128)S(1)} copy-done((f32[2,32,16,256]{3,2,1,0:T(8,128)S(1)}, f32[2,32,16,256]{3,2,1,0:T(8,128)}, u32[]{:S(2)}) %copy-start.5) | copy-done | bytes 1048600
  79.2 1.0 %copy-done.9 = f32[1064,128]{1,0:T(8,128)S(1)} copy-done((f32[1064,128]{1,0:T(8,128)S(1)}, f32[1064,128]{1,0:T(8,128)}, u32[]{:S(2)}) %copy-start.9) | copy-done | bytes 544792
  80.2 3.8 %local_part.3.refs_0_ = f32[2,32,2,16,128]{4,3,2,1,0:T(8,128)S(1)} custom-call(f32[2,32,16,256]{3,2,1,0:T(8,128)S(1)} %copy-done.5, f32[32,16,256]{2,1,0:T(8,128)S(1)} %copy-done.4, f32[1064,128]{1,0:T(8,128)S(1)} %collective-permute-done.8.refs_2_, f32[1064,128]{1,0:T(8,128)S(1)} %copy-done.9, f32[2,32,16,256]{3,2,1,0:T(8,128)S(1)} %copy-done.3), custom_call_target="tpu_custom_call" | custom-call | tf_op jit(solution)/shard_map/local_part/pallas_call | solution.py:316
  84.1 6.4 %last_part.1 = f32[2,32,16,256]{3,2,1,0:T(8,128)} custom-call(f32[2,32,2,16,128]{4,3,2,1,0:T(8,128)S(1)} %local_part.3.refs_0_, f32[424,128]{1,0:T(8,128)S(1)} %collective-permute-done.12.refs_1_, f32[424,128]{1,0:T(8,128)S(1)} %collective-permute-done.13.refs_2_, f32[40,128]{1,0:T(8,128)S(1)} %collective-permute-done.14.refs_3_, ...), custom_call_target="tpu_custom_call" | custom-call | tf_op jit(solution)/shard_map/last_part/pallas_call | solution.py:358
  (78 shorter events, 12.8 us)
Async XLA Ops:
  0.6 1.3 %copy-start = (f32[32,9,1024]{2,0,1:T(8,128)S(1)}, f32[32,9,1024]{2,0,1:T(8,128)}, u32[]{:S(2)}) copy-start(f32[32,9,1024]{2,0,1:T(8,128)} %param.9) | copy-start | bytes 3538948
  4.5 28.3 %copy-start.3 = (f32[2,32,16,256]{3,2,1,0:T(8,128)S(1)}, f32[2,32,16,256]{3,2,1,0:T(8,128)}, u32[]{:S(2)}) copy-start(f32[2,32,16,256]{3,2,1,0:T(8,128)} %refs_4_.1) | copy-start | bytes 3145732
  4.5 28.3 %copy-start.4 = (f32[32,16,256]{2,1,0:T(8,128)S(1)}, f32[32,16,256]{2,1,0:T(8,128)}, u32[]{:S(2)}) copy-start(f32[32,16,256]{2,1,0:T(8,128)} %refs_1_.3) | copy-start | bytes 1572868
  8.1 15.1 %collective-permute-start = (f32[1064,128]{1,0:T(8,128)S(1)}, f32[1064,128]{1,0:T(8,128)S(1)}, u32[]{:S(2)}, u32[]{:S(2)}) collective-permute-start(f32[1064,128]{1,0:T(8,128)S(1)} %get-tuple-element.13), channel_id=1, source_target_pairs={{0,1},{1,2},{2,3},{3,4},{4,5},{5,6},{6,7},{7,8},{8,9},{9,10},{10,1... | collective-permute-start | bytes 1634312 | tf_op jit(solution)/shard_map/ppermute | solution.py:306
  8.1 15.1 %collective-permute-start.1 = (f32[1064,128]{1,0:T(8,128)S(1)}, f32[1064,128]{1,0:T(8,128)S(1)}, u32[]{:S(2)}, u32[]{:S(2)}) collective-permute-start(f32[1064,128]{1,0:T(8,128)S(1)} %get-tuple-element.14), channel_id=1, source_target_pairs={{0,31},{1,0},{2,1},{3,2},{4,3},{5,4},{6,5},{7,6},{8,7},{9,8},{10,9... | collective-permute-start | bytes 1634312 | tf_op jit(solution)/shard_map/ppermute | solution.py:306
  9.9 12.8 %collective-permute-start.3 = (f32[40,128]{1,0:T(8,128)S(1)}, f32[40,128]{1,0:T(8,128)S(1)}, u32[]{:S(2)}, u32[]{:S(2)}) collective-permute-start(f32[40,128]{1,0:T(8,128)S(1)} %get-tuple-element.16), channel_id=1, source_target_pairs={{0,30},{1,31},{2,0},{3,1},{4,2},{5,3},{6,4},{7,5},{8,6},{9,7},{10,... | collective-permute-start | bytes 61448 | tf_op jit(solution)/shard_map/ppermute | solution.py:306
  10.6 12.1 %collective-permute-start.2 = (f32[40,128]{1,0:T(8,128)S(1)}, f32[40,128]{1,0:T(8,128)S(1)}, u32[]{:S(2)}, u32[]{:S(2)}) collective-permute-start(f32[40,128]{1,0:T(8,128)S(1)} %get-tuple-element.16), channel_id=1, source_target_pairs={{0,2},{1,3},{2,4},{3,5},{4,6},{5,7},{6,8},{7,9},{8,10},{9,11},{10,... | collective-permute-start | bytes 61448 | tf_op jit(solution)/shard_map/ppermute | solution.py:306
  23.3 6.3 %copy-start.17 = (f32[32,8]{1,0:T(8,128)}, f32[32,8]{1,0:T(8,128)S(1)}, u32[]{:S(2)}) copy-start(f32[32,8]{1,0:T(8,128)S(1)} %broadcast.3) | copy-start | bytes 3076
  25.5 12.6 %collective-permute-start.5 = (f32[424,128]{1,0:T(8,128)}, f32[424,128]{1,0:T(8,128)S(1)}, u32[]{:S(2)}, u32[]{:S(2)}) collective-permute-start(f32[424,128]{1,0:T(8,128)} %get-tuple-element.26), channel_id=1, source_target_pairs={{0,224},{32,0},{64,32},{96,64},{128,96},{160,128},{192,160},{224,1... | collective-permute-start | bytes 651272 | tf_op jit(solution)/shard_map/ppermute | solution.py:306
  29.6 8.5 %copy-start.13 = (s32[32]{0:T(128)S(1)}, s32[32]{0:T(128)}, u32[]{:S(2)}) copy-start(s32[32]{0:T(128)} %refs_9_.3) | copy-start | bytes 388
  29.6 8.5 %copy-start.14 = (f32[9]{0:T(128)S(1)}, f32[9]{0:T(128)}, u32[]{:S(2)}) copy-start(f32[9]{0:T(128)} %refs_7_.3) | copy-start | bytes 112
  29.6 8.5 %copy-start.1 = (f32[32,9,1024]{2,0,1:T(8,128)S(1)}, f32[32,9,1024]{2,0,1:T(8,128)}, u32[]{:S(2)}) copy-start(f32[32,9,1024]{2,0,1:T(8,128)} %param.9) | copy-start | bytes 3538948
  29.6 8.5 %collective-permute-start.4 = (f32[424,128]{1,0:T(8,128)S(1)}, f32[424,128]{1,0:T(8,128)S(1)}, u32[]{:S(2)}, u32[]{:S(2)}) collective-permute-start(f32[424,128]{1,0:T(8,128)S(1)} %get-tuple-element.27), channel_id=1, source_target_pairs={{0,32},{32,64},{64,96},{96,128},{128,160},{160,192},{192,224},{224... | collective-permute-start | bytes 651272 | tf_op jit(solution)/shard_map/ppermute | solution.py:306
  29.7 7.9 %collective-permute-start.7 = (f32[40,128]{1,0:T(8,128)S(1)}, f32[40,128]{1,0:T(8,128)S(1)}, u32[]{:S(2)}, u32[]{:S(2)}) collective-permute-start(f32[40,128]{1,0:T(8,128)S(1)} %concatenate.13.refs_5_), channel_id=1, source_target_pairs={{0,192},{32,224},{64,0},{96,32},{128,64},{160,96},{192,128},{224,1... | collective-permute-start | bytes 61448 | tf_op jit(solution)/shard_map/ppermute | solution.py:306
  32.2 5.9 %collective-permute-start.6 = (f32[40,128]{1,0:T(8,128)S(1)}, f32[40,128]{1,0:T(8,128)S(1)}, u32[]{:S(2)}, u32[]{:S(2)}) collective-permute-start(f32[40,128]{1,0:T(8,128)S(1)} %concatenate.13.refs_5_), channel_id=1, source_target_pairs={{0,64},{32,96},{64,128},{96,160},{128,192},{160,224},{192,0},{224,... | collective-permute-start | bytes 61448 | tf_op jit(solution)/shard_map/ppermute | solution.py:306
  33.8 4.4 %copy-start.11 = (s32[3,32]{1,0:T(4,128)S(1)}, s32[3,32]{1,0:T(4,128)}, u32[]{:S(2)}) copy-start(s32[3,32]{1,0:T(4,128)} %refs_8_.3) | copy-start | bytes 1156
  47.5 16.3 %collective-permute-start.8 = (f32[1064,128]{1,0:T(8,128)S(1)}, f32[1064,128]{1,0:T(8,128)S(1)}, u32[]{:S(2)}, u32[]{:S(2)}) collective-permute-start(f32[1064,128]{1,0:T(8,128)S(1)} %get-tuple-element.19), channel_id=1, source_target_pairs={{0,1},{1,2},{2,3},{3,4},{4,5},{5,6},{6,7},{7,8},{8,9},{9,10},{10,1... | collective-permute-start | bytes 1634312 | tf_op jit(solution)/shard_map/ppermute | solution.py:306
  47.5 16.9 %collective-permute-start.9 = (f32[1064,128]{1,0:T(8,128)S(1)}, f32[1064,128]{1,0:T(8,128)S(1)}, u32[]{:S(2)}, u32[]{:S(2)}) collective-permute-start(f32[1064,128]{1,0:T(8,128)S(1)} %get-tuple-element.20), channel_id=1, source_target_pairs={{0,31},{1,0},{2,1},{3,2},{4,3},{5,4},{6,5},{7,6},{8,7},{9,8},{10,9... | collective-permute-start | bytes 1634312 | tf_op jit(solution)/shard_map/ppermute | solution.py:306
  49.3 12.3 %collective-permute-start.11 = (f32[40,128]{1,0:T(8,128)S(1)}, f32[40,128]{1,0:T(8,128)S(1)}, u32[]{:S(2)}, u32[]{:S(2)}) collective-permute-start(f32[40,128]{1,0:T(8,128)S(1)} %get-tuple-element.22), channel_id=1, source_target_pairs={{0,30},{1,31},{2,0},{3,1},{4,2},{5,3},{6,4},{7,5},{8,6},{9,7},{10,... | collective-permute-start | bytes 61448 | tf_op jit(solution)/shard_map/ppermute | solution.py:306
  49.3 13.4 %collective-permute-start.10 = (f32[40,128]{1,0:T(8,128)S(1)}, f32[40,128]{1,0:T(8,128)S(1)}, u32[]{:S(2)}, u32[]{:S(2)}) collective-permute-start(f32[40,128]{1,0:T(8,128)S(1)} %get-tuple-element.22), channel_id=1, source_target_pairs={{0,2},{1,3},{2,4},{3,5},{4,6},{5,7},{6,8},{7,9},{8,10},{9,11},{10,... | collective-permute-start | bytes 61448 | tf_op jit(solution)/shard_map/ppermute | solution.py:306
  71.1 13.0 %collective-permute-start.13 = (f32[424,128]{1,0:T(8,128)}, f32[424,128]{1,0:T(8,128)S(1)}, u32[]{:S(2)}, u32[]{:S(2)}) collective-permute-start(f32[424,128]{1,0:T(8,128)} %get-tuple-element.24), channel_id=1, source_target_pairs={{0,224},{32,0},{64,32},{96,64},{128,96},{160,128},{192,160},{224,1... | collective-permute-start | bytes 651272 | tf_op jit(solution)/shard_map/ppermute | solution.py:306
  75.0 9.1 %collective-permute-start.12 = (f32[424,128]{1,0:T(8,128)S(1)}, f32[424,128]{1,0:T(8,128)S(1)}, u32[]{:S(2)}, u32[]{:S(2)}) collective-permute-start(f32[424,128]{1,0:T(8,128)S(1)} %get-tuple-element.25), channel_id=1, source_target_pairs={{0,32},{32,64},{64,96},{96,128},{128,160},{160,192},{192,224},{224... | collective-permute-start | bytes 651272 | tf_op jit(solution)/shard_map/ppermute | solution.py:306
  75.0 9.0 %collective-permute-start.15 = (f32[40,128]{1,0:T(8,128)S(1)}, f32[40,128]{1,0:T(8,128)S(1)}, u32[]{:S(2)}, u32[]{:S(2)}) collective-permute-start(f32[40,128]{1,0:T(8,128)S(1)} %concatenate.15.refs_5_), channel_id=1, source_target_pairs={{0,192},{32,224},{64,0},{96,32},{128,64},{160,96},{192,128},{224,1... | collective-permute-start | bytes 61448 | tf_op jit(solution)/shard_map/ppermute | solution.py:306
  76.5 7.6 %collective-permute-start.14 = (f32[40,128]{1,0:T(8,128)S(1)}, f32[40,128]{1,0:T(8,128)S(1)}, u32[]{:S(2)}, u32[]{:S(2)}) collective-permute-start(f32[40,128]{1,0:T(8,128)S(1)} %concatenate.15.refs_5_), channel_id=1, source_target_pairs={{0,64},{32,96},{64,128},{96,160},{128,192},{160,224},{192,0},{224,... | collective-permute-start | bytes 61448 | tf_op jit(solution)/shard_map/ppermute | solution.py:306
  (10 other events, 8.9 us)
where the time goes:
time: 90.9 us; the launch traced here: 90.5 us
  starting transfers between devices  28.2 us (31%)
  Pallas kernels  25.7 us (28%)
  local copies, waits for them, and re-layouts  20.8 us (23%)
  waiting for transfers between devices  14.9 us (16%)
    ppermute x16, starting transfers between devices, shift(): lax.ppermute(value, axis, [(i, (i + step) % devices) for i in range(devic...  28.2 us
    pallas_call x2, Pallas kernels, apply(): pl.pallas_call(body, out_shape=shaped(*FIELD) if last else (shaped(*FIELD...  15.1 us
    ppermute x16, waiting for transfers between devices, shift(): lax.ppermute(value, axis, [(i, (i + step) % devices) for i in range(devic...  14.9 us
    unnamed x36, local copies, waits for them, and re-layouts  10.1 us
    pallas_call x2, Pallas kernels, local_part(): pl.pallas_call(body, out_shape=shaped(*WORK), in_specs=[VMEM] * len(args)...  7.62 us
    slice x10, local copies, waits for them, and re-layouts, apply(): tile[SLOTS:SLOTS + 1]  3.42 us
    pallas_call x1, Pallas kernels, shards(): pl.pallas_call(first_kernel, out_shape=SENT, in_specs=[VMEM, VMEM, SMEM,...  2.95 us
    slice x10, local copies, waits for them, and re-layouts, apply(): tile[:SLOTS, :WIDTH]  2.42 us
  transfers between devices with their start and end apart: 16, of which 3 were waited for; matrix products, arithmetic and copies ran while one was open for 4% of the time, Pallas kernels for 8%

commit v1 on v0

v1 whole, which is shorter than its diff:
```python
import jax
import jax.numpy as jnp
from jax import lax
from jax.experimental import pallas as pl
from jax.experimental.pallas import tpu as pltpu
from jax.sharding import PartitionSpec as P

LAPLACE_COEFFS = (
    -5369.0 / 1800.0,
    12.0 / 7.0,
    -15.0 / 56.0,
    10.0 / 189.0,
    -1.0 / 112.0,
    2.0 / 1925.0,
    -1.0 / 16632.0,
)
SPACING = 0.4
CENTER = 45.0
HALF_WIDTH = 48.0
KINETIC = -0.5 / (SPACING * SPACING)
REACH = 6

ORB = 2
NPROJ = 9
LANES = 128
CX, CY, NZ = 32, 16, 256
SLOTS = 32
GROUPS = SLOTS // 8
ATOMS = 5120
WIDTH = 24
ATOM_LANE = 96
BLOCK = 8
COLUMN = 5 * BLOCK
PLANES = ORB * CX * 2
Y_ROWS = BLOCK + REACH * PLANES + 8
X_ROWS = ORB * REACH * 2 * CY

VMEM = pl.BlockSpec(memory_space=pltpu.VMEM)
SMEM = pl.BlockSpec(memory_space=pltpu.SMEM)
ANY = pl.BlockSpec(memory_space=pl.ANY)
HBM = pl.BlockSpec(memory_space=pltpu.HBM)
F32 = jnp.float32


def iota(shape, axis):
    return lax.broadcasted_iota(jnp.int32, shape, axis)


def swap_groups(x):
    row = iota((1, 8, LANES), 1)
    group = iota((1, 8, LANES), 2) // 16
    for d in (4, 2, 1):
        row_bit, group_bit = ((row & d) != 0, (group & d) != 0)
        later = pltpu.roll(pltpu.roll(x, 8 - d, 1), 16 * d, 2)
        if d == 4:
            other = later
        else:
            earlier = pltpu.roll(pltpu.roll(x, d, 1), LANES - 16 * d, 2)
            other = jnp.where(group_bit, later, earlier)
        x = jnp.where(row_bit == group_bit, x, other)
    return x


def corner(offset_ref, slot):
    z = offset_ref[2, slot]
    return offset_ref[0, slot], offset_ref[1, slot], z // LANES, z % LANES


def project(work, proj_ref, offset_ref, atom_ref, part):
    lane = iota((1, 8, LANES), 2)
    group_of_lane = lane // 16
    flat_lane = iota((BLOCK, LANES), 1)
    flat_row = iota((BLOCK, LANES), 0)
    block = jnp.zeros((BLOCK, LANES), F32)
    for s in range(SLOTS):
        place = (flat_row == s // 8) & (flat_lane == ATOM_LANE + s % 8)
        block = jnp.where(place, atom_ref[s].astype(F32), block)

    def group_step(g, block):
        patches = [jnp.zeros((8, 8, LANES), F32) for _ in range(ORB)]
        for i in range(8):
            x, y, half, z = corner(offset_ref, g * 8 + i)
            shift = (16 * i + LANES - z) % LANES
            for o in range(ORB):
                near = work[o, pl.ds(x, 8), half, pl.ds(y, 8), :]
                far = work[o, pl.ds(x, 8), 1, pl.ds(y, 8), :]
                window = pltpu.roll(jnp.where(lane >= z, near, far), shift, 2)
                patches[o] = jnp.where(group_of_lane == i, window, patches[o])
        patches = [swap_groups(patch) for patch in patches]
        tile = jnp.zeros((8, LANES), F32)
        rows = pl.ds(pl.multiple_of(g * 8, 8), 8)
        for p in range(NPROJ):
            values = [proj_ref[p, rows, LANES * a : LANES * (a + 1)] for a in range(8)]
            for o in range(ORB):
                total = values[0] * patches[o][0]
                for a in range(1, 8):
                    total = total + values[a] * patches[o][a]
                summed = jnp.sum(total, axis=1, keepdims=True)
                tile = jnp.where(flat_lane == 2 * p + o, summed, tile)
        return block + pltpu.roll(tile, g * WIDTH, 1)

    part[...] = lax.fori_loop(0, GROUPS, group_step, block, unroll=True)


def pack(work, part, y_up, y_down, x_up, x_down):
    for n in range(PLANES):
        o, x, half = (n // (2 * CX), n // 2 % CX, n % 2)
        y_down[BLOCK + REACH * n : BLOCK + REACH * n + 8, :] = work[o, x, half, 0:8, :]
    for n in reversed(range(PLANES)):
        o, x, half = (n // (2 * CX), n // 2 % CX, n % 2)
        y_up[REACH * (n + 1) : REACH * (n + 1) + 8, :] = work[o, x, half, 8:16, :]
    for target in (y_up, y_down):
        target[0:BLOCK, :] = part[...]
        target[Y_ROWS - 8 : Y_ROWS, :] = jnp.zeros((8, LANES), F32)
    for o in range(ORB):
        rows = slice(o * REACH * 32, (o + 1) * REACH * 32)
        x_up[rows, :] = work[o, CX - REACH : CX].reshape(REACH * 32, LANES)
        x_down[rows, :] = work[o, 0:REACH].reshape(REACH * 32, LANES)


def first_kernel(v, proj_hbm, offset_hbm, atom_hbm, y_up, y_down, x_up, x_down, part,
                 work, proj_ref, offset_ref, atom_ref, sems):
    copies = [
        pltpu.make_async_copy(offset_hbm, offset_ref, sems.at[0]),
        pltpu.make_async_copy(atom_hbm, atom_ref, sems.at[1]),
        pltpu.make_async_copy(v.at[:, :, :, 0:LANES], work.at[:, :, 0], sems.at[2]),
        pltpu.make_async_copy(v.at[:, :, :, LANES:NZ], work.at[:, :, 1], sems.at[3]),
        pltpu.make_async_copy(proj_hbm, proj_ref, sems.at[4]),
    ]
    for copy in copies:
        copy.start()
    for copy in copies:
        copy.wait()
    project(work, proj_ref, offset_ref, atom_ref, part)
    pack(work, part, y_up, y_down, x_up, x_down)


def local_kernel(scale, second, *refs):
    if second:
        field, potential, _, orbital, full, out, pad, along_z = refs
        halves = [field[:, :, half] for half in range(2)]
        for half in range(2):
            full[:, :, :, LANES * half : LANES * (half + 1)] = halves[half]
    else:
        field, potential, _, out, pad, along_z = refs
        halves = [field[:, :, :, LANES * half : LANES * (half + 1)] for half in range(2)]
    weights = [scale * KINETIC / HALF_WIDTH * w for w in LAPLACE_COEFFS]

    gap = jnp.abs(iota((NZ, NZ), 0) - iota((NZ, NZ), 1))
    band = jnp.zeros((NZ, NZ), F32)
    for r in range(1, REACH + 1):
        band = jnp.where(gap == r, weights[r], band)
    summed = None
    for half in range(2):
        term = jnp.dot(
            halves[half].reshape(ORB * CX * CY, LANES),
            band[LANES * half : LANES * (half + 1)],
            precision=lax.Precision.HIGHEST,
            preferred_element_type=F32,
        )
        summed = term if summed is None else summed + term
    along_z[...] = summed

    for o in range(ORB):
        for x in range(REACH):
            pad[o, x, :, 8:24, :] = jnp.zeros((2, CY, LANES), F32)
            pad[o, x + REACH + CX, :, 8:24, :] = jnp.zeros((2, CY, LANES), F32)
        pad[o, REACH : REACH + CX, :, 0:8, :] = jnp.zeros((CX, 2, 8, LANES), F32)
        pad[o, REACH : REACH + CX, :, 24:32, :] = jnp.zeros((CX, 2, 8, LANES), F32)
        for half in range(2):
            pad[o, REACH : REACH + CX, half, 8:24, :] = halves[half][o]

    def step(n, carry):
        o, x = (n // CX, n % CX)
        for half in range(2):
            lanes = slice(LANES * half, LANES * (half + 1))
            for t in range(2):
                rows = slice(8 + 8 * t, 16 + 8 * t)
                here = pad[o, x + REACH, half, rows, :]
                factor = potential[x, 8 * t : 8 * t + 8, lanes] * (scale / HALF_WIDTH) + (
                    3.0 * weights[0] - scale * CENTER / HALF_WIDTH
                )
                total = factor * here
                depth = pl.ds(pl.multiple_of(n * CY + 8 * t, 8), 8)
                total = total + along_z[depth, lanes]
                for r in range(1, REACH + 1):
                    paired = (
                        pad[o, x + REACH + r, half, rows, :] + pad[o, x + REACH - r, half, rows, :]
                    )
                    paired = paired + (
                        pad[o, x + REACH, half, 8 + 8 * t + r : 16 + 8 * t + r, :]
                        + pad[o, x + REACH, half, 8 + 8 * t - r : 16 + 8 * t - r, :]
                    )
                    total = total + weights[r] * paired
                if second:
                    total = total - orbital[o, x, 8 * t : 8 * t + 8, lanes]
                out[o, x, half, 8 * t : 8 * t + 8, :] = total
        return carry

    lax.fori_loop(0, ORB * CX, step, 0)


def edge_kernel(scale, before_ref, after_ref, local, out, before, after, sems):
    copies = [
        pltpu.make_async_copy(before_ref, before, sems.at[0]),
        pltpu.make_async_copy(after_ref, after, sems.at[1]),
    ]
    for copy in copies:
        copy.start()
    row = iota((8, LANES), 0)
    low, high = ([None], [None])
    for r in range(1, REACH + 1):
        weight = scale * KINETIC / HALF_WIDTH * LAPLACE_COEFFS[r]
        low.append(jnp.where(row < r, weight, 0.0).astype(F32))
        high.append(jnp.where(row >= 8 - r, weight, 0.0).astype(F32))
    for copy in copies:
        copy.wait()

    def step(n, carry):
        o, x = (n // CX, n % CX)
        for half in range(2):
            start = (n * 2 + half) * REACH
            first = local[o, x, half, 0:8, :]
            second = local[o, x, half, 8:16, :]
            for r in range(1, REACH + 1):
                first = first + low[r] * before[pl.ds(start + BLOCK + REACH - r, 8), :]
                second = second + high[r] * after[pl.ds(start + r, 8), :]
            out[o, x, half, 0:8, :] = first
            out[o, x, half, 8:16, :] = second
        return carry

    lax.fori_loop(0, ORB * CX, step, 0, unroll=4)


def gather_kernel(two_before, before, part, after, two_after, x_up_in, x_down_in, local,
                  x_up, x_down, column, sems):
    sources = (
        two_before,
        before.at[0:BLOCK],
        part,
        after.at[0:BLOCK],
        two_after,
    )
    copies = []
    for k, source in enumerate(sources):
        for n, (target, start) in enumerate(((x_up, X_ROWS), (x_down, X_ROWS), (column, 0))):
            rows = pl.ds(start + BLOCK * k, BLOCK)
            copies.append(pltpu.make_async_copy(source, target.at[rows], sems.at[3 * k + n]))
    for copy in copies:
        copy.start()
    for copy in copies:
        copy.wait()


def coefficients(columns, atom_ref):
    row = iota((8, LANES), 0)
    lane = iota((BLOCK, LANES), 1)
    own = []
    for g in range(GROUPS):
        held = jnp.full((8, LANES), -1.0, F32)
        for i in range(8):
            atom = atom_ref[8 * g + i]
            atom = jnp.where(atom < ATOMS, atom, -1)
            held = jnp.where(row == i, atom.astype(F32), held)
        own.append(held)
    own = jnp.concatenate(own, axis=0)
    result = jnp.zeros((GROUPS * SLOTS, 3 * LANES), F32)
    for values in columns:
        high = values.astype(jnp.bfloat16)
        rest = values - high.astype(F32)
        middle = rest.astype(jnp.bfloat16)
        low = (rest - middle.astype(F32)).astype(jnp.bfloat16)
        atoms = jnp.full((BLOCK, LANES), -2.0, F32)
        for k in range(5):
            tile = values[BLOCK * k : BLOCK * (k + 1)]
            moved = pltpu.roll(tile, LANES - ATOM_LANE + 8 * k, 1)
            atoms = jnp.where(lane // 8 == k, moved, atoms)
        same = jnp.concatenate(
            [jnp.where(own == atoms[g : g + 1, :], 1.0, 0.0) for g in range(GROUPS)], axis=0
        )
        same = same[:, :COLUMN].astype(jnp.bfloat16)
        result = result + jnp.dot(
            same, jnp.concatenate([high, middle, low], axis=1), preferred_element_type=F32
        )
    result = result[:, :LANES] + result[:, LANES : 2 * LANES] + result[:, 2 * LANES :]
    total = result[:SLOTS]
    for g in range(1, GROUPS):
        total = total + pltpu.roll(result[SLOTS * g : SLOTS * (g + 1)], LANES - WIDTH * g, 1)
    return total


def finish(scale, local, before_ref, after_ref, two_before, two_after, column, proj_ref,
           strength_ref, offset_ref, atom_ref, work, before, after, table, held, split, sems):
    weights = [scale * KINETIC / HALF_WIDTH * w for w in LAPLACE_COEFFS]
    copies = [
        pltpu.make_async_copy(before_ref, before, sems.at[0]),
        pltpu.make_async_copy(after_ref, after, sems.at[1]),
    ]
    for copy in copies:
        copy.start()
    work[:, REACH : CX - REACH] = local[:, REACH : CX - REACH]
    count = 0
    for s in range(SLOTS):
        split[count] = s
        z = offset_ref[2, s]
        count = count + jnp.where((z > LANES - 16) & (z < LANES), 1, 0)
    for copy in copies:
        copy.wait()
    table[...] = coefficients(
        (
            column[...],
            before[X_ROWS:, :],
            after[X_ROWS:, :],
            two_before[...],
            two_after[...],
        ),
        atom_ref,
    )
    for o in range(ORB):
        for j in range(REACH):
            low = local[o, j]
            for i in range(j, REACH):
                rows = slice((o * REACH + i) * 32, (o * REACH + i + 1) * 32)
                low = low + weights[j + REACH - i] * before[rows, :].reshape(2, CY, LANES)
            work[o, j] = low
            high = local[o, CX - REACH + j]
            for i in range(j + 1):
                rows = slice((o * REACH + i) * 32, (o * REACH + i + 1) * 32)
                high = high + weights[REACH + i - j] * after[rows, :].reshape(2, CY, LANES)
            work[o, CX - REACH + j] = high

    lane = iota((1, 8, LANES), 2)

    def group_step(g, carry):
        rows = pl.ds(pl.multiple_of(g * 8, 8), 8)
        factors = table[rows, :]
        added = [[None] * 8 for _ in range(ORB)]
        for p in range(NPROJ):
            strength = strength_ref[p] * (scale / HALF_WIDTH)
            spread = [
                jnp.broadcast_to(factors[:, 2 * p + o : 2 * p + o + 1], (8, LANES)) * strength
                for o in range(ORB)
            ]
            for a in range(8):
                values = proj_ref[p, rows, LANES * a : LANES * (a + 1)]
                for o in range(ORB):
                    term = values * spread[o]
                    added[o][a] = term if p == 0 else added[o][a] + term
        patches = [swap_groups(jnp.stack(added[o])) for o in range(ORB)]
        for o in range(ORB):
            held[g, o] = patches[o]
        for i in range(8):
            x, y, half, z = corner(offset_ref, g * 8 + i)
            shift = (z + LANES - 16 * i) % LANES
            inside = (lane >= z) & (lane < z + 16)
            places = [(o, pl.ds(x, 8), half, pl.ds(y, 8), slice(None)) for o in range(ORB)]
            sums = [
                work[places[o]] + jnp.where(inside, pltpu.roll(patches[o], shift, 2), 0.0)
                for o in range(ORB)
            ]
            for o in range(ORB):
                work[places[o]] = sums[o]
        return carry

    lax.fori_loop(0, GROUPS, group_step, 0, unroll=True)

    def split_step(n, carry):
        s = split[n]
        x, y, half, z = corner(offset_ref, s)
        shift = (z + LANES - 16 * (s % 8)) % LANES
        for o in range(ORB):
            place = (o, pl.ds(x, 8), 1, pl.ds(y, 8), slice(None))
            moved = pltpu.roll(held[s // 8, o], shift, 2)
            work[place] = work[place] + jnp.where(lane < z + 16 - LANES, moved, 0.0)
        return carry

    lax.fori_loop(0, count, split_step, 0)


def middle_kernel(scale, local, before_ref, after_ref, two_before, two_after, column, proj_ref,
                  strength_ref, offset_ref, atom_ref, work, y_up, y_down, x_up, x_down, part,
                  *scratch):
    finish(scale, local, before_ref, after_ref, two_before, two_after, column, proj_ref,
           strength_ref, offset_ref, atom_ref, work, *scratch)
    project(work, proj_ref, offset_ref, atom_ref, part)
    pack(work, part, y_up, y_down, x_up, x_down)


def last_kernel(scale, local, before_ref, after_ref, two_before, two_after, column, proj_ref,
                strength_ref, offset_ref, atom_ref, out, work, *scratch):
    finish(scale, local, before_ref, after_ref, two_before, two_after, column, proj_ref,
           strength_ref, offset_ref, atom_ref, work, *scratch)
    for half in range(2):
        out[:, :, :, LANES * half : LANES * (half + 1)] = work[:, :, half]


def shaped(*shape):
    return jax.ShapeDtypeStruct(shape, F32)


PARAMS = pltpu.CompilerParams(vmem_limit_bytes=16 * 1024 * 1024)
FIELD = (ORB, CX, CY, NZ)
WORK = (ORB, CX, 2, CY, LANES)
SENT = (
    shaped(Y_ROWS, LANES),
    shaped(Y_ROWS, LANES),
    shaped(X_ROWS + COLUMN, LANES),
    shaped(X_ROWS + COLUMN, LANES),
    shaped(BLOCK, LANES),
)


def cost(microseconds):
    return pl.CostEstimate(
        flops=0, transcendentals=0, bytes_accessed=int(microseconds * 3.0e6)
    )


def shift(value, axis, step):
    devices = lax.axis_size(axis)
    return lax.ppermute(value, axis, [(i, (i + step) % devices) for i in range(devices)])


def local_part(scale, field, potential, part, orbital):
    second = orbital is not None
    args = (field, potential, part) + ((orbital,) if second else ())

    def local_body(*refs):
        local_kernel(scale, second, *refs)

    return pl.pallas_call(
        local_body,
        out_shape=(shaped(*FIELD), shaped(*WORK)) if second else shaped(*WORK),
        in_specs=[VMEM, VMEM, ANY] + [VMEM] * (len(args) - 3),
        out_specs=(VMEM, VMEM) if second else VMEM,
        scratch_shapes=[
            pltpu.VMEM((ORB, CX + 2 * REACH, 2, 32, LANES), F32),
            pltpu.VMEM((ORB * CX * CY, NZ), F32),
        ],
        compiler_params=PARAMS,
        cost_estimate=cost(4),
        name="local_part",
    )(*args)


def edge_part(scale, before, after, local):
    def edge_body(*refs):
        edge_kernel(scale, *refs)

    return pl.pallas_call(
        edge_body,
        out_shape=shaped(*WORK),
        in_specs=[ANY, ANY, VMEM],
        out_specs=VMEM,
        scratch_shapes=[pltpu.VMEM((Y_ROWS, LANES), F32)] * 2 + [pltpu.SemaphoreType.DMA((2,))],
        compiler_params=PARAMS,
        cost_estimate=cost(2),
        name="edge_part",
    )(before, after, local)


def gather_part(two_before, before, part, after, two_after, x_up, x_down, local):
    return pl.pallas_call(
        gather_kernel,
        out_shape=(SENT[2], SENT[3], shaped(COLUMN, LANES)),
        in_specs=[ANY] * 8,
        out_specs=(ANY,) * 3,
        scratch_shapes=[pltpu.SemaphoreType.DMA((15,))],
        input_output_aliases={5: 0, 6: 1},
        compiler_params=PARAMS,
        cost_estimate=cost(1),
        name="gather_part",
    )(two_before, before, part, after, two_after, x_up, x_down, local)


def apply(scale, field, potential, sent, orbital, shared):
    second = orbital is not None
    y_up, y_down, x_up, x_down, part = sent
    projectors, strengths, offsets, atoms = shared
    y_before = shift(y_up, "gy", 1)
    y_after = shift(y_down, "gy", -1)
    y_two_before = shift(part, "gy", 2)
    y_two_after = shift(part, "gy", -2)
    local = local_part(scale, field, potential, part, orbital)
    if second:
        full, local = local
    x_up, x_down, column = gather_part(
        y_two_before, y_before, part, y_after, y_two_after, x_up, x_down, local
    )
    x_before = shift(x_up, "gx", 1)
    x_after = shift(x_down, "gx", -1)
    x_two_before = shift(column, "gx", 2)
    x_two_after = shift(column, "gx", -2)
    local = edge_part(scale, y_before, y_after, local)
    kernel = last_kernel if second else middle_kernel

    def end_body(*refs):
        kernel(scale, *refs)

    scratch = [
        pltpu.VMEM((X_ROWS + COLUMN, LANES), F32),
        pltpu.VMEM((X_ROWS + COLUMN, LANES), F32),
        pltpu.VMEM((SLOTS, LANES), F32),
        pltpu.VMEM((GROUPS, ORB, 8, 8, LANES), F32),
        pltpu.SMEM((SLOTS + 1,), jnp.int32),
        pltpu.SemaphoreType.DMA((2,)),
    ]
    result = pl.pallas_call(
        end_body,
        out_shape=shaped(*FIELD) if second else (shaped(*WORK),) + SENT,
        in_specs=[VMEM, ANY, ANY, VMEM, VMEM, VMEM, VMEM] + [SMEM] * 3,
        out_specs=VMEM if second else (VMEM,) * 6,
        scratch_shapes=([pltpu.VMEM(WORK, F32)] if second else []) + scratch,
        compiler_params=PARAMS,
        cost_estimate=cost(6),
        name="last_part" if second else "middle_part",
    )(local, x_before, x_after, x_two_before, x_two_after, column, projectors, strengths, offsets,
      atoms)
    return (full, result) if second else result


def shards(orbitals, potential, projectors, strengths, atom_owner, slot_atom, slot_offset):
    projectors = jnp.transpose(projectors, (1, 0, 2))
    shared = (projectors, strengths, slot_offset, slot_atom)
    sent = pl.pallas_call(
        first_kernel,
        out_shape=SENT,
        in_specs=[HBM] * 4,
        out_specs=(VMEM,) * 5,
        scratch_shapes=[
            pltpu.VMEM(WORK, F32),
            pltpu.VMEM((NPROJ, SLOTS, 8 * LANES), F32),
            pltpu.SMEM((3, SLOTS), jnp.int32),
            pltpu.SMEM((SLOTS,), jnp.int32),
            pltpu.SemaphoreType.DMA((5,)),
        ],
        compiler_params=PARAMS,
        cost_estimate=cost(3),
        name="first_part",
    )(orbitals, projectors, slot_offset, slot_atom)
    field, *sent = apply(1.0, orbitals, potential, sent, None, shared)
    return apply(2.0, field, potential, sent, orbitals, shared)


def solution(mesh):
    return jax.shard_map(
        shards,
        mesh=mesh,
        in_specs=(
            P(None, "gx", "gy", None),
            P("gx", "gy", None),
            P(("gx", "gy"), None, None),
            P(),
            P(),
            P(("gx", "gy")),
            P(None, ("gx", "gy")),
        ),
        out_specs=(P(None, "gx", "gy", None), P(None, "gx", "gy", None)),
        check_vma=False,
    )
```

time: 90.9 us -> 68.6 us (0.75)
  local copies, waits for them, and re-layouts: 20.8 us -> 3.84 us
  waiting for transfers between devices: 14.9 us -> 7.65 us
    ppermute x16, waiting for transfers between devices: 14.9 us -> 7.65 us  [shift(): lax.ppermute(value, axis, [(i, (i + step) % devices) for i in range(devic...]
    unnamed x36 -> x16, local copies, waits for them, and re-layouts: 10.1 us -> 3.84 us
    slice x22 -> x0, local copies, waits for them, and re-layouts: 5.85 us -> none  [the longest x10 3.42 us: apply(): tile[SLOTS:SLOTS + 1]]
    concatenate x4 -> x0, local copies, waits for them, and re-layouts: 3.65 us -> none  [the longest x2 2.09 us: apply(): jnp.concatenate([sums] + [tile[SLOTS:SLOTS + 1] for tile in tiles] + [til...]
    dynamic_update_slice x2 -> x0, local copies, waits for them, and re-layouts: 1.21 us -> none  [apply(): x_down = lax.dynamic_update_slice(x_down, block, (X_ROWS, 0))]
    pallas_call x5 -> x9, Pallas kernels: 25.7 us -> 26.3 us  [the longest x2 10.2 us: local_part(): pl.pallas_call(local_body, out_shape=(shaped(*FIELD), shaped(*WORK)) if s...]
  transfers between devices with their start and end apart: 16 -> 16, of which waited for: 3 -> 6; matrix products, arithmetic and copies ran while one was open for 4% -> 0% of each run, Pallas kernels for 8% -> 19%
where the time goes in v1:
time: 68.6 us; the launch traced here: 67.4 us
  starting transfers between devices  28.7 us (42%)
  Pallas kernels  26.3 us (38%)
  waiting for transfers between devices  7.65 us (11%)
  local copies, waits for them, and re-layouts  3.84 us (6%)
  between operations  0.92 us (1%)
    ppermute x16, starting transfers between devices, shift(): lax.ppermute(value, axis, [(i, (i + step) % devices) for i in range(devic...  28.7 us
    pallas_call x2, Pallas kernels, local_part(): pl.pallas_call(local_body, out_shape=(shaped(*FIELD), shaped(*WORK)) if s...  10.2 us
    pallas_call x2, Pallas kernels, apply(): pl.pallas_call(end_body, out_shape=shaped(*FIELD) if second else (shaped(...  10.2 us
    ppermute x16, waiting for transfers between devices, shift(): lax.ppermute(value, axis, [(i, (i + step) % devices) for i in range(devic...  7.65 us
    unnamed x16, local copies, waits for them, and re-layouts  3.84 us
    pallas_call x1, Pallas kernels, shards(): pl.pallas_call(first_kernel, out_shape=SENT, in_specs=[HBM] * 4, out_spec...  3.15 us
    pallas_call x2, Pallas kernels, edge_part(): pl.pallas_call(edge_body, out_shape=shaped(*WORK), in_specs=[ANY, ANY, VM...  2.33 us
  transfers between devices with their start and end apart: 16, of which 6 were waited for; matrix products, arithmetic and copies ran while one was open for 0% of the time, Pallas kernels for 19%

profile of v1, /device:TPU:30, one launch (start us, length us, event | category | flops | bytes accessed | tf_op | source)
XLA Modules:
  0.0 67.4 jit_solution(17578077243598839185)
XLA Ops:
  0.6 1.3 %copy-done = f32[32,9,1024]{2,0,1:T(8,128)S(1)} copy-done((f32[32,9,1024]{2,0,1:T(8,128)S(1)}, f32[32,9,1024]{2,0,1:T(8,128)}, u32[]{:S(2)}) %copy-start) | copy-done | bytes 1179672
  1.9 1.2 %copy-done.2 = f32[2,32,16,256]{3,2,1,0:T(8,128)S(1)} copy-done((f32[2,32,16,256]{3,2,1,0:T(8,128)S(1)}, f32[2,32,16,256]{3,2,1,0:T(8,128)}, u32[]{:S(2)}) %copy-start.2) | copy-done | bytes 1048600
  4.5 3.2 %first_part.1 = (f32[784,128]{1,0:T(8,128)S(1)}, f32[784,128]{1,0:T(8,128)S(1)}, f32[424,128]{1,0:T(8,128)S(1)}, f32[424,128]{1,0:T(8,128)S(1)}, f32[8,128]{1,0:T(8,128)S(1)}) custom-call(f32[2,32,16,256]{3,2,1,0:T(8,128)S(1)} %copy-done.2, f32[9,32,1024]{2,1,0:T(8,128)S(1)} %bitcast.1, s32[3,32]{1,0:T(4,128)S(1)} %copy-done.5, s32[32]{0:T(128)S(1)} %copy-done.6), custom_call_target="tpu_custom_call" | custom-call | bytes 9000000 | tf_op jit(solution)/shard_map/first_part/pallas_call | solution.py:525
  7.7 1.7 %collective-permute-start.1 = (f32[784,128]{1,0:T(8,128)S(1)}, f32[784,128]{1,0:T(8,128)S(1)}, u32[]{:S(2)}, u32[]{:S(2)}) collective-permute-start(f32[784,128]{1,0:T(8,128)S(1)} %get-tuple-element.22), channel_id=1, source_target_pairs={{0,31},{1,0},{2,1},{3,2},{4,3},{5,4},{6,5},{7,6},{8,7},{9,8},{10,9... | collective-permute-start | bytes 1204232 | tf_op jit(solution)/shard_map/ppermute | solution.py:421
  9.5 0.7 %collective-permute-start.3 = (f32[8,128]{1,0:T(8,128)S(1)}, f32[8,128]{1,0:T(8,128)S(1)}, u32[]{:S(2)}, u32[]{:S(2)}) collective-permute-start(f32[8,128]{1,0:T(8,128)S(1)} %get-tuple-element.23.refs_2_.part), channel_id=1, source_target_pairs={{0,30},{1,31},{2,0},{3,1},{4,2},{5,3},{6,4},{7,5},{8,6},{9,7},{10,... | collective-permute-start | bytes 12296 | tf_op jit(solution)/shard_map/ppermute | solution.py:421
  10.2 4.6 %collective-permute-start.2 = (f32[8,128]{1,0:T(8,128)S(1)}, f32[8,128]{1,0:T(8,128)S(1)}, u32[]{:S(2)}, u32[]{:S(2)}) collective-permute-start(f32[8,128]{1,0:T(8,128)S(1)} %get-tuple-element.23.refs_2_.part), channel_id=1, source_target_pairs={{0,2},{1,3},{2,4},{3,5},{4,6},{5,7},{6,8},{7,9},{8,10},{9,11},{10,... | collective-permute-start | bytes 12296 | tf_op jit(solution)/shard_map/ppermute | solution.py:421
  14.8 4.6 %local_part.2.refs_2_.local = f32[2,32,2,16,128]{4,3,2,1,0:T(8,128)S(1)} custom-call(f32[2,32,16,256]{3,2,1,0:T(8,128)S(1)} %copy-done.2, f32[32,16,256]{2,1,0:T(8,128)S(1)} %copy-done.4, f32[8,128]{1,0:T(8,128)S(1)} %get-tuple-element.23.refs_2_.part), custom_call_target="tpu_custom_call" | custom-call | bytes 12000000 | tf_op jit(solution)/shard_map/local_part/pallas_call | solution.py:431
  19.4 1.1 %collective-permute-done.3.two_after = f32[8,128]{1,0:T(8,128)S(1)} collective-permute-done((f32[8,128]{1,0:T(8,128)S(1)}, f32[8,128]{1,0:T(8,128)S(1)}, u32[]{:S(2)}, u32[]{:S(2)}) %collective-permute-start.3) | collective-permute-done | bytes 4128 | tf_op jit(solution)/shard_map/ppermute | solution.py:421
  20.8 0.9 %collective-permute-start.4 = (f32[424,128]{1,0:T(8,128)S(1)}, f32[424,128]{1,0:T(8,128)S(1)}, u32[]{:S(2)}, u32[]{:S(2)}) collective-permute-start(f32[424,128]{1,0:T(8,128)S(1)} %get-tuple-element.26), channel_id=1, source_target_pairs={{0,32},{32,64},{64,96},{96,128},{128,160},{160,192},{192,224},{224... | collective-permute-start | bytes 651272 | tf_op jit(solution)/shard_map/ppermute | solution.py:421
  21.7 4.0 %collective-permute-start.5 = (f32[424,128]{1,0:T(8,128)S(1)}, f32[424,128]{1,0:T(8,128)S(1)}, u32[]{:S(2)}, u32[]{:S(2)}) collective-permute-start(f32[424,128]{1,0:T(8,128)S(1)} %get-tuple-element.27), channel_id=1, source_target_pairs={{0,224},{32,0},{64,32},{96,64},{128,96},{160,128},{192,160},{224,1... | collective-permute-start | bytes 651272 | tf_op jit(solution)/shard_map/ppermute | solution.py:421
  25.7 2.4 %collective-permute-start.7 = (f32[40,128]{1,0:T(8,128)S(1)}, f32[40,128]{1,0:T(8,128)S(1)}, u32[]{:S(2)}, u32[]{:S(2)}) collective-permute-start(f32[40,128]{1,0:T(8,128)S(1)} %get-tuple-element.28.refs_5_), channel_id=1, source_target_pairs={{0,192},{32,224},{64,0},{96,32},{128,64},{160,96},{192,128},{224,1... | collective-permute-start | bytes 61448 | tf_op jit(solution)/shard_map/ppermute | solution.py:421
  28.6 1.2 %edge_part.2.refs_0_ = f32[2,32,2,16,128]{4,3,2,1,0:T(8,128)S(1)} custom-call(f32[784,128]{1,0:T(8,128)S(1)} %collective-permute-done.refs_0_.before, f32[784,128]{1,0:T(8,128)S(1)} %collective-permute-done.1.refs_1_.after, f32[2,32,2,16,128]{4,3,2,1,0:T(8,128)S(1)} %local_part.2.refs_2_.local), custom_call_target="tpu_custom_call" | custom-call | bytes 6000000 | tf_op jit(solution)/shard_map/edge_part/pallas_call | solution.py:450
  29.8 0.7 %collective-permute-done.7.refs_4_ = f32[40,128]{1,0:T(8,128)S(1)} collective-permute-done((f32[40,128]{1,0:T(8,128)S(1)}, f32[40,128]{1,0:T(8,128)S(1)}, u32[]{:S(2)}, u32[]{:S(2)}) %collective-permute-start.7) | collective-permute-done | bytes 20512 | tf_op jit(solution)/shard_map/ppermute | solution.py:421
  30.5 3.5 %collective-permute-done.6.refs_3_ = f32[40,128]{1,0:T(8,128)S(1)} collective-permute-done((f32[40,128]{1,0:T(8,128)S(1)}, f32[40,128]{1,0:T(8,128)S(1)}, u32[]{:S(2)}, u32[]{:S(2)}) %collective-permute-start.6) | collective-permute-done | bytes 20512 | tf_op jit(solution)/shard_map/ppermute | solution.py:421
  34.0 5.9 %middle_part.1 = (f32[2,32,2,16,128]{4,3,2,1,0:T(8,128)S(1)}, f32[784,128]{1,0:T(8,128)S(1)}, f32[784,128]{1,0:T(8,128)S(1)}, f32[424,128]{1,0:T(8,128)S(1)}, f3...) custom-call(f32[2,32,2,16,128]{4,3,2,1,0:T(8,128)S(1)} %edge_part.2.refs_0_, f32[424,128]{1,0:T(8,128)S(1)} %collective-permute-done.4.refs_1_, ...), custom_call_target="tpu_custom_call" | custom-call | bytes 18000000 | tf_op jit(solution)/shard_map/middle_part/pallas_call | solution.py:508
  40.0 1.7 %collective-permute-start.9 = (f32[784,128]{1,0:T(8,128)S(1)}, f32[784,128]{1,0:T(8,128)S(1)}, u32[]{:S(2)}, u32[]{:S(2)}) collective-permute-start(f32[784,128]{1,0:T(8,128)S(1)} %get-tuple-element.33), channel_id=1, source_target_pairs={{0,31},{1,0},{2,1},{3,2},{4,3},{5,4},{6,5},{7,6},{8,7},{9,8},{10,9... | collective-permute-start | bytes 1204232 | tf_op jit(solution)/shard_map/ppermute | solution.py:421
  41.7 5.6 %collective-permute-start.10 = (f32[8,128]{1,0:T(8,128)S(1)}, f32[8,128]{1,0:T(8,128)S(1)}, u32[]{:S(2)}, u32[]{:S(2)}) collective-permute-start(f32[8,128]{1,0:T(8,128)S(1)} %get-tuple-element.30.refs_2_.part), channel_id=1, source_target_pairs={{0,2},{1,3},{2,4},{3,5},{4,6},{5,7},{6,8},{7,9},{8,10},{9,11},{10,... | collective-permute-start | bytes 12296 | tf_op jit(solution)/shard_map/ppermute | solution.py:421
  47.4 5.6 %local_part.3 = (f32[2,32,16,256]{3,2,1,0:T(8,128)}, f32[2,32,2,16,128]{4,3,2,1,0:T(8,128)S(1)}) custom-call(f32[2,32,2,16,128]{4,3,2,1,0:T(8,128)S(1)} %get-tuple-element.29.refs_0_, f32[32,16,256]{2,1,0:T(8,128)S(1)} %copy-done.4, f32[8,128]{1,0:T(8,128)S(1)} %get-tuple-element.30.refs_2_.part, f32[2,32,16,256]{3,2,1,0:T(8,128)S(1)} %copy-done.3), custom_call_target="tpu_custom_call" | custom-call | bytes 12000000 | tf_op jit(solution)/shard_map/local_part/pallas_call | solution.py:431
  53.5 1.1 %collective-permute-start.12 = (f32[424,128]{1,0:T(8,128)S(1)}, f32[424,128]{1,0:T(8,128)S(1)}, u32[]{:S(2)}, u32[]{:S(2)}) collective-permute-start(f32[424,128]{1,0:T(8,128)S(1)} %get-tuple-element.37), channel_id=1, source_target_pairs={{0,32},{32,64},{64,96},{96,128},{128,160},{160,192},{192,224},{224... | collective-permute-start | bytes 651272 | tf_op jit(solution)/shard_map/ppermute | solution.py:421
  54.6 2.2 %collective-permute-start.13 = (f32[424,128]{1,0:T(8,128)S(1)}, f32[424,128]{1,0:T(8,128)S(1)}, u32[]{:S(2)}, u32[]{:S(2)}) collective-permute-start(f32[424,128]{1,0:T(8,128)S(1)} %get-tuple-element.38), channel_id=1, source_target_pairs={{0,224},{32,0},{64,32},{96,64},{128,96},{160,128},{192,160},{224,1... | collective-permute-start | bytes 651272 | tf_op jit(solution)/shard_map/ppermute | solution.py:421
  57.1 2.7 %collective-permute-start.14 = (f32[40,128]{1,0:T(8,128)S(1)}, f32[40,128]{1,0:T(8,128)S(1)}, u32[]{:S(2)}, u32[]{:S(2)}) collective-permute-start(f32[40,128]{1,0:T(8,128)S(1)} %get-tuple-element.39.refs_5_), channel_id=1, source_target_pairs={{0,64},{32,96},{64,128},{96,160},{128,192},{160,224},{192,0},{224,... | collective-permute-start | bytes 61448 | tf_op jit(solution)/shard_map/ppermute | solution.py:421
  59.7 1.2 %edge_part.3.refs_0_ = f32[2,32,2,16,128]{4,3,2,1,0:T(8,128)S(1)} custom-call(f32[784,128]{1,0:T(8,128)S(1)} %collective-permute-done.8.refs_0_.before, f32[784,128]{1,0:T(8,128)S(1)} %collective-permute-done.9.refs_1_.after, f32[2,32,2,16,128]{4,3,2,1,0:T(8,128)S(1)} %get-tuple-element.34.refs_2_.local), custom_call_target="tpu_custom_call" | custom-call | bytes 6000000 | tf_op jit(solution)/shard_map/edge_part/pallas_call | solution.py:450
  60.9 1.6 %collective-permute-done.15.refs_4_ = f32[40,128]{1,0:T(8,128)S(1)} collective-permute-done((f32[40,128]{1,0:T(8,128)S(1)}, f32[40,128]{1,0:T(8,128)S(1)}, u32[]{:S(2)}, u32[]{:S(2)}) %collective-permute-start.15) | collective-permute-done | bytes 20512 | tf_op jit(solution)/shard_map/ppermute | solution.py:421
  63.0 4.2 %last_part.1 = f32[2,32,16,256]{3,2,1,0:T(8,128)} custom-call(f32[2,32,2,16,128]{4,3,2,1,0:T(8,128)S(1)} %edge_part.3.refs_0_, f32[424,128]{1,0:T(8,128)S(1)} %collective-permute-done.12.refs_1_, f32[424,128]{1,0:T(8,128)S(1)} %collective-permute-done.13.refs_2_, f32[40,128]{1,0:T(8,128)S(1)} %collective-permute-done.14.refs_3_, ...), custom_call_target="tpu_custom_call" | custom-call | bytes 18000000 | tf_op jit(solution)/shard_map/last_part/pallas_call | solution.py:508
  (33 shorter events, 3.6 us)
Async XLA Ops:
  0.6 1.3 %copy-start = (f32[32,9,1024]{2,0,1:T(8,128)S(1)}, f32[32,9,1024]{2,0,1:T(8,128)}, u32[]{:S(2)}) copy-start(f32[32,9,1024]{2,0,1:T(8,128)} %param.9) | copy-start | bytes 3538948
  1.9 1.2 %copy-start.2 = (f32[2,32,16,256]{3,2,1,0:T(8,128)S(1)}, f32[2,32,16,256]{3,2,1,0:T(8,128)}, u32[]{:S(2)}) copy-start(f32[2,32,16,256]{3,2,1,0:T(8,128)} %refs_3_.1) | copy-start | bytes 3145732
  3.1 0.7 %copy-start.5 = (s32[3,32]{1,0:T(4,128)S(1)}, s32[3,32]{1,0:T(4,128)}, u32[]{:S(2)}) copy-start(s32[3,32]{1,0:T(4,128)} %refs_8_.3) | copy-start | bytes 1156
  3.8 0.7 copy-start.6
  4.5 10.3 %copy-start.4 = (f32[32,16,256]{2,1,0:T(8,128)S(1)}, f32[32,16,256]{2,1,0:T(8,128)}, u32[]{:S(2)}) copy-start(f32[32,16,256]{2,1,0:T(8,128)} %refs_1_.3) | copy-start | bytes 1572868
  7.6 12.9 %collective-permute-start = (f32[784,128]{1,0:T(8,128)S(1)}, f32[784,128]{1,0:T(8,128)S(1)}, u32[]{:S(2)}, u32[]{:S(2)}) collective-permute-start(f32[784,128]{1,0:T(8,128)S(1)} %get-tuple-element.21), channel_id=1, source_target_pairs={{0,1},{1,2},{2,3},{3,4},{4,5},{5,6},{6,7},{7,8},{8,9},{9,10},{10,1... | collective-permute-start | bytes 1204232 | tf_op jit(solution)/shard_map/ppermute | solution.py:421
  7.7 12.8 %collective-permute-start.1 = (f32[784,128]{1,0:T(8,128)S(1)}, f32[784,128]{1,0:T(8,128)S(1)}, u32[]{:S(2)}, u32[]{:S(2)}) collective-permute-start(f32[784,128]{1,0:T(8,128)S(1)} %get-tuple-element.22), channel_id=1, source_target_pairs={{0,31},{1,0},{2,1},{3,2},{4,3},{5,4},{6,5},{7,6},{8,7},{9,8},{10,9... | collective-permute-start | bytes 1204232 | tf_op jit(solution)/shard_map/ppermute | solution.py:421
  9.5 11.1 %collective-permute-start.3 = (f32[8,128]{1,0:T(8,128)S(1)}, f32[8,128]{1,0:T(8,128)S(1)}, u32[]{:S(2)}, u32[]{:S(2)}) collective-permute-start(f32[8,128]{1,0:T(8,128)S(1)} %get-tuple-element.23.refs_2_.part), channel_id=1, source_target_pairs={{0,30},{1,31},{2,0},{3,1},{4,2},{5,3},{6,4},{7,5},{8,6},{9,7},{10,... | collective-permute-start | bytes 12296 | tf_op jit(solution)/shard_map/ppermute | solution.py:421
  10.2 10.3 %collective-permute-start.2 = (f32[8,128]{1,0:T(8,128)S(1)}, f32[8,128]{1,0:T(8,128)S(1)}, u32[]{:S(2)}, u32[]{:S(2)}) collective-permute-start(f32[8,128]{1,0:T(8,128)S(1)} %get-tuple-element.23.refs_2_.part), channel_id=1, source_target_pairs={{0,2},{1,3},{2,4},{3,5},{4,6},{5,7},{6,8},{7,9},{8,10},{9,11},{10,... | collective-permute-start | bytes 12296 | tf_op jit(solution)/shard_map/ppermute | solution.py:421
  20.8 13.2 %collective-permute-start.4 = (f32[424,128]{1,0:T(8,128)S(1)}, f32[424,128]{1,0:T(8,128)S(1)}, u32[]{:S(2)}, u32[]{:S(2)}) collective-permute-start(f32[424,128]{1,0:T(8,128)S(1)} %get-tuple-element.26), channel_id=1, source_target_pairs={{0,32},{32,64},{64,96},{96,128},{128,160},{160,192},{192,224},{224... | collective-permute-start | bytes 651272 | tf_op jit(solution)/shard_map/ppermute | solution.py:421
  21.7 12.3 %collective-permute-start.5 = (f32[424,128]{1,0:T(8,128)S(1)}, f32[424,128]{1,0:T(8,128)S(1)}, u32[]{:S(2)}, u32[]{:S(2)}) collective-permute-start(f32[424,128]{1,0:T(8,128)S(1)} %get-tuple-element.27), channel_id=1, source_target_pairs={{0,224},{32,0},{64,32},{96,64},{128,96},{160,128},{192,160},{224,1... | collective-permute-start | bytes 651272 | tf_op jit(solution)/shard_map/ppermute | solution.py:421
  25.7 8.3 %copy-start.1 = (f32[32,9,1024]{2,0,1:T(8,128)S(1)}, f32[32,9,1024]{2,0,1:T(8,128)}, u32[]{:S(2)}) copy-start(f32[32,9,1024]{2,0,1:T(8,128)} %param.9) | copy-start | bytes 3538948
  25.7 8.3 %copy-start.7 = (f32[9]{0:T(128)S(1)}, f32[9]{0:T(128)}, u32[]{:S(2)}) copy-start(f32[9]{0:T(128)} %refs_7_.3) | copy-start | bytes 112
  25.7 4.8 %collective-permute-start.7 = (f32[40,128]{1,0:T(8,128)S(1)}, f32[40,128]{1,0:T(8,128)S(1)}, u32[]{:S(2)}, u32[]{:S(2)}) collective-permute-start(f32[40,128]{1,0:T(8,128)S(1)} %get-tuple-element.28.refs_5_), channel_id=1, source_target_pairs={{0,192},{32,224},{64,0},{96,32},{128,64},{160,96},{192,128},{224,1... | collective-permute-start | bytes 61448 | tf_op jit(solution)/shard_map/ppermute | solution.py:421
  28.1 5.9 %collective-permute-start.6 = (f32[40,128]{1,0:T(8,128)S(1)}, f32[40,128]{1,0:T(8,128)S(1)}, u32[]{:S(2)}, u32[]{:S(2)}) collective-permute-start(f32[40,128]{1,0:T(8,128)S(1)} %get-tuple-element.28.refs_5_), channel_id=1, source_target_pairs={{0,64},{32,96},{64,128},{96,160},{128,192},{160,224},{192,0},{224,... | collective-permute-start | bytes 61448 | tf_op jit(solution)/shard_map/ppermute | solution.py:421
  29.8 17.6 %copy-start.3 = (f32[2,32,16,256]{3,2,1,0:T(8,128)S(1)}, f32[2,32,16,256]{3,2,1,0:T(8,128)}, u32[]{:S(2)}) copy-start(f32[2,32,16,256]{3,2,1,0:T(8,128)} %refs_3_.1) | copy-start | bytes 3145732
  39.9 13.3 %collective-permute-start.8 = (f32[784,128]{1,0:T(8,128)S(1)}, f32[784,128]{1,0:T(8,128)S(1)}, u32[]{:S(2)}, u32[]{:S(2)}) collective-permute-start(f32[784,128]{1,0:T(8,128)S(1)} %get-tuple-element.32), channel_id=1, source_target_pairs={{0,1},{1,2},{2,3},{3,4},{4,5},{5,6},{6,7},{7,8},{8,9},{9,10},{10,1... | collective-permute-start | bytes 1204232 | tf_op jit(solution)/shard_map/ppermute | solution.py:421
  40.0 13.2 %collective-permute-start.9 = (f32[784,128]{1,0:T(8,128)S(1)}, f32[784,128]{1,0:T(8,128)S(1)}, u32[]{:S(2)}, u32[]{:S(2)}) collective-permute-start(f32[784,128]{1,0:T(8,128)S(1)} %get-tuple-element.33), channel_id=1, source_target_pairs={{0,31},{1,0},{2,1},{3,2},{4,3},{5,4},{6,5},{7,6},{8,7},{9,8},{10,9... | collective-permute-start | bytes 1204232 | tf_op jit(solution)/shard_map/ppermute | solution.py:421
  41.7 11.5 %collective-permute-start.11 = (f32[8,128]{1,0:T(8,128)S(1)}, f32[8,128]{1,0:T(8,128)S(1)}, u32[]{:S(2)}, u32[]{:S(2)}) collective-permute-start(f32[8,128]{1,0:T(8,128)S(1)} %get-tuple-element.30.refs_2_.part), channel_id=1, source_target_pairs={{0,30},{1,31},{2,0},{3,1},{4,2},{5,3},{6,4},{7,5},{8,6},{9,7},{10,... | collective-permute-start | bytes 12296 | tf_op jit(solution)/shard_map/ppermute | solution.py:421
  41.7 11.5 %collective-permute-start.10 = (f32[8,128]{1,0:T(8,128)S(1)}, f32[8,128]{1,0:T(8,128)S(1)}, u32[]{:S(2)}, u32[]{:S(2)}) collective-permute-start(f32[8,128]{1,0:T(8,128)S(1)} %get-tuple-element.30.refs_2_.part), channel_id=1, source_target_pairs={{0,2},{1,3},{2,4},{3,5},{4,6},{5,7},{6,8},{7,9},{8,10},{9,11},{10,... | collective-permute-start | bytes 12296 | tf_op jit(solution)/shard_map/ppermute | solution.py:421
  53.5 9.5 %collective-permute-start.12 = (f32[424,128]{1,0:T(8,128)S(1)}, f32[424,128]{1,0:T(8,128)S(1)}, u32[]{:S(2)}, u32[]{:S(2)}) collective-permute-start(f32[424,128]{1,0:T(8,128)S(1)} %get-tuple-element.37), channel_id=1, source_target_pairs={{0,32},{32,64},{64,96},{96,128},{128,160},{160,192},{192,224},{224... | collective-permute-start | bytes 651272 | tf_op jit(solution)/shard_map/ppermute | solution.py:421
  54.6 8.4 %collective-permute-start.13 = (f32[424,128]{1,0:T(8,128)S(1)}, f32[424,128]{1,0:T(8,128)S(1)}, u32[]{:S(2)}, u32[]{:S(2)}) collective-permute-start(f32[424,128]{1,0:T(8,128)S(1)} %get-tuple-element.38), channel_id=1, source_target_pairs={{0,224},{32,0},{64,32},{96,64},{128,96},{160,128},{192,160},{224,1... | collective-permute-start | bytes 651272 | tf_op jit(solution)/shard_map/ppermute | solution.py:421
  56.8 5.7 %collective-permute-start.15 = (f32[40,128]{1,0:T(8,128)S(1)}, f32[40,128]{1,0:T(8,128)S(1)}, u32[]{:S(2)}, u32[]{:S(2)}) collective-permute-start(f32[40,128]{1,0:T(8,128)S(1)} %get-tuple-element.39.refs_5_), channel_id=1, source_target_pairs={{0,192},{32,224},{64,0},{96,32},{128,64},{160,96},{192,128},{224,1... | collective-permute-start | bytes 61448 | tf_op jit(solution)/shard_map/ppermute | solution.py:421
  57.1 5.9 %collective-permute-start.14 = (f32[40,128]{1,0:T(8,128)S(1)}, f32[40,128]{1,0:T(8,128)S(1)}, u32[]{:S(2)}, u32[]{:S(2)}) collective-permute-start(f32[40,128]{1,0:T(8,128)S(1)} %get-tuple-element.39.refs_5_), channel_id=1, source_target_pairs={{0,64},{32,96},{64,128},{96,160},{128,192},{160,224},{192,0},{224,... | collective-permute-start | bytes 61448 | tf_op jit(solution)/shard_map/ppermute | solution.py:421

commit v2 on v1

--- a/solution.py
+++ b/solution.py
@@ -46,19 +46,37 @@
     return lax.broadcasted_iota(jnp.int32, shape, axis)
 
 
+def swap_list_row(tiles):
+    row = iota((8, LANES), 0)
+    for d in (1, 2, 4):
+        first = (row & d) == 0
+        new = list(tiles)
+        for k in range(8):
+            if k & d == 0:
+                low, high = (tiles[k], tiles[k | d])
+                new[k] = jnp.where(first, low, pltpu.roll(high, d, 0))
+                new[k | d] = jnp.where(first, pltpu.roll(low, 8 - d, 0), high)
+        tiles = new
+    return tiles
+
+
+def turned(tile, lanes):
+    return pltpu.roll(tile, lanes % LANES, 1) if lanes % LANES else tile
+
+
+def swap_list_group(tiles):
+    group = iota((8, LANES), 1) // 16
+    tiles = [turned(tile, 16 * k) for k, tile in enumerate(tiles)]
+    tiles = [tiles[-k % 8] for k in range(8)]
+    for d in (1, 2, 4):
+        moved = (group & d) != 0
+        tiles = [jnp.where(moved, tiles[(k - d) % 8], tiles[k]) for k in range(8)]
+    return [turned(tile, -16 * k) for k, tile in enumerate(tiles)]
+
+
 def swap_groups(x):
-    row = iota((1, 8, LANES), 1)
-    group = iota((1, 8, LANES), 2) // 16
-    for d in (4, 2, 1):
-        row_bit, group_bit = ((row & d) != 0, (group & d) != 0)
-        later = pltpu.roll(pltpu.roll(x, 8 - d, 1), 16 * d, 2)
-        if d == 4:
-            other = later
-        else:
-            earlier = pltpu.roll(pltpu.roll(x, d, 1), LANES - 16 * d, 2)
-            other = jnp.where(group_bit, later, earlier)
-        x = jnp.where(row_bit == group_bit, x, other)
-    return x
+    tiles = swap_list_row([x[k] for k in range(8)])
+    return jnp.stack(swap_list_row(swap_list_group(tiles)))
 
 
 def corner(offset_ref, slot):
@@ -102,65 +120,87 @@
     part[...] = lax.fori_loop(0, GROUPS, group_step, block, unroll=True)
 
 
-def pack(work, part, y_up, y_down, x_up, x_down):
+def pack_y(work, part, up, down):
     for n in range(PLANES):
         o, x, half = (n // (2 * CX), n // 2 % CX, n % 2)
-        y_down[BLOCK + REACH * n : BLOCK + REACH * n + 8, :] = work[o, x, half, 0:8, :]
+        down[BLOCK + REACH * n : BLOCK + REACH * n + 8, :] = work[o, x, half, 0:8, :]
     for n in reversed(range(PLANES)):
         o, x, half = (n // (2 * CX), n // 2 % CX, n % 2)
-        y_up[REACH * (n + 1) : REACH * (n + 1) + 8, :] = work[o, x, half, 8:16, :]
-    for target in (y_up, y_down):
-        target[0:BLOCK, :] = part[...]
+        up[REACH * (n + 1) : REACH * (n + 1) + 8, :] = work[o, x, half, 8:16, :]
+    for target in (up, down):
+        if part is not None:
+            target[0:BLOCK, :] = part[...]
         target[Y_ROWS - 8 : Y_ROWS, :] = jnp.zeros((8, LANES), F32)
+
+
+def pack_x(work, x_up, x_down):
     for o in range(ORB):
         rows = slice(o * REACH * 32, (o + 1) * REACH * 32)
         x_up[rows, :] = work[o, CX - REACH : CX].reshape(REACH * 32, LANES)
         x_down[rows, :] = work[o, 0:REACH].reshape(REACH * 32, LANES)
 
 
-def first_kernel(v, proj_hbm, offset_hbm, atom_hbm, y_up, y_down, x_up, x_down, part,
-                 work, proj_ref, offset_ref, atom_ref, sems):
+def is_odd():
+    return lax.axis_index("gy") % 2
+
+
+def first_kernel(v, proj_hbm, offset_hbm, atom_hbm, y_pair, y_next, x_up, x_down, part,
+                 work, proj_ref, offset_ref, atom_ref, block, packed, xs_up, xs_down, sems):
     copies = [
-        pltpu.make_async_copy(offset_hbm, offset_ref, sems.at[0]),
-        pltpu.make_async_copy(atom_hbm, atom_ref, sems.at[1]),
-        pltpu.make_async_copy(v.at[:, :, :, 0:LANES], work.at[:, :, 0], sems.at[2]),
-        pltpu.make_async_copy(v.at[:, :, :, LANES:NZ], work.at[:, :, 1], sems.at[3]),
+        pltpu.make_async_copy(v.at[:, :, :, 0:LANES], work.at[:, :, 0], sems.at[0]),
+        pltpu.make_async_copy(v.at[:, :, :, LANES:NZ], work.at[:, :, 1], sems.at[1]),
+        pltpu.make_async_copy(offset_hbm, offset_ref, sems.at[2]),
+        pltpu.make_async_copy(atom_hbm, atom_ref, sems.at[3]),
         pltpu.make_async_copy(proj_hbm, proj_ref, sems.at[4]),
     ]
     for copy in copies:
         copy.start()
-    for copy in copies:
+    for copy in copies[:2]:
         copy.wait()
-    project(work, proj_ref, offset_ref, atom_ref, part)
-    pack(work, part, y_up, y_down, x_up, x_down)
+    pack_y(work, None, packed.at[0], packed.at[1])
+    pack_x(work, xs_up, xs_down)
+    odd = is_odd()
+    halos = [
+        pltpu.make_async_copy(
+            source.at[pl.ds(start, rows)], target.at[pl.ds(start, rows)], sems.at[5 + k]
+        )
+        for k, (source, target, start, rows) in enumerate(
+            (
+                (packed.at[odd], y_pair, BLOCK, Y_ROWS - BLOCK),
+                (packed.at[1 - odd], y_next, BLOCK, Y_ROWS - BLOCK),
+                (xs_up, x_up, 0, X_ROWS),
+                (xs_down, x_down, 0, X_ROWS),
+            )
+        )
+    ]
+    for copy in halos:
+        copy.start()
+    for copy in copies[2:]:
+        copy.wait()
+    project(work, proj_ref, offset_ref, atom_ref, block)
+    blocks = [
+        pltpu.make_async_copy(block, target.at[pl.ds(0, BLOCK)], sems.at[9 + k])
+        for k, target in enumerate((y_pair, y_next, part))
+    ]
+    for copy in blocks:
+        copy.start()
+    for copy in halos + blocks:
+        copy.wait()
+
+
+def halves_of(field, split):
+    if split:
+        return [field[:, :, half] for half in range(2)]
+    return [field[:, :, :, LANES * half : LANES * (half + 1)] for half in range(2)]
 
 
 def local_kernel(scale, second, *refs):
     if second:
-        field, potential, _, orbital, full, out, pad, along_z = refs
-        halves = [field[:, :, half] for half in range(2)]
-        for half in range(2):
-            full[:, :, :, LANES * half : LANES * (half + 1)] = halves[half]
+        field, potential, orbital, out, pad = refs
     else:
-        field, potential, _, out, pad, along_z = refs
-        halves = [field[:, :, :, LANES * half : LANES * (half + 1)] for half in range(2)]
+        field, potential, out, pad = refs
+    halves = halves_of(field, second)
     weights = [scale * KINETIC / HALF_WIDTH * w for w in LAPLACE_COEFFS]
-
-    gap = jnp.abs(iota((NZ, NZ), 0) - iota((NZ, NZ), 1))
-    band = jnp.zeros((NZ, NZ), F32)
-    for r in range(1, REACH + 1):
-        band = jnp.where(gap == r, weights[r], band)
-    summed = None
-    for half in range(2):
-        term = jnp.dot(
-            halves[half].reshape(ORB * CX * CY, LANES),
-            band[LANES * half : LANES * (half + 1)],
-            precision=lax.Precision.HIGHEST,
-            preferred_element_type=F32,
-        )
-        summed = term if summed is None else summed + term
-    along_z[...] = summed
-
     for o in range(ORB):
         for x in range(REACH):
             pad[o, x, :, 8:24, :] = jnp.zeros((2, CY, LANES), F32)
@@ -181,8 +221,6 @@
                     3.0 * weights[0] - scale * CENTER / HALF_WIDTH
                 )
                 total = factor * here
-                depth = pl.ds(pl.multiple_of(n * CY + 8 * t, 8), 8)
-                total = total + along_z[depth, lanes]
                 for r in range(1, REACH + 1):
                     paired = (
                         pad[o, x + REACH + r, half, rows, :] + pad[o, x + REACH - r, half, rows, :]
@@ -200,46 +238,93 @@
     lax.fori_loop(0, ORB * CX, step, 0)
 
 
-def edge_kernel(scale, before_ref, after_ref, local, out, before, after, sems):
-    copies = [
-        pltpu.make_async_copy(before_ref, before, sems.at[0]),
-        pltpu.make_async_copy(after_ref, after, sems.at[1]),
+def edge_kernel(scale, second, pair_ref, next_ref, local, field, *refs):
+    if second:
+        full, out, along_z, before, after, sems = refs
+    else:
+        out, along_z, before, after, sems = refs
+    odd = is_odd()
+    even_copies = [
+        pltpu.make_async_copy(next_ref, before, sems.at[0]),
+        pltpu.make_async_copy(pair_ref, after, sems.at[1]),
     ]
-    for copy in copies:
-        copy.start()
+    odd_copies = [
+        pltpu.make_async_copy(pair_ref, before, sems.at[0]),
+        pltpu.make_async_copy(next_ref, after, sems.at[1]),
+    ]
+
+    @pl.when(odd == 0)
+    def _():
+        for copy in even_copies:
+            copy.start()
+
+    @pl.when(odd == 1)
+    def _():
+        for copy in odd_copies:
+            copy.start()
+
+    halves = halves_of(field, second)
+    if second:
+        for half in range(2):
+            full[:, :, :, LANES * half : LANES * (half + 1)] = halves[half]
+    gap = jnp.abs(iota((NZ, NZ), 0) - iota((NZ, NZ), 1))
+    band = jnp.zeros((NZ, NZ), F32)
+    for r in range(1, REACH + 1):
+        weight = scale * KINETIC / HALF_WIDTH * LAPLACE_COEFFS[r]
+        band = jnp.where(gap == r, weight, band)
+    summed = None
+    for half in range(2):
+        term = jnp.dot(
+            halves[half].reshape(ORB * CX * CY, LANES),
+            band[LANES * half : LANES * (half + 1)],
+            precision=lax.Precision.HIGHEST,
+            preferred_element_type=F32,
+        )
+        summed = term if summed is None else summed + term
+    along_z[...] = summed
     row = iota((8, LANES), 0)
     low, high = ([None], [None])
     for r in range(1, REACH + 1):
         weight = scale * KINETIC / HALF_WIDTH * LAPLACE_COEFFS[r]
         low.append(jnp.where(row < r, weight, 0.0).astype(F32))
         high.append(jnp.where(row >= 8 - r, weight, 0.0).astype(F32))
-    for copy in copies:
-        copy.wait()
+
+    @pl.when(odd == 0)
+    def _():
+        for copy in even_copies:
+            copy.wait()
+
+    @pl.when(odd == 1)
+    def _():
+        for copy in odd_copies:
+            copy.wait()
 
     def step(n, carry):
         o, x = (n // CX, n % CX)
+        depth = pl.multiple_of(n * CY, CY)
         for half in range(2):
+            lanes = slice(LANES * half, LANES * (half + 1))
             start = (n * 2 + half) * REACH
-            first = local[o, x, half, 0:8, :]
-            second = local[o, x, half, 8:16, :]
+            first = local[o, x, half, 0:8, :] + along_z[pl.ds(depth, 8), lanes]
+            second_rows = local[o, x, half, 8:16, :] + along_z[pl.ds(depth + 8, 8), lanes]
             for r in range(1, REACH + 1):
                 first = first + low[r] * before[pl.ds(start + BLOCK + REACH - r, 8), :]
-                second = second + high[r] * after[pl.ds(start + r, 8), :]
+                second_rows = second_rows + high[r] * after[pl.ds(start + r, 8), :]
             out[o, x, half, 0:8, :] = first
-            out[o, x, half, 8:16, :] = second
+            out[o, x, half, 8:16, :] = second_rows
         return carry
 
     lax.fori_loop(0, ORB * CX, step, 0, unroll=4)
 
 
-def gather_kernel(two_before, before, part, after, two_after, x_up_in, x_down_in, local,
+def gather_kernel(pair, after_pair, part, chips, after_chips, x_up_in, x_down_in, local,
                   x_up, x_down, column, sems):
     sources = (
-        two_before,
-        before.at[0:BLOCK],
+        pair.at[0:BLOCK],
+        after_pair.at[0:BLOCK],
         part,
-        after.at[0:BLOCK],
-        two_after,
+        chips,
+        after_chips,
     )
     copies = []
     for k, source in enumerate(sources):
@@ -378,12 +463,21 @@
 
 
 def middle_kernel(scale, local, before_ref, after_ref, two_before, two_after, column, proj_ref,
-                  strength_ref, offset_ref, atom_ref, work, y_up, y_down, x_up, x_down, part,
+                  strength_ref, offset_ref, atom_ref, work, y_pair, y_next, x_up, x_down, part,
                   *scratch):
     finish(scale, local, before_ref, after_ref, two_before, two_after, column, proj_ref,
            strength_ref, offset_ref, atom_ref, work, *scratch)
     project(work, proj_ref, offset_ref, atom_ref, part)
-    pack(work, part, y_up, y_down, x_up, x_down)
+    pack_x(work, x_up, x_down)
+    odd = is_odd()
+
+    @pl.when(odd == 0)
+    def _():
+        pack_y(work, part, y_pair, y_next)
+
+    @pl.when(odd == 1)
+    def _():
+        pack_y(work, part, y_next, y_pair)
 
 
 def last_kernel(scale, local, before_ref, after_ref, two_before, two_after, column, proj_ref,
@@ -421,45 +515,53 @@
     return lax.ppermute(value, axis, [(i, (i + step) % devices) for i in range(devices)])
 
 
-def local_part(scale, field, potential, part, orbital):
+def swapped(value, span, later):
+    devices = lax.axis_size("gy")
+    pairs = []
+    for i in range(devices):
+        up = (i // span + later) % 2 == 0
+        pairs.append((i, (i + (span if up else -span)) % devices))
+    return lax.ppermute(value, "gy", pairs)
+
+
+def local_part(scale, field, potential, orbital):
     second = orbital is not None
-    args = (field, potential, part) + ((orbital,) if second else ())
+    args = (field, potential) + ((orbital,) if second else ())
 
     def local_body(*refs):
         local_kernel(scale, second, *refs)
 
     return pl.pallas_call(
         local_body,
-        out_shape=(shaped(*FIELD), shaped(*WORK)) if second else shaped(*WORK),
-        in_specs=[VMEM, VMEM, ANY] + [VMEM] * (len(args) - 3),
-        out_specs=(VMEM, VMEM) if second else VMEM,
-        scratch_shapes=[
-            pltpu.VMEM((ORB, CX + 2 * REACH, 2, 32, LANES), F32),
-            pltpu.VMEM((ORB * CX * CY, NZ), F32),
-        ],
+        out_shape=shaped(*WORK),
+        in_specs=[VMEM] * len(args),
+        out_specs=VMEM,
+        scratch_shapes=[pltpu.VMEM((ORB, CX + 2 * REACH, 2, 32, LANES), F32)],
         compiler_params=PARAMS,
         cost_estimate=cost(4),
         name="local_part",
     )(*args)
 
 
-def edge_part(scale, before, after, local):
+def edge_part(scale, before, after, local, field, second):
     def edge_body(*refs):
-        edge_kernel(scale, *refs)
+        edge_kernel(scale, second, *refs)
 
     return pl.pallas_call(
         edge_body,
-        out_shape=shaped(*WORK),
-        in_specs=[ANY, ANY, VMEM],
-        out_specs=VMEM,
-        scratch_shapes=[pltpu.VMEM((Y_ROWS, LANES), F32)] * 2 + [pltpu.SemaphoreType.DMA((2,))],
+        out_shape=(shaped(*FIELD), shaped(*WORK)) if second else shaped(*WORK),
+        in_specs=[ANY, ANY, VMEM, VMEM],
+        out_specs=(VMEM, VMEM) if second else VMEM,
+        scratch_shapes=[pltpu.VMEM((ORB * CX * CY, NZ), F32)]
+        + [pltpu.VMEM((Y_ROWS, LANES), F32)] * 2
+        + [pltpu.SemaphoreType.DMA((2,))],
         compiler_params=PARAMS,
         cost_estimate=cost(2),
         name="edge_part",
-    )(before, after, local)
-
-
-def gather_part(two_before, before, part, after, two_after, x_up, x_down, local):
+    )(before, after, local, field)
+
+
+def gather_part(pair, after_pair, part, chips, after_chips, x_up, x_down, local):
     return pl.pallas_call(
         gather_kernel,
         out_shape=(SENT[2], SENT[3], shaped(COLUMN, LANES)),
@@ -470,28 +572,30 @@
         compiler_params=PARAMS,
         cost_estimate=cost(1),
         name="gather_part",
-    )(two_before, before, part, after, two_after, x_up, x_down, local)
+    )(pair, after_pair, part, chips, after_chips, x_up, x_down, local)
 
 
 def apply(scale, field, potential, sent, orbital, shared):
     second = orbital is not None
-    y_up, y_down, x_up, x_down, part = sent
+    y_pair, y_next, x_up, x_down, part = sent
     projectors, strengths, offsets, atoms = shared
-    y_before = shift(y_up, "gy", 1)
-    y_after = shift(y_down, "gy", -1)
-    y_two_before = shift(part, "gy", 2)
-    y_two_after = shift(part, "gy", -2)
-    local = local_part(scale, field, potential, part, orbital)
-    if second:
-        full, local = local
+    next_one = swapped(y_next, 1, 1)
+    next_two = swapped(part, 2, 1)
+    pair_two = swapped(part, 2, 0)
+    pair_one = swapped(y_pair, 1, 0)
+    if not second:
+        field, part = lax.optimization_barrier((field, part))
+    local = local_part(scale, field, potential, orbital)
     x_up, x_down, column = gather_part(
-        y_two_before, y_before, part, y_after, y_two_after, x_up, x_down, local
+        pair_one, next_one, part, pair_two, next_two, x_up, x_down, local
     )
     x_before = shift(x_up, "gx", 1)
     x_after = shift(x_down, "gx", -1)
     x_two_before = shift(column, "gx", 2)
     x_two_after = shift(column, "gx", -2)
-    local = edge_part(scale, y_before, y_after, local)
+    local = edge_part(scale, pair_one, next_one, local, field, second)
+    if second:
+        full, local = local
     kernel = last_kernel if second else middle_kernel
 
     def end_body(*refs):
@@ -526,15 +630,19 @@
         first_kernel,
         out_shape=SENT,
         in_specs=[HBM] * 4,
-        out_specs=(VMEM,) * 5,
+        out_specs=(HBM,) * 5,
         scratch_shapes=[
             pltpu.VMEM(WORK, F32),
             pltpu.VMEM((NPROJ, SLOTS, 8 * LANES), F32),
             pltpu.SMEM((3, SLOTS), jnp.int32),
             pltpu.SMEM((SLOTS,), jnp.int32),
-            pltpu.SemaphoreType.DMA((5,)),
+            pltpu.VMEM((BLOCK, LANES), F32),
+            pltpu.VMEM((2, Y_ROWS, LANES), F32),
+            pltpu.VMEM((X_ROWS, LANES), F32),
+            pltpu.VMEM((X_ROWS, LANES), F32),
+            pltpu.SemaphoreType.DMA((12,)),
         ],
-        compiler_params=PARAMS,
+        compiler_params=pltpu.CompilerParams(vmem_limit_bytes=60 * 1024 * 1024),
         cost_estimate=cost(3),
         name="first_part",
     )(orbitals, projectors, slot_offset, slot_atom)

time: 68.6 us -> 64.1 us (0.934); the launches traced: 67.4 us -> 64 us
  local copies, waits for them, and re-layouts: 3.84 us -> 0.03 us
  waiting for transfers between devices: 7.65 us -> 6.44 us
  Pallas kernels: 26.3 us -> 27.5 us
    ppermute x0 -> x8, starting transfers between devices: none -> 11.3 us  [swapped(): return lax.ppermute(value, 'gy', pairs)]
    ppermute x16 -> x8, starting transfers between devices: 28.7 us -> 17.7 us  [shift(): lax.ppermute(value, axis, [(i, (i + step) % devices) for i in range(devic...]
    ppermute x16 -> x8, waiting for transfers between devices: 7.65 us -> 0.02 us  [shift(): lax.ppermute(value, axis, [(i, (i + step) % devices) for i in range(devic...]
    ppermute x0 -> x8, waiting for transfers between devices: none -> 6.42 us  [swapped(): return lax.ppermute(value, 'gy', pairs)]
    unnamed x16 -> x18, local copies, waits for them, and re-layouts: 3.84 us -> 0.03 us
    pallas_call x1, Pallas kernels: 3.15 us -> 4.43 us  [shards(): pl.pallas_call(first_kernel, out_shape=SENT, in_specs=[HBM] * 4, out_spec...]
  transfers between devices with their start and end apart: 16 -> 16, of which waited for: 6 -> 2; matrix products, arithmetic and copies ran while one was open for 0% -> 0% of each run, Pallas kernels for 19% -> 20%
where the time goes in v2:
time: 64.1 us; the launch traced here: 64 us
  starting transfers between devices  29 us (45%)
  Pallas kernels  27.5 us (43%)
  waiting for transfers between devices  6.44 us (10%)
  between operations  1.05 us (2%)
    ppermute x8, starting transfers between devices, shift(): lax.ppermute(value, axis, [(i, (i + step) % devices) for i in range(devic...  17.7 us
    ppermute x8, starting transfers between devices, swapped(): return lax.ppermute(value, 'gy', pairs)  11.3 us
    pallas_call x2, Pallas kernels, apply(): pl.pallas_call(end_body, out_shape=shaped(*FIELD) if second else (shaped(...  9.85 us
    pallas_call x2, Pallas kernels, edge_part(): pl.pallas_call(edge_body, out_shape=(shaped(*FIELD), shaped(*WORK)) if se...  7.2 us
    ppermute x8, waiting for transfers between devices, swapped(): return lax.ppermute(value, 'gy', pairs)  6.42 us
    pallas_call x2, Pallas kernels, local_part(): pl.pallas_call(local_body, out_shape=shaped(*WORK), in_specs=[VMEM] * len...  5.52 us
    pallas_call x1, Pallas kernels, shards(): pl.pallas_call(first_kernel, out_shape=SENT, in_specs=[HBM] * 4, out_spec...  4.43 us
  transfers between devices with their start and end apart: 16, of which 2 were waited for; matrix products, arithmetic and copies ran while one was open for 0% of the time, Pallas kernels for 20%

profile of v2, /device:TPU:30, one launch (start us, length us, event | category | flops | bytes accessed | tf_op | source)
XLA Modules:
  0.0 64.0 jit_solution(8102875055934623411)
XLA Ops:
  0.6 4.4 %first_part.1 = (f32[784,128]{1,0:T(8,128)}, f32[784,128]{1,0:T(8,128)}, f32[424,128]{1,0:T(8,128)}, f32[424,128]{1,0:T(8,128)}, f32[8,128]{1,0:T(8,128)}) custom-call(f32[2,32,16,256]{3,2,1,0:T(8,128)} %refs_2_.1, f32[9,32,1024]{2,1,0:T(8,128)} %bitcast.1, s32[3,32]{1,0:T(4,128)} %refs_8_.3, s32[32]{0:T(128)} %refs_9_.3), custom_call_target="tpu_custom_call" | custom-call | bytes 9000000 | tf_op jit(solution)/shard_map/first_part/pallas_call | solution.py:629
  5.2 0.9 %collective-permute-start.1 = (f32[784,128]{1,0:T(8,128)}, f32[784,128]{1,0:T(8,128)S(1)}, u32[]{:S(2)}, u32[]{:S(2)}) collective-permute-start(f32[784,128]{1,0:T(8,128)} %get-tuple-element.24), channel_id=1, source_target_pairs={{0,31},{1,2},{2,1},{3,4},{4,3},{5,6},{6,5},{7,8},{8,7},{9,10},{10,... | collective-permute-start | bytes 1204232 | tf_op jit(solution)/shard_map/ppermute | solution.py:524
  6.1 0.4 collective-permute-start.2
  6.5 4.2 %collective-permute-start.3 = (f32[8,128]{1,0:T(8,128)}, f32[8,128]{1,0:T(8,128)S(1)}, u32[]{:S(2)}, u32[]{:S(2)}) collective-permute-start(f32[8,128]{1,0:T(8,128)} %get-tuple-element.27.part), channel_id=1, source_target_pairs={{0,30},{1,31},{2,4},{3,5},{4,2},{5,3},{6,8},{7,9},{8,6},{9,7},{10,... | collective-permute-start | bytes 12296 | tf_op jit(solution)/shard_map/ppermute | solution.py:524
  10.7 2.7 %local_part.2.refs_2_.local = f32[2,32,2,16,128]{4,3,2,1,0:T(8,128)S(1)} custom-call(f32[2,32,16,256]{3,2,1,0:T(8,128)S(1)} %copy-done, f32[32,16,256]{2,1,0:T(8,128)S(1)} %copy-done.2), custom_call_target="tpu_custom_call" | custom-call | bytes 12000000 | tf_op jit(solution)/shard_map/local_part/pallas_call | solution.py:534
  13.5 3.3 %collective-permute-done.3.after_chips = f32[8,128]{1,0:T(8,128)S(1)} collective-permute-done((f32[8,128]{1,0:T(8,128)}, f32[8,128]{1,0:T(8,128)S(1)}, u32[]{:S(2)}, u32[]{:S(2)}) %collective-permute-start.3) | collective-permute-done | bytes 4128 | tf_op jit(solution)/shard_map/ppermute | solution.py:524
  16.8 0.2 gather_part.2
  17.1 2.0 %collective-permute-start.4 = (f32[424,128]{1,0:T(8,128)S(1)}, f32[424,128]{1,0:T(8,128)S(1)}, u32[]{:S(2)}, u32[]{:S(2)}) collective-permute-start(f32[424,128]{1,0:T(8,128)S(1)} %get-tuple-element.30), channel_id=1, source_target_pairs={{0,32},{32,64},{64,96},{96,128},{128,160},{160,192},{192,224},{224... | collective-permute-start | bytes 651272 | tf_op jit(solution)/shard_map/ppermute | solution.py:515
  19.1 4.0 %collective-permute-start.5 = (f32[424,128]{1,0:T(8,128)S(1)}, f32[424,128]{1,0:T(8,128)S(1)}, u32[]{:S(2)}, u32[]{:S(2)}) collective-permute-start(f32[424,128]{1,0:T(8,128)S(1)} %get-tuple-element.31), channel_id=1, source_target_pairs={{0,224},{32,0},{64,32},{96,64},{128,96},{160,128},{192,160},{224,1... | collective-permute-start | bytes 651272 | tf_op jit(solution)/shard_map/ppermute | solution.py:515
  23.2 4.1 %collective-permute-start.7 = (f32[40,128]{1,0:T(8,128)S(1)}, f32[40,128]{1,0:T(8,128)S(1)}, u32[]{:S(2)}, u32[]{:S(2)}) collective-permute-start(f32[40,128]{1,0:T(8,128)S(1)} %get-tuple-element.32.refs_5_), channel_id=1, source_target_pairs={{0,192},{32,224},{64,0},{96,32},{128,64},{160,96},{192,128},{224,1... | collective-permute-start | bytes 61448 | tf_op jit(solution)/shard_map/ppermute | solution.py:515
  27.3 3.1 %edge_part.2.refs_0_ = f32[2,32,2,16,128]{4,3,2,1,0:T(8,128)S(1)} custom-call(f32[784,128]{1,0:T(8,128)S(1)} %collective-permute-done.refs_0_.pair, f32[784,128]{1,0:T(8,128)S(1)} %collective-permute-done.1.refs_1_.after_pair, f32[2,32,2,16,128]{4,3,2,1,0:T(8,128)S(1)} %local_part.2.refs_2_.local, f32[2,32,16,256]{3,2,1,0:T(8,128)S(1)} %copy-done), custom_call_target="tpu_custom_call" | custom-call | bytes 6000000 | tf_op jit(solution)/shard_map/edge_part/pallas_call | solution.py:550
  30.5 5.4 %middle_part.1 = (f32[2,32,2,16,128]{4,3,2,1,0:T(8,128)S(1)}, f32[784,128]{1,0:T(8,128)S(1)}, f32[784,128]{1,0:T(8,128)S(1)}, f32[424,128]{1,0:T(8,128)S(1)}, f3...) custom-call(f32[2,32,2,16,128]{4,3,2,1,0:T(8,128)S(1)} %edge_part.2.refs_0_, f32[424,128]{1,0:T(8,128)S(1)} %collective-permute-done.4.refs_1_, ...), custom_call_target="tpu_custom_call" | custom-call | bytes 18000000 | tf_op jit(solution)/shard_map/middle_part/pallas_call | solution.py:612
  36.0 0.3 collective-permute-start.8
  36.4 0.1 collective-permute-start.10
  36.5 5.2 %collective-permute-start.11 = (f32[8,128]{1,0:T(8,128)S(1)}, f32[8,128]{1,0:T(8,128)S(1)}, u32[]{:S(2)}, u32[]{:S(2)}) collective-permute-start(f32[8,128]{1,0:T(8,128)S(1)} %get-tuple-element.38.part), channel_id=1, source_target_pairs={{0,30},{1,31},{2,4},{3,5},{4,2},{5,3},{6,8},{7,9},{8,6},{9,7},{10,... | collective-permute-start | bytes 12296 | tf_op jit(solution)/shard_map/ppermute | solution.py:524
  41.7 2.8 %local_part.3.refs_2_.local = f32[2,32,2,16,128]{4,3,2,1,0:T(8,128)S(1)} custom-call(f32[2,32,2,16,128]{4,3,2,1,0:T(8,128)S(1)} %get-tuple-element.35.refs_0_.refs_3_, f32[32,16,256]{2,1,0:T(8,128)S(1)} %copy-done.2, f32[2,32,16,256]{3,2,1,0:T(8,128)S(1)} %copy-done), custom_call_target="tpu_custom_call" | custom-call | bytes 12000000 | tf_op jit(solution)/shard_map/local_part/pallas_call | solution.py:534
  44.5 3.1 %collective-permute-done.11.after_chips = f32[8,128]{1,0:T(8,128)S(1)} collective-permute-done((f32[8,128]{1,0:T(8,128)S(1)}, f32[8,128]{1,0:T(8,128)S(1)}, u32[]{:S(2)}, u32[]{:S(2)}) %collective-permute-start.11) | collective-permute-done | bytes 4128 | tf_op jit(solution)/shard_map/ppermute | solution.py:524
  47.6 0.2 gather_part.3
  47.9 0.4 collective-permute-start.12
  48.2 3.0 %collective-permute-start.13 = (f32[424,128]{1,0:T(8,128)S(1)}, f32[424,128]{1,0:T(8,128)S(1)}, u32[]{:S(2)}, u32[]{:S(2)}) collective-permute-start(f32[424,128]{1,0:T(8,128)S(1)} %get-tuple-element.42), channel_id=1, source_target_pairs={{0,224},{32,0},{64,32},{96,64},{128,96},{160,128},{192,160},{224,1... | collective-permute-start | bytes 651272 | tf_op jit(solution)/shard_map/ppermute | solution.py:515
  51.2 2.2 %collective-permute-start.14 = (f32[40,128]{1,0:T(8,128)S(1)}, f32[40,128]{1,0:T(8,128)S(1)}, u32[]{:S(2)}, u32[]{:S(2)}) collective-permute-start(f32[40,128]{1,0:T(8,128)S(1)} %get-tuple-element.43.refs_5_), channel_id=1, source_target_pairs={{0,64},{32,96},{64,128},{96,160},{128,192},{160,224},{192,0},{224,... | collective-permute-start | bytes 61448 | tf_op jit(solution)/shard_map/ppermute | solution.py:515
  53.4 1.9 %collective-permute-start.15 = (f32[40,128]{1,0:T(8,128)S(1)}, f32[40,128]{1,0:T(8,128)S(1)}, u32[]{:S(2)}, u32[]{:S(2)}) collective-permute-start(f32[40,128]{1,0:T(8,128)S(1)} %get-tuple-element.43.refs_5_), channel_id=1, source_target_pairs={{0,192},{32,224},{64,0},{96,32},{128,64},{160,96},{192,128},{224,1... | collective-permute-start | bytes 61448 | tf_op jit(solution)/shard_map/ppermute | solution.py:515
  55.3 4.1 %edge_part.3 = (f32[2,32,16,256]{3,2,1,0:T(8,128)}, f32[2,32,2,16,128]{4,3,2,1,0:T(8,128)S(1)}) custom-call(f32[784,128]{1,0:T(8,128)S(1)} %collective-permute-done.8.refs_0_.pair, f32[784,128]{1,0:T(8,128)S(1)} %collective-permute-done.9.refs_1_.after_pair, f32[2,32,2,16,128]{4,3,2,1,0:T(8,128)S(1)} %local_part.3.refs_2_.local, ...), custom_call_target="tpu_custom_call" | custom-call | bytes 6000000 | tf_op jit(solution)/shard_map/edge_part/pallas_call | solution.py:550
  59.5 4.4 %last_part.1 = f32[2,32,16,256]{3,2,1,0:T(8,128)} custom-call(f32[2,32,2,16,128]{4,3,2,1,0:T(8,128)S(1)} %get-tuple-element.37.refs_0_, f32[424,128]{1,0:T(8,128)S(1)} %collective-permute-done.12.refs_1_, f32[424,128]{1,0:T(8,128)S(1)} %collective-permute-done.13.refs_2_, f32[40,128]{1,0:T(8,128)S(1)} %collective-permute-done.14.refs_3_, ...), custom_call_target="tpu_custom_call" | custom-call | bytes 18000000 | tf_op jit(solution)/shard_map/last_part/pallas_call | solution.py:612
  (35 shorter events, 0.3 us)
Async XLA Ops:
  0.6 10.1 %copy-start = (f32[2,32,16,256]{3,2,1,0:T(8,128)S(1)}, f32[2,32,16,256]{3,2,1,0:T(8,128)}, u32[]{:S(2)}) copy-start(f32[2,32,16,256]{3,2,1,0:T(8,128)} %refs_2_.1) | copy-start | bytes 3145732
  0.6 10.1 %copy-start.2 = (f32[32,16,256]{2,1,0:T(8,128)S(1)}, f32[32,16,256]{2,1,0:T(8,128)}, u32[]{:S(2)}) copy-start(f32[32,16,256]{2,1,0:T(8,128)} %refs_1_.3) | copy-start | bytes 1572868
  5.1 11.7 %collective-permute-start = (f32[784,128]{1,0:T(8,128)}, f32[784,128]{1,0:T(8,128)S(1)}, u32[]{:S(2)}, u32[]{:S(2)}) collective-permute-start(f32[784,128]{1,0:T(8,128)} %get-tuple-element.23), channel_id=1, source_target_pairs={{0,1},{1,0},{2,3},{3,2},{4,5},{5,4},{6,7},{7,6},{8,9},{9,8},{10,11... | collective-permute-start | bytes 1204232 | tf_op jit(solution)/shard_map/ppermute | solution.py:524
  5.2 11.6 %collective-permute-start.1 = (f32[784,128]{1,0:T(8,128)}, f32[784,128]{1,0:T(8,128)S(1)}, u32[]{:S(2)}, u32[]{:S(2)}) collective-permute-start(f32[784,128]{1,0:T(8,128)} %get-tuple-element.24), channel_id=1, source_target_pairs={{0,31},{1,2},{2,1},{3,4},{4,3},{5,6},{6,5},{7,8},{8,7},{9,10},{10,... | collective-permute-start | bytes 1204232 | tf_op jit(solution)/shard_map/ppermute | solution.py:524
  6.1 10.7 %copy-start.3 = (f32[424,128]{1,0:T(8,128)S(1)}, f32[424,128]{1,0:T(8,128)}, u32[]{:S(2)}) copy-start(f32[424,128]{1,0:T(8,128)} %get-tuple-element.28.x_up_in) | copy-start | bytes 651268
  6.1 10.7 %copy-start.4 = (f32[424,128]{1,0:T(8,128)S(1)}, f32[424,128]{1,0:T(8,128)}, u32[]{:S(2)}) copy-start(f32[424,128]{1,0:T(8,128)} %get-tuple-element.29.x_down_in) | copy-start | bytes 651268
  6.1 10.7 %copy-start.7 = (f32[8,128]{1,0:T(8,128)S(1)}, f32[8,128]{1,0:T(8,128)}, u32[]{:S(2)}) copy-start(f32[8,128]{1,0:T(8,128)} %get-tuple-element.27.part) | copy-start | bytes 12292
  6.1 7.4 %collective-permute-start.2 = (f32[8,128]{1,0:T(8,128)}, f32[8,128]{1,0:T(8,128)S(1)}, u32[]{:S(2)}, u32[]{:S(2)}) collective-permute-start(f32[8,128]{1,0:T(8,128)} %get-tuple-element.27.part), channel_id=1, source_target_pairs={{0,2},{1,3},{2,0},{3,1},{4,6},{5,7},{6,4},{7,5},{8,10},{9,11},{10,... | collective-permute-start | bytes 12296 | tf_op jit(solution)/shard_map/ppermute | solution.py:524
  6.5 10.3 %collective-permute-start.3 = (f32[8,128]{1,0:T(8,128)}, f32[8,128]{1,0:T(8,128)S(1)}, u32[]{:S(2)}, u32[]{:S(2)}) collective-permute-start(f32[8,128]{1,0:T(8,128)} %get-tuple-element.27.part), channel_id=1, source_target_pairs={{0,30},{1,31},{2,4},{3,5},{4,2},{5,3},{6,8},{7,9},{8,6},{9,7},{10,... | collective-permute-start | bytes 12296 | tf_op jit(solution)/shard_map/ppermute | solution.py:524
  17.1 13.4 %collective-permute-start.4 = (f32[424,128]{1,0:T(8,128)S(1)}, f32[424,128]{1,0:T(8,128)S(1)}, u32[]{:S(2)}, u32[]{:S(2)}) collective-permute-start(f32[424,128]{1,0:T(8,128)S(1)} %get-tuple-element.30), channel_id=1, source_target_pairs={{0,32},{32,64},{64,96},{96,128},{128,160},{160,192},{192,224},{224... | collective-permute-start | bytes 651272 | tf_op jit(solution)/shard_map/ppermute | solution.py:515
  19.1 11.4 %collective-permute-start.5 = (f32[424,128]{1,0:T(8,128)S(1)}, f32[424,128]{1,0:T(8,128)S(1)}, u32[]{:S(2)}, u32[]{:S(2)}) collective-permute-start(f32[424,128]{1,0:T(8,128)S(1)} %get-tuple-element.31), channel_id=1, source_target_pairs={{0,224},{32,0},{64,32},{96,64},{128,96},{160,128},{192,160},{224,1... | collective-permute-start | bytes 651272 | tf_op jit(solution)/shard_map/ppermute | solution.py:515
  23.1 7.4 %copy-start.5 = (s32[3,32]{1,0:T(4,128)S(1)}, s32[3,32]{1,0:T(4,128)}, u32[]{:S(2)}) copy-start(s32[3,32]{1,0:T(4,128)} %refs_8_.3) | copy-start | bytes 1156
  23.1 7.4 %copy-start.6 = (s32[32]{0:T(128)S(1)}, s32[32]{0:T(128)}, u32[]{:S(2)}) copy-start(s32[32]{0:T(128)} %refs_9_.3) | copy-start | bytes 388
  23.1 7.4 %copy-start.8 = (f32[9]{0:T(128)S(1)}, f32[9]{0:T(128)}, u32[]{:S(2)}) copy-start(f32[9]{0:T(128)} %refs_7_.3) | copy-start | bytes 112
  23.1 7.3 %collective-permute-start.6 = (f32[40,128]{1,0:T(8,128)S(1)}, f32[40,128]{1,0:T(8,128)S(1)}, u32[]{:S(2)}, u32[]{:S(2)}) collective-permute-start(f32[40,128]{1,0:T(8,128)S(1)} %get-tuple-element.32.refs_5_), channel_id=1, source_target_pairs={{0,64},{32,96},{64,128},{96,160},{128,192},{160,224},{192,0},{224,... | collective-permute-start | bytes 61448 | tf_op jit(solution)/shard_map/ppermute | solution.py:515
  23.2 7.3 %collective-permute-start.7 = (f32[40,128]{1,0:T(8,128)S(1)}, f32[40,128]{1,0:T(8,128)S(1)}, u32[]{:S(2)}, u32[]{:S(2)}) collective-permute-start(f32[40,128]{1,0:T(8,128)S(1)} %get-tuple-element.32.refs_5_), channel_id=1, source_target_pairs={{0,192},{32,224},{64,0},{96,32},{128,64},{160,96},{192,128},{224,1... | collective-permute-start | bytes 61448 | tf_op jit(solution)/shard_map/ppermute | solution.py:515
  36.0 11.7 %collective-permute-start.8 = (f32[784,128]{1,0:T(8,128)S(1)}, f32[784,128]{1,0:T(8,128)S(1)}, u32[]{:S(2)}, u32[]{:S(2)}) collective-permute-start(f32[784,128]{1,0:T(8,128)S(1)} %get-tuple-element.33), channel_id=1, source_target_pairs={{0,1},{1,0},{2,3},{3,2},{4,5},{5,4},{6,7},{7,6},{8,9},{9,8},{10,11... | collective-permute-start | bytes 1204232 | tf_op jit(solution)/shard_map/ppermute | solution.py:524
  36.2 11.4 %collective-permute-start.9 = (f32[784,128]{1,0:T(8,128)S(1)}, f32[784,128]{1,0:T(8,128)S(1)}, u32[]{:S(2)}, u32[]{:S(2)}) collective-permute-start(f32[784,128]{1,0:T(8,128)S(1)} %get-tuple-element.34), channel_id=1, source_target_pairs={{0,31},{1,2},{2,1},{3,4},{4,3},{5,6},{6,5},{7,8},{8,7},{9,10},{10,... | collective-permute-start | bytes 1204232 | tf_op jit(solution)/shard_map/ppermute | solution.py:524
  36.4 8.2 %collective-permute-start.10 = (f32[8,128]{1,0:T(8,128)S(1)}, f32[8,128]{1,0:T(8,128)S(1)}, u32[]{:S(2)}, u32[]{:S(2)}) collective-permute-start(f32[8,128]{1,0:T(8,128)S(1)} %get-tuple-element.38.part), channel_id=1, source_target_pairs={{0,2},{1,3},{2,0},{3,1},{4,6},{5,7},{6,4},{7,5},{8,10},{9,11},{10,... | collective-permute-start | bytes 12296 | tf_op jit(solution)/shard_map/ppermute | solution.py:524
  36.5 11.2 %collective-permute-start.11 = (f32[8,128]{1,0:T(8,128)S(1)}, f32[8,128]{1,0:T(8,128)S(1)}, u32[]{:S(2)}, u32[]{:S(2)}) collective-permute-start(f32[8,128]{1,0:T(8,128)S(1)} %get-tuple-element.38.part), channel_id=1, source_target_pairs={{0,30},{1,31},{2,4},{3,5},{4,2},{5,3},{6,8},{7,9},{8,6},{9,7},{10,... | collective-permute-start | bytes 12296 | tf_op jit(solution)/shard_map/ppermute | solution.py:524
  47.9 11.6 %collective-permute-start.12 = (f32[424,128]{1,0:T(8,128)S(1)}, f32[424,128]{1,0:T(8,128)S(1)}, u32[]{:S(2)}, u32[]{:S(2)}) collective-permute-start(f32[424,128]{1,0:T(8,128)S(1)} %get-tuple-element.41), channel_id=1, source_target_pairs={{0,32},{32,64},{64,96},{96,128},{128,160},{160,192},{192,224},{224... | collective-permute-start | bytes 651272 | tf_op jit(solution)/shard_map/ppermute | solution.py:515
  48.2 11.2 %collective-permute-start.13 = (f32[424,128]{1,0:T(8,128)S(1)}, f32[424,128]{1,0:T(8,128)S(1)}, u32[]{:S(2)}, u32[]{:S(2)}) collective-permute-start(f32[424,128]{1,0:T(8,128)S(1)} %get-tuple-element.42), channel_id=1, source_target_pairs={{0,224},{32,0},{64,32},{96,64},{128,96},{160,128},{192,160},{224,1... | collective-permute-start | bytes 651272 | tf_op jit(solution)/shard_map/ppermute | solution.py:515
  51.2 8.2 %collective-permute-start.14 = (f32[40,128]{1,0:T(8,128)S(1)}, f32[40,128]{1,0:T(8,128)S(1)}, u32[]{:S(2)}, u32[]{:S(2)}) collective-permute-start(f32[40,128]{1,0:T(8,128)S(1)} %get-tuple-element.43.refs_5_), channel_id=1, source_target_pairs={{0,64},{32,96},{64,128},{96,160},{128,192},{160,224},{192,0},{224,... | collective-permute-start | bytes 61448 | tf_op jit(solution)/shard_map/ppermute | solution.py:515
  53.4 6.0 %collective-permute-start.15 = (f32[40,128]{1,0:T(8,128)S(1)}, f32[40,128]{1,0:T(8,128)S(1)}, u32[]{:S(2)}, u32[]{:S(2)}) collective-permute-start(f32[40,128]{1,0:T(8,128)S(1)} %get-tuple-element.43.refs_5_), channel_id=1, source_target_pairs={{0,192},{32,224},{64,0},{96,32},{128,64},{160,96},{192,128},{224,1... | collective-permute-start | bytes 61448 | tf_op jit(solution)/shard_map/ppermute | solution.py:515
  (1 other events, 7.4 us)

commit v3 on v2

--- a/solution.py
+++ b/solution.py
@@ -211,31 +211,31 @@
             pad[o, REACH : REACH + CX, half, 8:24, :] = halves[half][o]
 
     def step(n, carry):
-        o, x = (n // CX, n % CX)
+        o, x = (n // (CX // 4), n % (CX // 4) * 4)
         for half in range(2):
             lanes = slice(LANES * half, LANES * (half + 1))
             for t in range(2):
                 rows = slice(8 + 8 * t, 16 + 8 * t)
-                here = pad[o, x + REACH, half, rows, :]
-                factor = potential[x, 8 * t : 8 * t + 8, lanes] * (scale / HALF_WIDTH) + (
-                    3.0 * weights[0] - scale * CENTER / HALF_WIDTH
-                )
-                total = factor * here
-                for r in range(1, REACH + 1):
-                    paired = (
-                        pad[o, x + REACH + r, half, rows, :] + pad[o, x + REACH - r, half, rows, :]
+                line = [pad[o, x + k, half, rows, :] for k in range(4 + 2 * REACH)]
+                for q in range(4):
+                    factor = potential[x + q, 8 * t : 8 * t + 8, lanes] * (scale / HALF_WIDTH) + (
+                        3.0 * weights[0] - scale * CENTER / HALF_WIDTH
                     )
-                    paired = paired + (
-                        pad[o, x + REACH, half, 8 + 8 * t + r : 16 + 8 * t + r, :]
-                        + pad[o, x + REACH, half, 8 + 8 * t - r : 16 + 8 * t - r, :]
-                    )
-                    total = total + weights[r] * paired
-                if second:
-                    total = total - orbital[o, x, 8 * t : 8 * t + 8, lanes]
-                out[o, x, half, 8 * t : 8 * t + 8, :] = total
+                    middle = q + REACH
+                    total = factor * line[middle]
+                    for r in range(1, REACH + 1):
+                        paired = line[middle + r] + line[middle - r]
+                        paired = paired + (
+                            pad[o, x + middle, half, 8 + 8 * t + r : 16 + 8 * t + r, :]
+                            + pad[o, x + middle, half, 8 + 8 * t - r : 16 + 8 * t - r, :]
+                        )
+                        total = total + weights[r] * paired
+                    if second:
+                        total = total - orbital[o, x + q, 8 * t : 8 * t + 8, lanes]
+                    out[o, x + q, half, 8 * t : 8 * t + 8, :] = total
         return carry
 
-    lax.fori_loop(0, ORB * CX, step, 0)
+    lax.fori_loop(0, ORB * CX // 4, step, 0)
 
 
 def edge_kernel(scale, second, pair_ref, next_ref, local, field, *refs):
@@ -265,22 +265,31 @@
 
     halves = halves_of(field, second)
     if second:
-        for half in range(2):
-            full[:, :, :, LANES * half : LANES * (half + 1)] = halves[half]
+        fulls = [
+            pltpu.make_async_copy(
+                field.at[:, :, half],
+                full.at[:, :, :, LANES * half : LANES * (half + 1)],
+                sems.at[2 + half],
+            )
+            for half in range(2)
+        ]
+        for copy in fulls:
+            copy.start()
     gap = jnp.abs(iota((NZ, NZ), 0) - iota((NZ, NZ), 1))
     band = jnp.zeros((NZ, NZ), F32)
     for r in range(1, REACH + 1):
         weight = scale * KINETIC / HALF_WIDTH * LAPLACE_COEFFS[r]
         band = jnp.where(gap == r, weight, band)
-    summed = None
-    for half in range(2):
-        term = jnp.dot(
-            halves[half].reshape(ORB * CX * CY, LANES),
-            band[LANES * half : LANES * (half + 1)],
-            precision=lax.Precision.HIGHEST,
-            preferred_element_type=F32,
-        )
-        summed = term if summed is None else summed + term
+    values = jnp.concatenate(
+        [half.reshape(ORB * CX * CY, LANES) for half in halves], axis=1
+    )
+    value_high = values.astype(jnp.bfloat16)
+    value_low = (values - value_high.astype(F32)).astype(jnp.bfloat16)
+    band_high = band.astype(jnp.bfloat16)
+    band_low = (band - band_high.astype(F32)).astype(jnp.bfloat16)
+    summed = jnp.dot(value_high, band_high, preferred_element_type=F32)
+    summed = summed + jnp.dot(value_low, band_high, preferred_element_type=F32)
+    summed = summed + jnp.dot(value_high, band_low, preferred_element_type=F32)
     along_z[...] = summed
     row = iota((8, LANES), 0)
     low, high = ([None], [None])
@@ -315,6 +324,9 @@
         return carry
 
     lax.fori_loop(0, ORB * CX, step, 0, unroll=4)
+    if second:
+        for copy in fulls:
+            copy.wait()
 
 
 def gather_kernel(pair, after_pair, part, chips, after_chips, x_up_in, x_down_in, local,
@@ -374,23 +386,15 @@
     return total
 
 
-def finish(scale, local, before_ref, after_ref, two_before, two_after, column, proj_ref,
-           strength_ref, offset_ref, atom_ref, work, before, after, table, held, split, sems):
+def finish(scale, local, before, after, two_before, two_after, column, proj_ref,
+           strength_ref, offset_ref, atom_ref, work, table, held, split):
     weights = [scale * KINETIC / HALF_WIDTH * w for w in LAPLACE_COEFFS]
-    copies = [
-        pltpu.make_async_copy(before_ref, before, sems.at[0]),
-        pltpu.make_async_copy(after_ref, after, sems.at[1]),
-    ]
-    for copy in copies:
-        copy.start()
     work[:, REACH : CX - REACH] = local[:, REACH : CX - REACH]
     count = 0
     for s in range(SLOTS):
         split[count] = s
         z = offset_ref[2, s]
         count = count + jnp.where((z > LANES - 16) & (z < LANES), 1, 0)
-    for copy in copies:
-        copy.wait()
     table[...] = coefficients(
         (
             column[...],
@@ -551,10 +555,10 @@
         edge_body,
         out_shape=(shaped(*FIELD), shaped(*WORK)) if second else shaped(*WORK),
         in_specs=[ANY, ANY, VMEM, VMEM],
-        out_specs=(VMEM, VMEM) if second else VMEM,
+        out_specs=(HBM, VMEM) if second else VMEM,
         scratch_shapes=[pltpu.VMEM((ORB * CX * CY, NZ), F32)]
         + [pltpu.VMEM((Y_ROWS, LANES), F32)] * 2
-        + [pltpu.SemaphoreType.DMA((2,))],
+        + [pltpu.SemaphoreType.DMA((4,))],
         compiler_params=PARAMS,
         cost_estimate=cost(2),
         name="edge_part",
@@ -602,17 +606,14 @@
         kernel(scale, *refs)
 
     scratch = [
-        pltpu.VMEM((X_ROWS + COLUMN, LANES), F32),
-        pltpu.VMEM((X_ROWS + COLUMN, LANES), F32),
         pltpu.VMEM((SLOTS, LANES), F32),
         pltpu.VMEM((GROUPS, ORB, 8, 8, LANES), F32),
         pltpu.SMEM((SLOTS + 1,), jnp.int32),
-        pltpu.SemaphoreType.DMA((2,)),
     ]
     result = pl.pallas_call(
         end_body,
         out_shape=shaped(*FIELD) if second else (shaped(*WORK),) + SENT,
-        in_specs=[VMEM, ANY, ANY, VMEM, VMEM, VMEM, VMEM] + [SMEM] * 3,
+        in_specs=[VMEM] * 7 + [SMEM] * 3,
         out_specs=VMEM if second else (VMEM,) * 6,
         scratch_shapes=([pltpu.VMEM(WORK, F32)] if second else []) + scratch,
         compiler_params=PARAMS,

time: 64.1 us -> 61.9 us (0.966)
  Pallas kernels: 27.5 us -> 20.9 us
  waiting for transfers between devices: 6.44 us -> 11.5 us
    pallas_call x2, Pallas kernels: 7.2 us -> 3.82 us  [edge_part(): pl.pallas_call(edge_body, out_shape=(shaped(*FIELD), shaped(*WORK)) if se...]
    ppermute x8, waiting for transfers between devices: 0.02 us -> 3.38 us  [shift(): lax.ppermute(value, axis, [(i, (i + step) % devices) for i in range(devic...]
    pallas_call x2, Pallas kernels: 5.52 us -> 3.84 us  [local_part(): pl.pallas_call(local_body, out_shape=shaped(*WORK), in_specs=[VMEM] * len...]
    ppermute x8, waiting for transfers between devices: 6.42 us -> 8.09 us  [swapped(): return lax.ppermute(value, 'gy', pairs)]
    pallas_call x2, Pallas kernels: 9.85 us -> 8.27 us  [apply(): pl.pallas_call(end_body, out_shape=shaped(*FIELD) if second else (shaped(...]
  transfers between devices with their start and end apart: 16 -> 16, of which waited for: 2 -> 4; matrix products, arithmetic and copies ran while one was open for 0% -> 0% of each run, Pallas kernels for 20% -> 12%
where the time goes in v3:
time: 61.9 us; the launch traced here: 62 us
  starting transfers between devices  28.8 us (47%)
  Pallas kernels  20.9 us (34%)
  waiting for transfers between devices  11.5 us (19%)
  between operations  0.85 us (1%)
    ppermute x8, starting transfers between devices, shift(): lax.ppermute(value, axis, [(i, (i + step) % devices) for i in range(devic...  17.6 us
    ppermute x8, starting transfers between devices, swapped(): return lax.ppermute(value, 'gy', pairs)  11.2 us
    pallas_call x2, Pallas kernels, apply(): pl.pallas_call(end_body, out_shape=shaped(*FIELD) if second else (shaped(...  8.27 us
    ppermute x8, waiting for transfers between devices, swapped(): return lax.ppermute(value, 'gy', pairs)  8.09 us
    pallas_call x1, Pallas kernels, shards(): pl.pallas_call(first_kernel, out_shape=SENT, in_specs=[HBM] * 4, out_spec...  4.44 us
    pallas_call x2, Pallas kernels, local_part(): pl.pallas_call(local_body, out_shape=shaped(*WORK), in_specs=[VMEM] * len...  3.84 us
    pallas_call x2, Pallas kernels, edge_part(): pl.pallas_call(edge_body, out_shape=(shaped(*FIELD), shaped(*WORK)) if se...  3.82 us
    ppermute x8, waiting for transfers between devices, shift(): lax.ppermute(value, axis, [(i, (i + step) % devices) for i in range(devic...  3.38 us
  transfers between devices with their start and end apart: 16, of which 4 were waited for; matrix products, arithmetic and copies ran while one was open for 0% of the time, Pallas kernels for 12%

profile of v3, /device:TPU:30, one launch (start us, length us, event | category | flops | bytes accessed | tf_op | source)
XLA Modules:
  0.0 62.0 jit_solution(2528848363503634145)
XLA Ops:
  0.6 4.4 %first_part.1 = (f32[784,128]{1,0:T(8,128)}, f32[784,128]{1,0:T(8,128)}, f32[424,128]{1,0:T(8,128)}, f32[424,128]{1,0:T(8,128)}, f32[8,128]{1,0:T(8,128)}) custom-call(f32[2,32,16,256]{3,2,1,0:T(8,128)} %refs_2_.1, f32[9,32,1024]{2,1,0:T(8,128)} %bitcast.1, s32[3,32]{1,0:T(4,128)} %refs_8_.3, s32[32]{0:T(128)} %refs_9_.3), custom_call_target="tpu_custom_call" | custom-call | bytes 9000000 | tf_op jit(solution)/shard_map/first_part/pallas_call | solution.py:630
  5.2 0.8 %collective-permute-start.1 = (f32[784,128]{1,0:T(8,128)}, f32[784,128]{1,0:T(8,128)S(1)}, u32[]{:S(2)}, u32[]{:S(2)}) collective-permute-start(f32[784,128]{1,0:T(8,128)} %get-tuple-element.24), channel_id=1, source_target_pairs={{0,31},{1,2},{2,1},{3,4},{4,3},{5,6},{6,5},{7,8},{8,7},{9,10},{10,... | collective-permute-start | bytes 1204232 | tf_op jit(solution)/shard_map/ppermute | solution.py:528
  6.0 0.5 collective-permute-start.2
  6.5 4.3 %collective-permute-start.3 = (f32[8,128]{1,0:T(8,128)}, f32[8,128]{1,0:T(8,128)S(1)}, u32[]{:S(2)}, u32[]{:S(2)}) collective-permute-start(f32[8,128]{1,0:T(8,128)} %get-tuple-element.27.part), channel_id=1, source_target_pairs={{0,30},{1,31},{2,4},{3,5},{4,2},{5,3},{6,8},{7,9},{8,6},{9,7},{10,... | collective-permute-start | bytes 12296 | tf_op jit(solution)/shard_map/ppermute | solution.py:528
  10.8 1.9 %local_part.2.refs_2_.local = f32[2,32,2,16,128]{4,3,2,1,0:T(8,128)S(1)} custom-call(f32[2,32,16,256]{3,2,1,0:T(8,128)S(1)} %copy-done, f32[32,16,256]{2,1,0:T(8,128)S(1)} %copy-done.2), custom_call_target="tpu_custom_call" | custom-call | bytes 12000000 | tf_op jit(solution)/shard_map/local_part/pallas_call | solution.py:538
  12.7 4.1 %collective-permute-done.3.after_chips = f32[8,128]{1,0:T(8,128)S(1)} collective-permute-done((f32[8,128]{1,0:T(8,128)}, f32[8,128]{1,0:T(8,128)S(1)}, u32[]{:S(2)}, u32[]{:S(2)}) %collective-permute-start.3) | collective-permute-done | bytes 4128 | tf_op jit(solution)/shard_map/ppermute | solution.py:528
  16.8 0.2 gather_part.2
  17.1 2.0 %collective-permute-start.4 = (f32[424,128]{1,0:T(8,128)S(1)}, f32[424,128]{1,0:T(8,128)S(1)}, u32[]{:S(2)}, u32[]{:S(2)}) collective-permute-start(f32[424,128]{1,0:T(8,128)S(1)} %get-tuple-element.30), channel_id=1, source_target_pairs={{0,32},{32,64},{64,96},{96,128},{128,160},{160,192},{192,224},{224... | collective-permute-start | bytes 651272 | tf_op jit(solution)/shard_map/ppermute | solution.py:519
  19.1 4.0 %collective-permute-start.5 = (f32[424,128]{1,0:T(8,128)S(1)}, f32[424,128]{1,0:T(8,128)S(1)}, u32[]{:S(2)}, u32[]{:S(2)}) collective-permute-start(f32[424,128]{1,0:T(8,128)S(1)} %get-tuple-element.31), channel_id=1, source_target_pairs={{0,224},{32,0},{64,32},{96,64},{128,96},{160,128},{192,160},{224,1... | collective-permute-start | bytes 651272 | tf_op jit(solution)/shard_map/ppermute | solution.py:519
  23.2 4.1 %collective-permute-start.7 = (f32[40,128]{1,0:T(8,128)S(1)}, f32[40,128]{1,0:T(8,128)S(1)}, u32[]{:S(2)}, u32[]{:S(2)}) collective-permute-start(f32[40,128]{1,0:T(8,128)S(1)} %get-tuple-element.32.refs_5_), channel_id=1, source_target_pairs={{0,192},{32,224},{64,0},{96,32},{128,64},{160,96},{192,128},{224,1... | collective-permute-start | bytes 61448 | tf_op jit(solution)/shard_map/ppermute | solution.py:519
  27.3 1.9 %edge_part.2.refs_0_ = f32[2,32,2,16,128]{4,3,2,1,0:T(8,128)S(1)} custom-call(f32[784,128]{1,0:T(8,128)S(1)} %collective-permute-done.refs_0_.pair, f32[784,128]{1,0:T(8,128)S(1)} %collective-permute-done.1.refs_1_.after_pair, f32[2,32,2,16,128]{4,3,2,1,0:T(8,128)S(1)} %local_part.2.refs_2_.local, f32[2,32,16,256]{3,2,1,0:T(8,128)S(1)} %copy-done), custom_call_target="tpu_custom_call" | custom-call | bytes 6000000 | tf_op jit(solution)/shard_map/edge_part/pallas_call | solution.py:554
  29.2 0.9 %collective-permute-done.6.refs_3_ = f32[40,128]{1,0:T(8,128)S(1)} collective-permute-done((f32[40,128]{1,0:T(8,128)S(1)}, f32[40,128]{1,0:T(8,128)S(1)}, u32[]{:S(2)}, u32[]{:S(2)}) %collective-permute-start.6) | collective-permute-done | bytes 20512 | tf_op jit(solution)/shard_map/ppermute | solution.py:519
  30.1 4.7 %middle_part.1 = (f32[2,32,2,16,128]{4,3,2,1,0:T(8,128)S(1)}, f32[784,128]{1,0:T(8,128)S(1)}, f32[784,128]{1,0:T(8,128)S(1)}, f32[424,128]{1,0:T(8,128)S(1)}, f3...) custom-call(f32[2,32,2,16,128]{4,3,2,1,0:T(8,128)S(1)} %edge_part.2.refs_0_, f32[424,128]{1,0:T(8,128)S(1)} %collective-permute-done.4.refs_1_, ...), custom_call_target="tpu_custom_call" | custom-call | bytes 18000000 | tf_op jit(solution)/shard_map/middle_part/pallas_call | solution.py:613
  35.0 0.3 collective-permute-start.10
  35.3 5.1 %collective-permute-start.11 = (f32[8,128]{1,0:T(8,128)S(1)}, f32[8,128]{1,0:T(8,128)S(1)}, u32[]{:S(2)}, u32[]{:S(2)}) collective-permute-start(f32[8,128]{1,0:T(8,128)S(1)} %get-tuple-element.38.part), channel_id=1, source_target_pairs={{0,30},{1,31},{2,4},{3,5},{4,2},{5,3},{6,8},{7,9},{8,6},{9,7},{10,... | collective-permute-start | bytes 12296 | tf_op jit(solution)/shard_map/ppermute | solution.py:528
  40.3 1.9 %local_part.3.refs_2_.local = f32[2,32,2,16,128]{4,3,2,1,0:T(8,128)S(1)} custom-call(f32[2,32,2,16,128]{4,3,2,1,0:T(8,128)S(1)} %get-tuple-element.35.refs_0_.refs_3_, f32[32,16,256]{2,1,0:T(8,128)S(1)} %copy-done.2, f32[2,32,16,256]{3,2,1,0:T(8,128)S(1)} %copy-done), custom_call_target="tpu_custom_call" | custom-call | bytes 12000000 | tf_op jit(solution)/shard_map/local_part/pallas_call | solution.py:538
  42.3 4.0 %collective-permute-done.11.after_chips = f32[8,128]{1,0:T(8,128)S(1)} collective-permute-done((f32[8,128]{1,0:T(8,128)S(1)}, f32[8,128]{1,0:T(8,128)S(1)}, u32[]{:S(2)}, u32[]{:S(2)}) %collective-permute-start.11) | collective-permute-done | bytes 4128 | tf_op jit(solution)/shard_map/ppermute | solution.py:528
  46.5 0.8 %collective-permute-start.12 = (f32[424,128]{1,0:T(8,128)S(1)}, f32[424,128]{1,0:T(8,128)S(1)}, u32[]{:S(2)}, u32[]{:S(2)}) collective-permute-start(f32[424,128]{1,0:T(8,128)S(1)} %get-tuple-element.41), channel_id=1, source_target_pairs={{0,32},{32,64},{64,96},{96,128},{128,160},{160,192},{192,224},{224... | collective-permute-start | bytes 651272 | tf_op jit(solution)/shard_map/ppermute | solution.py:519
  47.3 2.5 %collective-permute-start.13 = (f32[424,128]{1,0:T(8,128)S(1)}, f32[424,128]{1,0:T(8,128)S(1)}, u32[]{:S(2)}, u32[]{:S(2)}) collective-permute-start(f32[424,128]{1,0:T(8,128)S(1)} %get-tuple-element.42), channel_id=1, source_target_pairs={{0,224},{32,0},{64,32},{96,64},{128,96},{160,128},{192,160},{224,1... | collective-permute-start | bytes 651272 | tf_op jit(solution)/shard_map/ppermute | solution.py:519
  49.8 3.0 %collective-permute-start.14 = (f32[40,128]{1,0:T(8,128)S(1)}, f32[40,128]{1,0:T(8,128)S(1)}, u32[]{:S(2)}, u32[]{:S(2)}) collective-permute-start(f32[40,128]{1,0:T(8,128)S(1)} %get-tuple-element.43.refs_5_), channel_id=1, source_target_pairs={{0,64},{32,96},{64,128},{96,160},{128,192},{160,224},{192,0},{224,... | collective-permute-start | bytes 61448 | tf_op jit(solution)/shard_map/ppermute | solution.py:519
  52.8 1.1 %collective-permute-start.15 = (f32[40,128]{1,0:T(8,128)S(1)}, f32[40,128]{1,0:T(8,128)S(1)}, u32[]{:S(2)}, u32[]{:S(2)}) collective-permute-start(f32[40,128]{1,0:T(8,128)S(1)} %get-tuple-element.43.refs_5_), channel_id=1, source_target_pairs={{0,192},{32,224},{64,0},{96,32},{128,64},{160,96},{192,128},{224,1... | collective-permute-start | bytes 61448 | tf_op jit(solution)/shard_map/ppermute | solution.py:519
  54.0 1.9 %edge_part.3 = (f32[2,32,16,256]{3,2,1,0:T(8,128)}, f32[2,32,2,16,128]{4,3,2,1,0:T(8,128)S(1)}) custom-call(f32[784,128]{1,0:T(8,128)S(1)} %collective-permute-done.8.refs_0_.pair, f32[784,128]{1,0:T(8,128)S(1)} %collective-permute-done.9.refs_1_.after_pair, f32[2,32,2,16,128]{4,3,2,1,0:T(8,128)S(1)} %local_part.3.refs_2_.local, ...), custom_call_target="tpu_custom_call" | custom-call | bytes 6000000 | tf_op jit(solution)/shard_map/edge_part/pallas_call | solution.py:554
  55.9 2.5 %collective-permute-done.15.refs_4_ = f32[40,128]{1,0:T(8,128)S(1)} collective-permute-done((f32[40,128]{1,0:T(8,128)S(1)}, f32[40,128]{1,0:T(8,128)S(1)}, u32[]{:S(2)}, u32[]{:S(2)}) %collective-permute-start.15) | collective-permute-done | bytes 20512 | tf_op jit(solution)/shard_map/ppermute | solution.py:519
  58.4 3.6 %last_part.1 = f32[2,32,16,256]{3,2,1,0:T(8,128)} custom-call(f32[2,32,2,16,128]{4,3,2,1,0:T(8,128)S(1)} %get-tuple-element.37.refs_0_, f32[424,128]{1,0:T(8,128)S(1)} %collective-permute-done.12.refs_1_, f32[424,128]{1,0:T(8,128)S(1)} %collective-permute-done.13.refs_2_, f32[40,128]{1,0:T(8,128)S(1)} %collective-permute-done.14.refs_3_, ...), custom_call_target="tpu_custom_call" | custom-call | bytes 18000000 | tf_op jit(solution)/shard_map/last_part/pallas_call | solution.py:613
  (35 shorter events, 0.7 us)
Async XLA Ops:
  0.6 10.1 %copy-start = (f32[2,32,16,256]{3,2,1,0:T(8,128)S(1)}, f32[2,32,16,256]{3,2,1,0:T(8,128)}, u32[]{:S(2)}) copy-start(f32[2,32,16,256]{3,2,1,0:T(8,128)} %refs_2_.1) | copy-start | bytes 3145732
  0.6 10.1 %copy-start.2 = (f32[32,16,256]{2,1,0:T(8,128)S(1)}, f32[32,16,256]{2,1,0:T(8,128)}, u32[]{:S(2)}) copy-start(f32[32,16,256]{2,1,0:T(8,128)} %refs_1_.3) | copy-start | bytes 1572868
  5.1 11.7 %collective-permute-start = (f32[784,128]{1,0:T(8,128)}, f32[784,128]{1,0:T(8,128)S(1)}, u32[]{:S(2)}, u32[]{:S(2)}) collective-permute-start(f32[784,128]{1,0:T(8,128)} %get-tuple-element.23), channel_id=1, source_target_pairs={{0,1},{1,0},{2,3},{3,2},{4,5},{5,4},{6,7},{7,6},{8,9},{9,8},{10,11... | collective-permute-start | bytes 1204232 | tf_op jit(solution)/shard_map/ppermute | solution.py:528
  5.2 11.6 %collective-permute-start.1 = (f32[784,128]{1,0:T(8,128)}, f32[784,128]{1,0:T(8,128)S(1)}, u32[]{:S(2)}, u32[]{:S(2)}) collective-permute-start(f32[784,128]{1,0:T(8,128)} %get-tuple-element.24), channel_id=1, source_target_pairs={{0,31},{1,2},{2,1},{3,4},{4,3},{5,6},{6,5},{7,8},{8,7},{9,10},{10,... | collective-permute-start | bytes 1204232 | tf_op jit(solution)/shard_map/ppermute | solution.py:528
  6.0 10.8 %copy-start.3 = (f32[424,128]{1,0:T(8,128)S(1)}, f32[424,128]{1,0:T(8,128)}, u32[]{:S(2)}) copy-start(f32[424,128]{1,0:T(8,128)} %get-tuple-element.28.x_up_in) | copy-start | bytes 651268
  6.0 10.8 %copy-start.4 = (f32[424,128]{1,0:T(8,128)S(1)}, f32[424,128]{1,0:T(8,128)}, u32[]{:S(2)}) copy-start(f32[424,128]{1,0:T(8,128)} %get-tuple-element.29.x_down_in) | copy-start | bytes 651268
  6.0 10.8 %copy-start.7 = (f32[8,128]{1,0:T(8,128)S(1)}, f32[8,128]{1,0:T(8,128)}, u32[]{:S(2)}) copy-start(f32[8,128]{1,0:T(8,128)} %get-tuple-element.27.part) | copy-start | bytes 12292
  6.0 6.6 %collective-permute-start.2 = (f32[8,128]{1,0:T(8,128)}, f32[8,128]{1,0:T(8,128)S(1)}, u32[]{:S(2)}, u32[]{:S(2)}) collective-permute-start(f32[8,128]{1,0:T(8,128)} %get-tuple-element.27.part), channel_id=1, source_target_pairs={{0,2},{1,3},{2,0},{3,1},{4,6},{5,7},{6,4},{7,5},{8,10},{9,11},{10,... | collective-permute-start | bytes 12296 | tf_op jit(solution)/shard_map/ppermute | solution.py:528
  6.5 10.3 %collective-permute-start.3 = (f32[8,128]{1,0:T(8,128)}, f32[8,128]{1,0:T(8,128)S(1)}, u32[]{:S(2)}, u32[]{:S(2)}) collective-permute-start(f32[8,128]{1,0:T(8,128)} %get-tuple-element.27.part), channel_id=1, source_target_pairs={{0,30},{1,31},{2,4},{3,5},{4,2},{5,3},{6,8},{7,9},{8,6},{9,7},{10,... | collective-permute-start | bytes 12296 | tf_op jit(solution)/shard_map/ppermute | solution.py:528
  17.1 13.0 %collective-permute-start.4 = (f32[424,128]{1,0:T(8,128)S(1)}, f32[424,128]{1,0:T(8,128)S(1)}, u32[]{:S(2)}, u32[]{:S(2)}) collective-permute-start(f32[424,128]{1,0:T(8,128)S(1)} %get-tuple-element.30), channel_id=1, source_target_pairs={{0,32},{32,64},{64,96},{96,128},{128,160},{160,192},{192,224},{224... | collective-permute-start | bytes 651272 | tf_op jit(solution)/shard_map/ppermute | solution.py:519
  19.1 11.0 %collective-permute-start.5 = (f32[424,128]{1,0:T(8,128)S(1)}, f32[424,128]{1,0:T(8,128)S(1)}, u32[]{:S(2)}, u32[]{:S(2)}) collective-permute-start(f32[424,128]{1,0:T(8,128)S(1)} %get-tuple-element.31), channel_id=1, source_target_pairs={{0,224},{32,0},{64,32},{96,64},{128,96},{160,128},{192,160},{224,1... | collective-permute-start | bytes 651272 | tf_op jit(solution)/shard_map/ppermute | solution.py:519
  23.1 7.0 %copy-start.5 = (s32[3,32]{1,0:T(4,128)S(1)}, s32[3,32]{1,0:T(4,128)}, u32[]{:S(2)}) copy-start(s32[3,32]{1,0:T(4,128)} %refs_8_.3) | copy-start | bytes 1156
  23.1 7.0 %copy-start.6 = (s32[32]{0:T(128)S(1)}, s32[32]{0:T(128)}, u32[]{:S(2)}) copy-start(s32[32]{0:T(128)} %refs_9_.3) | copy-start | bytes 388
  23.1 7.0 %copy-start.8 = (f32[9]{0:T(128)S(1)}, f32[9]{0:T(128)}, u32[]{:S(2)}) copy-start(f32[9]{0:T(128)} %refs_7_.3) | copy-start | bytes 112
  23.1 7.0 %collective-permute-start.6 = (f32[40,128]{1,0:T(8,128)S(1)}, f32[40,128]{1,0:T(8,128)S(1)}, u32[]{:S(2)}, u32[]{:S(2)}) collective-permute-start(f32[40,128]{1,0:T(8,128)S(1)} %get-tuple-element.32.refs_5_), channel_id=1, source_target_pairs={{0,64},{32,96},{64,128},{96,160},{128,192},{160,224},{192,0},{224,... | collective-permute-start | bytes 61448 | tf_op jit(solution)/shard_map/ppermute | solution.py:519
  23.2 6.9 %collective-permute-start.7 = (f32[40,128]{1,0:T(8,128)S(1)}, f32[40,128]{1,0:T(8,128)S(1)}, u32[]{:S(2)}, u32[]{:S(2)}) collective-permute-start(f32[40,128]{1,0:T(8,128)S(1)} %get-tuple-element.32.refs_5_), channel_id=1, source_target_pairs={{0,192},{32,224},{64,0},{96,32},{128,64},{160,96},{192,128},{224,1... | collective-permute-start | bytes 61448 | tf_op jit(solution)/shard_map/ppermute | solution.py:519
  34.8 11.5 %collective-permute-start.8 = (f32[784,128]{1,0:T(8,128)S(1)}, f32[784,128]{1,0:T(8,128)S(1)}, u32[]{:S(2)}, u32[]{:S(2)}) collective-permute-start(f32[784,128]{1,0:T(8,128)S(1)} %get-tuple-element.33), channel_id=1, source_target_pairs={{0,1},{1,0},{2,3},{3,2},{4,5},{5,4},{6,7},{7,6},{8,9},{9,8},{10,11... | collective-permute-start | bytes 1204232 | tf_op jit(solution)/shard_map/ppermute | solution.py:528
  34.9 11.4 %collective-permute-start.9 = (f32[784,128]{1,0:T(8,128)S(1)}, f32[784,128]{1,0:T(8,128)S(1)}, u32[]{:S(2)}, u32[]{:S(2)}) collective-permute-start(f32[784,128]{1,0:T(8,128)S(1)} %get-tuple-element.34), channel_id=1, source_target_pairs={{0,31},{1,2},{2,1},{3,4},{4,3},{5,6},{6,5},{7,8},{8,7},{9,10},{10,... | collective-permute-start | bytes 1204232 | tf_op jit(solution)/shard_map/ppermute | solution.py:528
  35.0 7.3 %collective-permute-start.10 = (f32[8,128]{1,0:T(8,128)S(1)}, f32[8,128]{1,0:T(8,128)S(1)}, u32[]{:S(2)}, u32[]{:S(2)}) collective-permute-start(f32[8,128]{1,0:T(8,128)S(1)} %get-tuple-element.38.part), channel_id=1, source_target_pairs={{0,2},{1,3},{2,0},{3,1},{4,6},{5,7},{6,4},{7,5},{8,10},{9,11},{10,... | collective-permute-start | bytes 12296 | tf_op jit(solution)/shard_map/ppermute | solution.py:528
  35.3 11.0 %collective-permute-start.11 = (f32[8,128]{1,0:T(8,128)S(1)}, f32[8,128]{1,0:T(8,128)S(1)}, u32[]{:S(2)}, u32[]{:S(2)}) collective-permute-start(f32[8,128]{1,0:T(8,128)S(1)} %get-tuple-element.38.part), channel_id=1, source_target_pairs={{0,30},{1,31},{2,4},{3,5},{4,2},{5,3},{6,8},{7,9},{8,6},{9,7},{10,... | collective-permute-start | bytes 12296 | tf_op jit(solution)/shard_map/ppermute | solution.py:528
  46.5 11.9 %collective-permute-start.12 = (f32[424,128]{1,0:T(8,128)S(1)}, f32[424,128]{1,0:T(8,128)S(1)}, u32[]{:S(2)}, u32[]{:S(2)}) collective-permute-start(f32[424,128]{1,0:T(8,128)S(1)} %get-tuple-element.41), channel_id=1, source_target_pairs={{0,32},{32,64},{64,96},{96,128},{128,160},{160,192},{192,224},{224... | collective-permute-start | bytes 651272 | tf_op jit(solution)/shard_map/ppermute | solution.py:519
  47.3 11.1 %collective-permute-start.13 = (f32[424,128]{1,0:T(8,128)S(1)}, f32[424,128]{1,0:T(8,128)S(1)}, u32[]{:S(2)}, u32[]{:S(2)}) collective-permute-start(f32[424,128]{1,0:T(8,128)S(1)} %get-tuple-element.42), channel_id=1, source_target_pairs={{0,224},{32,0},{64,32},{96,64},{128,96},{160,128},{192,160},{224,1... | collective-permute-start | bytes 651272 | tf_op jit(solution)/shard_map/ppermute | solution.py:519
  49.8 6.1 %collective-permute-start.14 = (f32[40,128]{1,0:T(8,128)S(1)}, f32[40,128]{1,0:T(8,128)S(1)}, u32[]{:S(2)}, u32[]{:S(2)}) collective-permute-start(f32[40,128]{1,0:T(8,128)S(1)} %get-tuple-element.43.refs_5_), channel_id=1, source_target_pairs={{0,64},{32,96},{64,128},{96,160},{128,192},{160,224},{192,0},{224,... | collective-permute-start | bytes 61448 | tf_op jit(solution)/shard_map/ppermute | solution.py:519
  52.8 5.6 %collective-permute-start.15 = (f32[40,128]{1,0:T(8,128)S(1)}, f32[40,128]{1,0:T(8,128)S(1)}, u32[]{:S(2)}, u32[]{:S(2)}) collective-permute-start(f32[40,128]{1,0:T(8,128)S(1)} %get-tuple-element.43.refs_5_), channel_id=1, source_target_pairs={{0,192},{32,224},{64,0},{96,32},{128,64},{160,96},{192,128},{224,1... | collective-permute-start | bytes 61448 | tf_op jit(solution)/shard_map/ppermute | solution.py:519
  (1 other events, 7.0 us)

commit v4 on v3

--- a/solution.py
+++ b/solution.py
@@ -84,9 +84,16 @@
     return offset_ref[0, slot], offset_ref[1, slot], z // LANES, z % LANES
 
 
-def project(work, proj_ref, offset_ref, atom_ref, part):
-    lane = iota((1, 8, LANES), 2)
-    group_of_lane = lane // 16
+def rotate(work, rotated):
+    for o in range(ORB):
+        for x in range(CX):
+            for half in range(2):
+                for t in range(2):
+                    rows = slice(8 * t, 8 * t + 8)
+                    rotated[o, x, half, rows, :] = turned(work[o, x, half, rows, :], 16 * (x % 8))
+
+
+def project(rotated, proj_ref, offset_ref, atom_ref, part):
     flat_lane = iota((BLOCK, LANES), 1)
     flat_row = iota((BLOCK, LANES), 0)
     block = jnp.zeros((BLOCK, LANES), F32)
@@ -94,19 +101,25 @@
         place = (flat_row == s // 8) & (flat_lane == ATOM_LANE + s % 8)
         block = jnp.where(place, atom_ref[s].astype(F32), block)
 
-    def group_step(g, block):
-        patches = [jnp.zeros((8, 8, LANES), F32) for _ in range(ORB)]
+    for g in range(GROUPS):
+        slots = [[None] * 8 for _ in range(ORB)]
         for i in range(8):
             x, y, half, z = corner(offset_ref, g * 8 + i)
-            shift = (16 * i + LANES - z) % LANES
+            place = flat_lane + (LANES - z)
+            window = (place // 16 - x) & 7
+            near = place % 16 < LANES - z
+            shift = (4 * LANES + LANES - z - 16 * x) % LANES
             for o in range(ORB):
-                near = work[o, pl.ds(x, 8), half, pl.ds(y, 8), :]
-                far = work[o, pl.ds(x, 8), 1, pl.ds(y, 8), :]
-                window = pltpu.roll(jnp.where(lane >= z, near, far), shift, 2)
-                patches[o] = jnp.where(group_of_lane == i, window, patches[o])
-        patches = [swap_groups(patch) for patch in patches]
+                low = rotated[o, x, half, pl.ds(y, 8), :]
+                high = rotated[o, x, 1, pl.ds(y, 8), :]
+                for a in range(1, 8):
+                    here = window == a
+                    low = jnp.where(here, rotated[o, x + a, half, pl.ds(y, 8), :], low)
+                    high = jnp.where(here, rotated[o, x + a, 1, pl.ds(y, 8), :], high)
+                slots[o][i] = pltpu.roll(jnp.where(near, low, high), shift, 1)
+        patches = [swap_list_group(swap_list_row(tiles)) for tiles in slots]
         tile = jnp.zeros((8, LANES), F32)
-        rows = pl.ds(pl.multiple_of(g * 8, 8), 8)
+        rows = slice(8 * g, 8 * g + 8)
         for p in range(NPROJ):
             values = [proj_ref[p, rows, LANES * a : LANES * (a + 1)] for a in range(8)]
             for o in range(ORB):
@@ -115,9 +128,9 @@
                     total = total + values[a] * patches[o][a]
                 summed = jnp.sum(total, axis=1, keepdims=True)
                 tile = jnp.where(flat_lane == 2 * p + o, summed, tile)
-        return block + pltpu.roll(tile, g * WIDTH, 1)
-
-    part[...] = lax.fori_loop(0, GROUPS, group_step, block, unroll=True)
+        block = block + turned(tile, g * WIDTH)
+
+    part[...] = block
 
 
 def pack_y(work, part, up, down):
@@ -145,7 +158,8 @@
 
 
 def first_kernel(v, proj_hbm, offset_hbm, atom_hbm, y_pair, y_next, x_up, x_down, part,
-                 work, proj_ref, offset_ref, atom_ref, block, packed, xs_up, xs_down, sems):
+                 work, rotated, proj_ref, offset_ref, atom_ref, block, packed, xs_up, xs_down,
+                 sems):
     copies = [
         pltpu.make_async_copy(v.at[:, :, :, 0:LANES], work.at[:, :, 0], sems.at[0]),
         pltpu.make_async_copy(v.at[:, :, :, LANES:NZ], work.at[:, :, 1], sems.at[1]),
@@ -175,9 +189,10 @@
     ]
     for copy in halos:
         copy.start()
+    rotate(work, rotated)
     for copy in copies[2:]:
         copy.wait()
-    project(work, proj_ref, offset_ref, atom_ref, block)
+    project(rotated, proj_ref, offset_ref, atom_ref, block)
     blocks = [
         pltpu.make_async_copy(block, target.at[pl.ds(0, BLOCK)], sems.at[9 + k])
         for k, target in enumerate((y_pair, y_next, part))
@@ -468,10 +483,11 @@
 
 def middle_kernel(scale, local, before_ref, after_ref, two_before, two_after, column, proj_ref,
                   strength_ref, offset_ref, atom_ref, work, y_pair, y_next, x_up, x_down, part,
-                  *scratch):
+                  rotated, *scratch):
     finish(scale, local, before_ref, after_ref, two_before, two_after, column, proj_ref,
            strength_ref, offset_ref, atom_ref, work, *scratch)
-    project(work, proj_ref, offset_ref, atom_ref, part)
+    rotate(work, rotated)
+    project(rotated, proj_ref, offset_ref, atom_ref, part)
     pack_x(work, x_up, x_down)
     odd = is_odd()
 
@@ -486,10 +502,19 @@
 
 def last_kernel(scale, local, before_ref, after_ref, two_before, two_after, column, proj_ref,
                 strength_ref, offset_ref, atom_ref, out, work, *scratch):
+    *scratch, sems = scratch
     finish(scale, local, before_ref, after_ref, two_before, two_after, column, proj_ref,
            strength_ref, offset_ref, atom_ref, work, *scratch)
-    for half in range(2):
-        out[:, :, :, LANES * half : LANES * (half + 1)] = work[:, :, half]
+    copies = [
+        pltpu.make_async_copy(
+            work.at[:, :, half], out.at[:, :, :, LANES * half : LANES * (half + 1)], sems.at[half]
+        )
+        for half in range(2)
+    ]
+    for copy in copies:
+        copy.start()
+    for copy in copies:
+        copy.wait()
 
 
 def shaped(*shape):
@@ -614,8 +639,10 @@
         end_body,
         out_shape=shaped(*FIELD) if second else (shaped(*WORK),) + SENT,
         in_specs=[VMEM] * 7 + [SMEM] * 3,
-        out_specs=VMEM if second else (VMEM,) * 6,
-        scratch_shapes=([pltpu.VMEM(WORK, F32)] if second else []) + scratch,
+        out_specs=HBM if second else (VMEM,) * 6,
+        scratch_shapes=[pltpu.VMEM(WORK, F32)]
+        + scratch
+        + ([pltpu.SemaphoreType.DMA((2,))] if second else []),
         compiler_params=PARAMS,
         cost_estimate=cost(6),
         name="last_part" if second else "middle_part",
@@ -633,6 +660,7 @@
         in_specs=[HBM] * 4,
         out_specs=(HBM,) * 5,
         scratch_shapes=[
+            pltpu.VMEM(WORK, F32),
             pltpu.VMEM(WORK, F32),
             pltpu.VMEM((NPROJ, SLOTS, 8 * LANES), F32),
             pltpu.SMEM((3, SLOTS), jnp.int32),

time: 61.9 us -> 60.6 us (0.979)
  Pallas kernels: 20.9 us -> 19.2 us
    pallas_call x1, Pallas kernels: 4.44 us -> 3.38 us  [shards(): pl.pallas_call(first_kernel, out_shape=SENT, in_specs=[HBM] * 4, out_spec...]
  transfers between devices with their start and end apart: 16 -> 16, of which waited for: 4 -> 4; matrix products, arithmetic and copies ran while one was open for 0% -> 0% of each run, Pallas kernels for 12% -> 13%
where the time goes in v4:
time: 60.6 us; the launch traced here: 60.5 us
  starting transfers between devices  28.9 us (48%)
  Pallas kernels  19.2 us (32%)
  waiting for transfers between devices  11.4 us (19%)
  between operations  1.01 us (2%)
    ppermute x8, starting transfers between devices, shift(): lax.ppermute(value, axis, [(i, (i + step) % devices) for i in range(devic...  17.7 us
    ppermute x8, starting transfers between devices, swapped(): return lax.ppermute(value, 'gy', pairs)  11.2 us
    ppermute x8, waiting for transfers between devices, swapped(): return lax.ppermute(value, 'gy', pairs)  8.09 us
    pallas_call x2, Pallas kernels, apply(): pl.pallas_call(end_body, out_shape=shaped(*FIELD) if second else (shaped(...  7.7 us
    pallas_call x2, Pallas kernels, local_part(): pl.pallas_call(local_body, out_shape=shaped(*WORK), in_specs=[VMEM] * len...  3.84 us
    pallas_call x2, Pallas kernels, edge_part(): pl.pallas_call(edge_body, out_shape=(shaped(*FIELD), shaped(*WORK)) if se...  3.82 us
    pallas_call x1, Pallas kernels, shards(): pl.pallas_call(first_kernel, out_shape=SENT, in_specs=[HBM] * 4, out_spec...  3.38 us
    ppermute x8, waiting for transfers between devices, shift(): lax.ppermute(value, axis, [(i, (i + step) % devices) for i in range(devic...  3.27 us
  transfers between devices with their start and end apart: 16, of which 4 were waited for; matrix products, arithmetic and copies ran while one was open for 0% of the time, Pallas kernels for 13%

profile of v4, /device:TPU:30, one launch (start us, length us, event | category | flops | bytes accessed | tf_op | source)
XLA Modules:
  0.0 60.5 jit_solution(2701256925919956141)
XLA Ops:
  0.6 3.4 %first_part.1 = (f32[784,128]{1,0:T(8,128)}, f32[784,128]{1,0:T(8,128)}, f32[424,128]{1,0:T(8,128)}, f32[424,128]{1,0:T(8,128)}, f32[8,128]{1,0:T(8,128)}) custom-call(f32[2,32,16,256]{3,2,1,0:T(8,128)} %refs_2_.1, f32[9,32,1024]{2,1,0:T(8,128)} %bitcast.1, s32[3,32]{1,0:T(4,128)} %refs_8_.3, s32[32]{0:T(128)} %refs_9_.3), custom_call_target="tpu_custom_call" | custom-call | bytes 9000000 | tf_op jit(solution)/shard_map/first_part/pallas_call | solution.py:657
  4.1 0.9 %collective-permute-start.1 = (f32[784,128]{1,0:T(8,128)}, f32[784,128]{1,0:T(8,128)S(1)}, u32[]{:S(2)}, u32[]{:S(2)}) collective-permute-start(f32[784,128]{1,0:T(8,128)} %get-tuple-element.24), channel_id=1, source_target_pairs={{0,31},{1,2},{2,1},{3,4},{4,3},{5,6},{6,5},{7,8},{8,7},{9,10},{10,... | collective-permute-start | bytes 1204232 | tf_op jit(solution)/shard_map/ppermute | solution.py:553
  5.0 0.5 collective-permute-start.2
  5.5 4.2 %collective-permute-start.3 = (f32[8,128]{1,0:T(8,128)}, f32[8,128]{1,0:T(8,128)S(1)}, u32[]{:S(2)}, u32[]{:S(2)}) collective-permute-start(f32[8,128]{1,0:T(8,128)} %get-tuple-element.27.part), channel_id=1, source_target_pairs={{0,30},{1,31},{2,4},{3,5},{4,2},{5,3},{6,8},{7,9},{8,6},{9,7},{10,... | collective-permute-start | bytes 12296 | tf_op jit(solution)/shard_map/ppermute | solution.py:553
  9.7 1.9 %local_part.2.refs_2_.local = f32[2,32,2,16,128]{4,3,2,1,0:T(8,128)S(1)} custom-call(f32[2,32,16,256]{3,2,1,0:T(8,128)S(1)} %copy-done, f32[32,16,256]{2,1,0:T(8,128)S(1)} %copy-done.2), custom_call_target="tpu_custom_call" | custom-call | bytes 12000000 | tf_op jit(solution)/shard_map/local_part/pallas_call | solution.py:563
  11.6 4.1 %collective-permute-done.3.after_chips = f32[8,128]{1,0:T(8,128)S(1)} collective-permute-done((f32[8,128]{1,0:T(8,128)}, f32[8,128]{1,0:T(8,128)S(1)}, u32[]{:S(2)}, u32[]{:S(2)}) %collective-permute-start.3) | collective-permute-done | bytes 4128 | tf_op jit(solution)/shard_map/ppermute | solution.py:553
  15.8 0.2 gather_part.2
  16.0 2.0 %collective-permute-start.4 = (f32[424,128]{1,0:T(8,128)S(1)}, f32[424,128]{1,0:T(8,128)S(1)}, u32[]{:S(2)}, u32[]{:S(2)}) collective-permute-start(f32[424,128]{1,0:T(8,128)S(1)} %get-tuple-element.30), channel_id=1, source_target_pairs={{0,32},{32,64},{64,96},{96,128},{128,160},{160,192},{192,224},{224... | collective-permute-start | bytes 651272 | tf_op jit(solution)/shard_map/ppermute | solution.py:544
  18.0 4.1 %collective-permute-start.5 = (f32[424,128]{1,0:T(8,128)S(1)}, f32[424,128]{1,0:T(8,128)S(1)}, u32[]{:S(2)}, u32[]{:S(2)}) collective-permute-start(f32[424,128]{1,0:T(8,128)S(1)} %get-tuple-element.31), channel_id=1, source_target_pairs={{0,224},{32,0},{64,32},{96,64},{128,96},{160,128},{192,160},{224,1... | collective-permute-start | bytes 651272 | tf_op jit(solution)/shard_map/ppermute | solution.py:544
  22.2 4.1 %collective-permute-start.7 = (f32[40,128]{1,0:T(8,128)S(1)}, f32[40,128]{1,0:T(8,128)S(1)}, u32[]{:S(2)}, u32[]{:S(2)}) collective-permute-start(f32[40,128]{1,0:T(8,128)S(1)} %get-tuple-element.32.refs_5_), channel_id=1, source_target_pairs={{0,192},{32,224},{64,0},{96,32},{128,64},{160,96},{192,128},{224,1... | collective-permute-start | bytes 61448 | tf_op jit(solution)/shard_map/ppermute | solution.py:544
  26.3 1.9 %edge_part.2.refs_0_ = f32[2,32,2,16,128]{4,3,2,1,0:T(8,128)S(1)} custom-call(f32[784,128]{1,0:T(8,128)S(1)} %collective-permute-done.refs_0_.pair, f32[784,128]{1,0:T(8,128)S(1)} %collective-permute-done.1.refs_1_.after_pair, f32[2,32,2,16,128]{4,3,2,1,0:T(8,128)S(1)} %local_part.2.refs_2_.local, f32[2,32,16,256]{3,2,1,0:T(8,128)S(1)} %copy-done), custom_call_target="tpu_custom_call" | custom-call | bytes 6000000 | tf_op jit(solution)/shard_map/edge_part/pallas_call | solution.py:579
  28.2 0.9 %collective-permute-done.6.refs_3_ = f32[40,128]{1,0:T(8,128)S(1)} collective-permute-done((f32[40,128]{1,0:T(8,128)S(1)}, f32[40,128]{1,0:T(8,128)S(1)}, u32[]{:S(2)}, u32[]{:S(2)}) %collective-permute-start.6) | collective-permute-done | bytes 20512 | tf_op jit(solution)/shard_map/ppermute | solution.py:544
  29.1 4.1 %middle_part.1 = (f32[2,32,2,16,128]{4,3,2,1,0:T(8,128)S(1)}, f32[784,128]{1,0:T(8,128)S(1)}, f32[784,128]{1,0:T(8,128)S(1)}, f32[424,128]{1,0:T(8,128)S(1)}, f3...) custom-call(f32[2,32,2,16,128]{4,3,2,1,0:T(8,128)S(1)} %edge_part.2.refs_0_, f32[424,128]{1,0:T(8,128)S(1)} %collective-permute-done.4.refs_1_, ...), custom_call_target="tpu_custom_call" | custom-call | bytes 18000000 | tf_op jit(solution)/shard_map/middle_part/pallas_call | solution.py:638
  33.6 5.3 %collective-permute-start.11 = (f32[8,128]{1,0:T(8,128)S(1)}, f32[8,128]{1,0:T(8,128)S(1)}, u32[]{:S(2)}, u32[]{:S(2)}) collective-permute-start(f32[8,128]{1,0:T(8,128)S(1)} %get-tuple-element.38.part), channel_id=1, source_target_pairs={{0,30},{1,31},{2,4},{3,5},{4,2},{5,3},{6,8},{7,9},{8,6},{9,7},{10,... | collective-permute-start | bytes 12296 | tf_op jit(solution)/shard_map/ppermute | solution.py:553
  38.8 1.9 %local_part.3.refs_2_.local = f32[2,32,2,16,128]{4,3,2,1,0:T(8,128)S(1)} custom-call(f32[2,32,2,16,128]{4,3,2,1,0:T(8,128)S(1)} %get-tuple-element.35.refs_0_.refs_3_, f32[32,16,256]{2,1,0:T(8,128)S(1)} %copy-done.2, f32[2,32,16,256]{3,2,1,0:T(8,128)S(1)} %copy-done), custom_call_target="tpu_custom_call" | custom-call | bytes 12000000 | tf_op jit(solution)/shard_map/local_part/pallas_call | solution.py:563
  40.8 4.0 %collective-permute-done.11.after_chips = f32[8,128]{1,0:T(8,128)S(1)} collective-permute-done((f32[8,128]{1,0:T(8,128)S(1)}, f32[8,128]{1,0:T(8,128)S(1)}, u32[]{:S(2)}, u32[]{:S(2)}) %collective-permute-start.11) | collective-permute-done | bytes 4128 | tf_op jit(solution)/shard_map/ppermute | solution.py:553
  44.8 0.2 gather_part.3
  45.0 1.2 %collective-permute-start.12 = (f32[424,128]{1,0:T(8,128)S(1)}, f32[424,128]{1,0:T(8,128)S(1)}, u32[]{:S(2)}, u32[]{:S(2)}) collective-permute-start(f32[424,128]{1,0:T(8,128)S(1)} %get-tuple-element.41), channel_id=1, source_target_pairs={{0,32},{32,64},{64,96},{96,128},{128,160},{160,192},{192,224},{224... | collective-permute-start | bytes 651272 | tf_op jit(solution)/shard_map/ppermute | solution.py:544
  46.2 2.1 %collective-permute-start.13 = (f32[424,128]{1,0:T(8,128)S(1)}, f32[424,128]{1,0:T(8,128)S(1)}, u32[]{:S(2)}, u32[]{:S(2)}) collective-permute-start(f32[424,128]{1,0:T(8,128)S(1)} %get-tuple-element.42), channel_id=1, source_target_pairs={{0,224},{32,0},{64,32},{96,64},{128,96},{160,128},{192,160},{224,1... | collective-permute-start | bytes 651272 | tf_op jit(solution)/shard_map/ppermute | solution.py:544
  48.3 2.9 %collective-permute-start.14 = (f32[40,128]{1,0:T(8,128)S(1)}, f32[40,128]{1,0:T(8,128)S(1)}, u32[]{:S(2)}, u32[]{:S(2)}) collective-permute-start(f32[40,128]{1,0:T(8,128)S(1)} %get-tuple-element.43.refs_5_), channel_id=1, source_target_pairs={{0,64},{32,96},{64,128},{96,160},{128,192},{160,224},{192,0},{224,... | collective-permute-start | bytes 61448 | tf_op jit(solution)/shard_map/ppermute | solution.py:544
  51.2 1.2 %collective-permute-start.15 = (f32[40,128]{1,0:T(8,128)S(1)}, f32[40,128]{1,0:T(8,128)S(1)}, u32[]{:S(2)}, u32[]{:S(2)}) collective-permute-start(f32[40,128]{1,0:T(8,128)S(1)} %get-tuple-element.43.refs_5_), channel_id=1, source_target_pairs={{0,192},{32,224},{64,0},{96,32},{128,64},{160,96},{192,128},{224,1... | collective-permute-start | bytes 61448 | tf_op jit(solution)/shard_map/ppermute | solution.py:544
  52.5 1.9 %edge_part.3 = (f32[2,32,16,256]{3,2,1,0:T(8,128)}, f32[2,32,2,16,128]{4,3,2,1,0:T(8,128)S(1)}) custom-call(f32[784,128]{1,0:T(8,128)S(1)} %collective-permute-done.8.refs_0_.pair, f32[784,128]{1,0:T(8,128)S(1)} %collective-permute-done.9.refs_1_.after_pair, f32[2,32,2,16,128]{4,3,2,1,0:T(8,128)S(1)} %local_part.3.refs_2_.local, ...), custom_call_target="tpu_custom_call" | custom-call | bytes 6000000 | tf_op jit(solution)/shard_map/edge_part/pallas_call | solution.py:579
  54.4 2.4 %collective-permute-done.15.refs_4_ = f32[40,128]{1,0:T(8,128)S(1)} collective-permute-done((f32[40,128]{1,0:T(8,128)S(1)}, f32[40,128]{1,0:T(8,128)S(1)}, u32[]{:S(2)}, u32[]{:S(2)}) %collective-permute-start.15) | collective-permute-done | bytes 20512 | tf_op jit(solution)/shard_map/ppermute | solution.py:544
  56.8 3.6 %last_part.1 = f32[2,32,16,256]{3,2,1,0:T(8,128)} custom-call(f32[2,32,2,16,128]{4,3,2,1,0:T(8,128)S(1)} %get-tuple-element.37.refs_0_, f32[424,128]{1,0:T(8,128)S(1)} %collective-permute-done.12.refs_1_, f32[424,128]{1,0:T(8,128)S(1)} %collective-permute-done.13.refs_2_, f32[40,128]{1,0:T(8,128)S(1)} %collective-permute-done.14.refs_3_, ...), custom_call_target="tpu_custom_call" | custom-call | bytes 18000000 | tf_op jit(solution)/shard_map/last_part/pallas_call | solution.py:638
  (35 shorter events, 0.5 us)
Async XLA Ops:
  0.6 9.1 %copy-start = (f32[2,32,16,256]{3,2,1,0:T(8,128)S(1)}, f32[2,32,16,256]{3,2,1,0:T(8,128)}, u32[]{:S(2)}) copy-start(f32[2,32,16,256]{3,2,1,0:T(8,128)} %refs_2_.1) | copy-start | bytes 3145732
  0.6 9.1 %copy-start.2 = (f32[32,16,256]{2,1,0:T(8,128)S(1)}, f32[32,16,256]{2,1,0:T(8,128)}, u32[]{:S(2)}) copy-start(f32[32,16,256]{2,1,0:T(8,128)} %refs_1_.3) | copy-start | bytes 1572868
  4.0 11.7 %collective-permute-start = (f32[784,128]{1,0:T(8,128)}, f32[784,128]{1,0:T(8,128)S(1)}, u32[]{:S(2)}, u32[]{:S(2)}) collective-permute-start(f32[784,128]{1,0:T(8,128)} %get-tuple-element.23), channel_id=1, source_target_pairs={{0,1},{1,0},{2,3},{3,2},{4,5},{5,4},{6,7},{7,6},{8,9},{9,8},{10,11... | collective-permute-start | bytes 1204232 | tf_op jit(solution)/shard_map/ppermute | solution.py:553
  4.1 11.6 %collective-permute-start.1 = (f32[784,128]{1,0:T(8,128)}, f32[784,128]{1,0:T(8,128)S(1)}, u32[]{:S(2)}, u32[]{:S(2)}) collective-permute-start(f32[784,128]{1,0:T(8,128)} %get-tuple-element.24), channel_id=1, source_target_pairs={{0,31},{1,2},{2,1},{3,4},{4,3},{5,6},{6,5},{7,8},{8,7},{9,10},{10,... | collective-permute-start | bytes 1204232 | tf_op jit(solution)/shard_map/ppermute | solution.py:553
  5.0 10.7 %copy-start.3 = (f32[424,128]{1,0:T(8,128)S(1)}, f32[424,128]{1,0:T(8,128)}, u32[]{:S(2)}) copy-start(f32[424,128]{1,0:T(8,128)} %get-tuple-element.28.x_up_in) | copy-start | bytes 651268
  5.0 10.7 %copy-start.4 = (f32[424,128]{1,0:T(8,128)S(1)}, f32[424,128]{1,0:T(8,128)}, u32[]{:S(2)}) copy-start(f32[424,128]{1,0:T(8,128)} %get-tuple-element.29.x_down_in) | copy-start | bytes 651268
  5.0 10.7 %copy-start.7 = (f32[8,128]{1,0:T(8,128)S(1)}, f32[8,128]{1,0:T(8,128)}, u32[]{:S(2)}) copy-start(f32[8,128]{1,0:T(8,128)} %get-tuple-element.27.part) | copy-start | bytes 12292
  5.0 6.6 %collective-permute-start.2 = (f32[8,128]{1,0:T(8,128)}, f32[8,128]{1,0:T(8,128)S(1)}, u32[]{:S(2)}, u32[]{:S(2)}) collective-permute-start(f32[8,128]{1,0:T(8,128)} %get-tuple-element.27.part), channel_id=1, source_target_pairs={{0,2},{1,3},{2,0},{3,1},{4,6},{5,7},{6,4},{7,5},{8,10},{9,11},{10,... | collective-permute-start | bytes 12296 | tf_op jit(solution)/shard_map/ppermute | solution.py:553
  5.5 10.3 %collective-permute-start.3 = (f32[8,128]{1,0:T(8,128)}, f32[8,128]{1,0:T(8,128)S(1)}, u32[]{:S(2)}, u32[]{:S(2)}) collective-permute-start(f32[8,128]{1,0:T(8,128)} %get-tuple-element.27.part), channel_id=1, source_target_pairs={{0,30},{1,31},{2,4},{3,5},{4,2},{5,3},{6,8},{7,9},{8,6},{9,7},{10,... | collective-permute-start | bytes 12296 | tf_op jit(solution)/shard_map/ppermute | solution.py:553
  16.0 13.1 %collective-permute-start.4 = (f32[424,128]{1,0:T(8,128)S(1)}, f32[424,128]{1,0:T(8,128)S(1)}, u32[]{:S(2)}, u32[]{:S(2)}) collective-permute-start(f32[424,128]{1,0:T(8,128)S(1)} %get-tuple-element.30), channel_id=1, source_target_pairs={{0,32},{32,64},{64,96},{96,128},{128,160},{160,192},{192,224},{224... | collective-permute-start | bytes 651272 | tf_op jit(solution)/shard_map/ppermute | solution.py:544
  18.0 11.1 %collective-permute-start.5 = (f32[424,128]{1,0:T(8,128)S(1)}, f32[424,128]{1,0:T(8,128)S(1)}, u32[]{:S(2)}, u32[]{:S(2)}) collective-permute-start(f32[424,128]{1,0:T(8,128)S(1)} %get-tuple-element.31), channel_id=1, source_target_pairs={{0,224},{32,0},{64,32},{96,64},{128,96},{160,128},{192,160},{224,1... | collective-permute-start | bytes 651272 | tf_op jit(solution)/shard_map/ppermute | solution.py:544
  22.1 7.0 %copy-start.5 = (s32[3,32]{1,0:T(4,128)S(1)}, s32[3,32]{1,0:T(4,128)}, u32[]{:S(2)}) copy-start(s32[3,32]{1,0:T(4,128)} %refs_8_.3) | copy-start | bytes 1156
  22.1 7.0 %copy-start.6 = (s32[32]{0:T(128)S(1)}, s32[32]{0:T(128)}, u32[]{:S(2)}) copy-start(s32[32]{0:T(128)} %refs_9_.3) | copy-start | bytes 388
  22.1 7.0 %copy-start.8 = (f32[9]{0:T(128)S(1)}, f32[9]{0:T(128)}, u32[]{:S(2)}) copy-start(f32[9]{0:T(128)} %refs_7_.3) | copy-start | bytes 112
  22.1 7.0 %collective-permute-start.6 = (f32[40,128]{1,0:T(8,128)S(1)}, f32[40,128]{1,0:T(8,128)S(1)}, u32[]{:S(2)}, u32[]{:S(2)}) collective-permute-start(f32[40,128]{1,0:T(8,128)S(1)} %get-tuple-element.32.refs_5_), channel_id=1, source_target_pairs={{0,64},{32,96},{64,128},{96,160},{128,192},{160,224},{192,0},{224,... | collective-permute-start | bytes 61448 | tf_op jit(solution)/shard_map/ppermute | solution.py:544
  22.2 6.9 %collective-permute-start.7 = (f32[40,128]{1,0:T(8,128)S(1)}, f32[40,128]{1,0:T(8,128)S(1)}, u32[]{:S(2)}, u32[]{:S(2)}) collective-permute-start(f32[40,128]{1,0:T(8,128)S(1)} %get-tuple-element.32.refs_5_), channel_id=1, source_target_pairs={{0,192},{32,224},{64,0},{96,32},{128,64},{160,96},{192,128},{224,1... | collective-permute-start | bytes 61448 | tf_op jit(solution)/shard_map/ppermute | solution.py:544
  33.3 11.5 %collective-permute-start.8 = (f32[784,128]{1,0:T(8,128)S(1)}, f32[784,128]{1,0:T(8,128)S(1)}, u32[]{:S(2)}, u32[]{:S(2)}) collective-permute-start(f32[784,128]{1,0:T(8,128)S(1)} %get-tuple-element.33), channel_id=1, source_target_pairs={{0,1},{1,0},{2,3},{3,2},{4,5},{5,4},{6,7},{7,6},{8,9},{9,8},{10,11... | collective-permute-start | bytes 1204232 | tf_op jit(solution)/shard_map/ppermute | solution.py:553
  33.4 11.4 %collective-permute-start.9 = (f32[784,128]{1,0:T(8,128)S(1)}, f32[784,128]{1,0:T(8,128)S(1)}, u32[]{:S(2)}, u32[]{:S(2)}) collective-permute-start(f32[784,128]{1,0:T(8,128)S(1)} %get-tuple-element.34), channel_id=1, source_target_pairs={{0,31},{1,2},{2,1},{3,4},{4,3},{5,6},{6,5},{7,8},{8,7},{9,10},{10,... | collective-permute-start | bytes 1204232 | tf_op jit(solution)/shard_map/ppermute | solution.py:553
  33.5 7.3 %collective-permute-start.10 = (f32[8,128]{1,0:T(8,128)S(1)}, f32[8,128]{1,0:T(8,128)S(1)}, u32[]{:S(2)}, u32[]{:S(2)}) collective-permute-start(f32[8,128]{1,0:T(8,128)S(1)} %get-tuple-element.38.part), channel_id=1, source_target_pairs={{0,2},{1,3},{2,0},{3,1},{4,6},{5,7},{6,4},{7,5},{8,10},{9,11},{10,... | collective-permute-start | bytes 12296 | tf_op jit(solution)/shard_map/ppermute | solution.py:553
  33.6 11.2 %collective-permute-start.11 = (f32[8,128]{1,0:T(8,128)S(1)}, f32[8,128]{1,0:T(8,128)S(1)}, u32[]{:S(2)}, u32[]{:S(2)}) collective-permute-start(f32[8,128]{1,0:T(8,128)S(1)} %get-tuple-element.38.part), channel_id=1, source_target_pairs={{0,30},{1,31},{2,4},{3,5},{4,2},{5,3},{6,8},{7,9},{8,6},{9,7},{10,... | collective-permute-start | bytes 12296 | tf_op jit(solution)/shard_map/ppermute | solution.py:553
  45.0 11.8 %collective-permute-start.12 = (f32[424,128]{1,0:T(8,128)S(1)}, f32[424,128]{1,0:T(8,128)S(1)}, u32[]{:S(2)}, u32[]{:S(2)}) collective-permute-start(f32[424,128]{1,0:T(8,128)S(1)} %get-tuple-element.41), channel_id=1, source_target_pairs={{0,32},{32,64},{64,96},{96,128},{128,160},{160,192},{192,224},{224... | collective-permute-start | bytes 651272 | tf_op jit(solution)/shard_map/ppermute | solution.py:544
  46.2 10.6 %collective-permute-start.13 = (f32[424,128]{1,0:T(8,128)S(1)}, f32[424,128]{1,0:T(8,128)S(1)}, u32[]{:S(2)}, u32[]{:S(2)}) collective-permute-start(f32[424,128]{1,0:T(8,128)S(1)} %get-tuple-element.42), channel_id=1, source_target_pairs={{0,224},{32,0},{64,32},{96,64},{128,96},{160,128},{192,160},{224,1... | collective-permute-start | bytes 651272 | tf_op jit(solution)/shard_map/ppermute | solution.py:544
  48.3 6.1 %collective-permute-start.14 = (f32[40,128]{1,0:T(8,128)S(1)}, f32[40,128]{1,0:T(8,128)S(1)}, u32[]{:S(2)}, u32[]{:S(2)}) collective-permute-start(f32[40,128]{1,0:T(8,128)S(1)} %get-tuple-element.43.refs_5_), channel_id=1, source_target_pairs={{0,64},{32,96},{64,128},{96,160},{128,192},{160,224},{192,0},{224,... | collective-permute-start | bytes 61448 | tf_op jit(solution)/shard_map/ppermute | solution.py:544
  51.2 5.6 %collective-permute-start.15 = (f32[40,128]{1,0:T(8,128)S(1)}, f32[40,128]{1,0:T(8,128)S(1)}, u32[]{:S(2)}, u32[]{:S(2)}) collective-permute-start(f32[40,128]{1,0:T(8,128)S(1)} %get-tuple-element.43.refs_5_), channel_id=1, source_target_pairs={{0,192},{32,224},{64,0},{96,32},{128,64},{160,96},{192,128},{224,1... | collective-permute-start | bytes 61448 | tf_op jit(solution)/shard_map/ppermute | solution.py:544
  (1 other events, 7.0 us)

commit v5 on v4

--- a/solution.py
+++ b/solution.py
@@ -402,9 +402,9 @@
 
 
 def finish(scale, local, before, after, two_before, two_after, column, proj_ref,
-           strength_ref, offset_ref, atom_ref, work, table, held, split):
+           strength_ref, offset_ref, atom_ref, work, table, held, split, extra):
     weights = [scale * KINETIC / HALF_WIDTH * w for w in LAPLACE_COEFFS]
-    work[:, REACH : CX - REACH] = local[:, REACH : CX - REACH]
+    extra[...] = jnp.zeros(WORK, F32)
     count = 0
     for s in range(SLOTS):
         split[count] = s
@@ -433,10 +433,15 @@
                 high = high + weights[REACH + i - j] * after[rows, :].reshape(2, CY, LANES)
             work[o, CX - REACH + j] = high
 
-    lane = iota((1, 8, LANES), 2)
-
-    def group_step(g, carry):
-        rows = pl.ds(pl.multiple_of(g * 8, 8), 8)
+    lane = iota((8, LANES), 1)
+
+    def windows(slot):
+        x, y, half, z = corner(offset_ref, slot)
+        place = lane + (LANES - z)
+        return x, y, half, z, (place // 16 - x) & 7, place % 16 < LANES - z
+
+    for g in range(GROUPS):
+        rows = slice(8 * g, 8 * g + 8)
         factors = table[rows, :]
         added = [[None] * 8 for _ in range(ORB)]
         for p in range(NPROJ):
@@ -450,35 +455,42 @@
                 for o in range(ORB):
                     term = values * spread[o]
                     added[o][a] = term if p == 0 else added[o][a] + term
-        patches = [swap_groups(jnp.stack(added[o])) for o in range(ORB)]
-        for o in range(ORB):
-            held[g, o] = patches[o]
+        slots = [swap_list_row(swap_list_group(added[o])) for o in range(ORB)]
         for i in range(8):
-            x, y, half, z = corner(offset_ref, g * 8 + i)
-            shift = (z + LANES - 16 * i) % LANES
-            inside = (lane >= z) & (lane < z + 16)
-            places = [(o, pl.ds(x, 8), half, pl.ds(y, 8), slice(None)) for o in range(ORB)]
-            sums = [
-                work[places[o]] + jnp.where(inside, pltpu.roll(patches[o], shift, 2), 0.0)
-                for o in range(ORB)
-            ]
+            x, y, half, z, window, near = windows(g * 8 + i)
+            shift = (z + 16 * x) % LANES
+            moved = [pltpu.roll(slots[o][i], shift, 1) for o in range(ORB)]
             for o in range(ORB):
-                work[places[o]] = sums[o]
-        return carry
-
-    lax.fori_loop(0, GROUPS, group_step, 0, unroll=True)
+                held[g, o, i] = moved[o]
+            sums = []
+            for a in range(8):
+                here = (window == a) & near
+                for o in range(ORB):
+                    sums.append(
+                        extra[o, x + a, half, pl.ds(y, 8), :] + jnp.where(here, moved[o], 0.0)
+                    )
+            for a in range(8):
+                for o in range(ORB):
+                    extra[o, x + a, half, pl.ds(y, 8), :] = sums[ORB * a + o]
 
     def split_step(n, carry):
         s = split[n]
-        x, y, half, z = corner(offset_ref, s)
-        shift = (z + LANES - 16 * (s % 8)) % LANES
-        for o in range(ORB):
-            place = (o, pl.ds(x, 8), 1, pl.ds(y, 8), slice(None))
-            moved = pltpu.roll(held[s // 8, o], shift, 2)
-            work[place] = work[place] + jnp.where(lane < z + 16 - LANES, moved, 0.0)
+        x, y, half, z, window, near = windows(s)
+        for a in range(8):
+            here = (window == a) & jnp.logical_not(near)
+            for o in range(ORB):
+                place = (o, x + a, 1, pl.ds(y, 8), slice(None))
+                extra[place] = extra[place] + jnp.where(here, held[s // 8, o, s % 8], 0.0)
         return carry
 
     lax.fori_loop(0, count, split_step, 0)
+    for o in range(ORB):
+        for x in range(CX):
+            base = local if REACH <= x < CX - REACH else work
+            for half in range(2):
+                for t in range(2):
+                    place = (o, x, half, slice(8 * t, 8 * t + 8), slice(None))
+                    work[place] = base[place] + turned(extra[place], -16 * (x % 8))
 
 
 def middle_kernel(scale, local, before_ref, after_ref, two_before, two_after, column, proj_ref,
@@ -634,6 +646,7 @@
         pltpu.VMEM((SLOTS, LANES), F32),
         pltpu.VMEM((GROUPS, ORB, 8, 8, LANES), F32),
         pltpu.SMEM((SLOTS + 1,), jnp.int32),
+        pltpu.VMEM(WORK, F32),
     ]
     result = pl.pallas_call(
         end_body,

time: 60.6 us -> 59.9 us (0.988)
    pallas_call x2, Pallas kernels: 7.7 us -> 7.08 us  [apply(): pl.pallas_call(end_body, out_shape=shaped(*FIELD) if second else (shaped(...]
where the time goes in v5:
time: 59.9 us; the launch traced here: 59.8 us
  starting transfers between devices  28.8 us (48%)
  Pallas kernels  18.6 us (31%)
  waiting for transfers between devices  11.3 us (19%)
  between operations  1.01 us (2%)
    ppermute x8, starting transfers between devices, shift(): lax.ppermute(value, axis, [(i, (i + step) % devices) for i in range(devic...  17.7 us
    ppermute x8, starting transfers between devices, swapped(): return lax.ppermute(value, 'gy', pairs)  11.2 us
    ppermute x8, waiting for transfers between devices, swapped(): return lax.ppermute(value, 'gy', pairs)  8.09 us
    pallas_call x2, Pallas kernels, apply(): pl.pallas_call(end_body, out_shape=shaped(*FIELD) if second else (shaped(...  7.08 us
    pallas_call x2, Pallas kernels, local_part(): pl.pallas_call(local_body, out_shape=shaped(*WORK), in_specs=[VMEM] * len...  3.84 us
    pallas_call x2, Pallas kernels, edge_part(): pl.pallas_call(edge_body, out_shape=(shaped(*FIELD), shaped(*WORK)) if se...  3.82 us
    pallas_call x1, Pallas kernels, shards(): pl.pallas_call(first_kernel, out_shape=SENT, in_specs=[HBM] * 4, out_spec...  3.39 us
    ppermute x8, waiting for transfers between devices, shift(): lax.ppermute(value, axis, [(i, (i + step) % devices) for i in range(devic...  3.24 us
  transfers between devices with their start and end apart: 16, of which 4 were waited for; matrix products, arithmetic and copies ran while one was open for 0% of the time, Pallas kernels for 13%

profile of v5, /device:TPU:30, one launch (start us, length us, event | category | flops | bytes accessed | tf_op | source)
XLA Modules:
  0.0 59.8 jit_solution(18194700845094493998)
XLA Ops:
  0.6 3.4 %first_part.1 = (f32[784,128]{1,0:T(8,128)}, f32[784,128]{1,0:T(8,128)}, f32[424,128]{1,0:T(8,128)}, f32[424,128]{1,0:T(8,128)}, f32[8,128]{1,0:T(8,128)}) custom-call(f32[2,32,16,256]{3,2,1,0:T(8,128)} %refs_2_.1, f32[9,32,1024]{2,1,0:T(8,128)} %bitcast.1, s32[3,32]{1,0:T(4,128)} %refs_8_.3, s32[32]{0:T(128)} %refs_9_.3), custom_call_target="tpu_custom_call" | custom-call | bytes 9000000 | tf_op jit(solution)/shard_map/first_part/pallas_call | solution.py:670
  4.2 0.8 %collective-permute-start.1 = (f32[784,128]{1,0:T(8,128)}, f32[784,128]{1,0:T(8,128)S(1)}, u32[]{:S(2)}, u32[]{:S(2)}) collective-permute-start(f32[784,128]{1,0:T(8,128)} %get-tuple-element.24), channel_id=1, source_target_pairs={{0,31},{1,2},{2,1},{3,4},{4,3},{5,6},{6,5},{7,8},{8,7},{9,10},{10,... | collective-permute-start | bytes 1204232 | tf_op jit(solution)/shard_map/ppermute | solution.py:565
  5.0 0.5 collective-permute-start.2
  5.5 4.2 %collective-permute-start.3 = (f32[8,128]{1,0:T(8,128)}, f32[8,128]{1,0:T(8,128)S(1)}, u32[]{:S(2)}, u32[]{:S(2)}) collective-permute-start(f32[8,128]{1,0:T(8,128)} %get-tuple-element.27.part), channel_id=1, source_target_pairs={{0,30},{1,31},{2,4},{3,5},{4,2},{5,3},{6,8},{7,9},{8,6},{9,7},{10,... | collective-permute-start | bytes 12296 | tf_op jit(solution)/shard_map/ppermute | solution.py:565
  9.7 1.9 %local_part.2.refs_2_.local = f32[2,32,2,16,128]{4,3,2,1,0:T(8,128)S(1)} custom-call(f32[2,32,16,256]{3,2,1,0:T(8,128)S(1)} %copy-done, f32[32,16,256]{2,1,0:T(8,128)S(1)} %copy-done.2), custom_call_target="tpu_custom_call" | custom-call | bytes 12000000 | tf_op jit(solution)/shard_map/local_part/pallas_call | solution.py:575
  11.6 4.1 %collective-permute-done.3.after_chips = f32[8,128]{1,0:T(8,128)S(1)} collective-permute-done((f32[8,128]{1,0:T(8,128)}, f32[8,128]{1,0:T(8,128)S(1)}, u32[]{:S(2)}, u32[]{:S(2)}) %collective-permute-start.3) | collective-permute-done | bytes 4128 | tf_op jit(solution)/shard_map/ppermute | solution.py:565
  15.8 0.2 gather_part.2
  16.0 1.9 %collective-permute-start.4 = (f32[424,128]{1,0:T(8,128)S(1)}, f32[424,128]{1,0:T(8,128)S(1)}, u32[]{:S(2)}, u32[]{:S(2)}) collective-permute-start(f32[424,128]{1,0:T(8,128)S(1)} %get-tuple-element.30), channel_id=1, source_target_pairs={{0,32},{32,64},{64,96},{96,128},{128,160},{160,192},{192,224},{224... | collective-permute-start | bytes 651272 | tf_op jit(solution)/shard_map/ppermute | solution.py:556
  18.0 4.1 %collective-permute-start.5 = (f32[424,128]{1,0:T(8,128)S(1)}, f32[424,128]{1,0:T(8,128)S(1)}, u32[]{:S(2)}, u32[]{:S(2)}) collective-permute-start(f32[424,128]{1,0:T(8,128)S(1)} %get-tuple-element.31), channel_id=1, source_target_pairs={{0,224},{32,0},{64,32},{96,64},{128,96},{160,128},{192,160},{224,1... | collective-permute-start | bytes 651272 | tf_op jit(solution)/shard_map/ppermute | solution.py:556
  22.1 4.1 %collective-permute-start.7 = (f32[40,128]{1,0:T(8,128)S(1)}, f32[40,128]{1,0:T(8,128)S(1)}, u32[]{:S(2)}, u32[]{:S(2)}) collective-permute-start(f32[40,128]{1,0:T(8,128)S(1)} %get-tuple-element.32.refs_5_), channel_id=1, source_target_pairs={{0,192},{32,224},{64,0},{96,32},{128,64},{160,96},{192,128},{224,1... | collective-permute-start | bytes 61448 | tf_op jit(solution)/shard_map/ppermute | solution.py:556
  26.3 1.9 %edge_part.2.refs_0_ = f32[2,32,2,16,128]{4,3,2,1,0:T(8,128)S(1)} custom-call(f32[784,128]{1,0:T(8,128)S(1)} %collective-permute-done.refs_0_.pair, f32[784,128]{1,0:T(8,128)S(1)} %collective-permute-done.1.refs_1_.after_pair, f32[2,32,2,16,128]{4,3,2,1,0:T(8,128)S(1)} %local_part.2.refs_2_.local, f32[2,32,16,256]{3,2,1,0:T(8,128)S(1)} %copy-done), custom_call_target="tpu_custom_call" | custom-call | bytes 6000000 | tf_op jit(solution)/shard_map/edge_part/pallas_call | solution.py:591
  28.2 0.9 %collective-permute-done.6.refs_3_ = f32[40,128]{1,0:T(8,128)S(1)} collective-permute-done((f32[40,128]{1,0:T(8,128)S(1)}, f32[40,128]{1,0:T(8,128)S(1)}, u32[]{:S(2)}, u32[]{:S(2)}) %collective-permute-start.6) | collective-permute-done | bytes 20512 | tf_op jit(solution)/shard_map/ppermute | solution.py:556
  29.1 3.8 %middle_part.1 = (f32[2,32,2,16,128]{4,3,2,1,0:T(8,128)S(1)}, f32[784,128]{1,0:T(8,128)S(1)}, f32[784,128]{1,0:T(8,128)S(1)}, f32[424,128]{1,0:T(8,128)S(1)}, f3...) custom-call(f32[2,32,2,16,128]{4,3,2,1,0:T(8,128)S(1)} %edge_part.2.refs_0_, f32[424,128]{1,0:T(8,128)S(1)} %collective-permute-done.4.refs_1_, ...), custom_call_target="tpu_custom_call" | custom-call | bytes 18000000 | tf_op jit(solution)/shard_map/middle_part/pallas_call | solution.py:651
  33.2 5.3 %collective-permute-start.11 = (f32[8,128]{1,0:T(8,128)S(1)}, f32[8,128]{1,0:T(8,128)S(1)}, u32[]{:S(2)}, u32[]{:S(2)}) collective-permute-start(f32[8,128]{1,0:T(8,128)S(1)} %get-tuple-element.38.part), channel_id=1, source_target_pairs={{0,30},{1,31},{2,4},{3,5},{4,2},{5,3},{6,8},{7,9},{8,6},{9,7},{10,... | collective-permute-start | bytes 12296 | tf_op jit(solution)/shard_map/ppermute | solution.py:565
  38.5 1.9 %local_part.3.refs_2_.local = f32[2,32,2,16,128]{4,3,2,1,0:T(8,128)S(1)} custom-call(f32[2,32,2,16,128]{4,3,2,1,0:T(8,128)S(1)} %get-tuple-element.35.refs_0_.refs_3_, f32[32,16,256]{2,1,0:T(8,128)S(1)} %copy-done.2, f32[2,32,16,256]{3,2,1,0:T(8,128)S(1)} %copy-done), custom_call_target="tpu_custom_call" | custom-call | bytes 12000000 | tf_op jit(solution)/shard_map/local_part/pallas_call | solution.py:575
  40.4 4.0 %collective-permute-done.11.after_chips = f32[8,128]{1,0:T(8,128)S(1)} collective-permute-done((f32[8,128]{1,0:T(8,128)S(1)}, f32[8,128]{1,0:T(8,128)S(1)}, u32[]{:S(2)}, u32[]{:S(2)}) %collective-permute-start.11) | collective-permute-done | bytes 4128 | tf_op jit(solution)/shard_map/ppermute | solution.py:565
  44.4 0.2 gather_part.3
  44.6 0.9 %collective-permute-start.12 = (f32[424,128]{1,0:T(8,128)S(1)}, f32[424,128]{1,0:T(8,128)S(1)}, u32[]{:S(2)}, u32[]{:S(2)}) collective-permute-start(f32[424,128]{1,0:T(8,128)S(1)} %get-tuple-element.41), channel_id=1, source_target_pairs={{0,32},{32,64},{64,96},{96,128},{128,160},{160,192},{192,224},{224... | collective-permute-start | bytes 651272 | tf_op jit(solution)/shard_map/ppermute | solution.py:556
  45.5 2.4 %collective-permute-start.13 = (f32[424,128]{1,0:T(8,128)S(1)}, f32[424,128]{1,0:T(8,128)S(1)}, u32[]{:S(2)}, u32[]{:S(2)}) collective-permute-start(f32[424,128]{1,0:T(8,128)S(1)} %get-tuple-element.42), channel_id=1, source_target_pairs={{0,224},{32,0},{64,32},{96,64},{128,96},{160,128},{192,160},{224,1... | collective-permute-start | bytes 651272 | tf_op jit(solution)/shard_map/ppermute | solution.py:556
  48.0 2.9 %collective-permute-start.14 = (f32[40,128]{1,0:T(8,128)S(1)}, f32[40,128]{1,0:T(8,128)S(1)}, u32[]{:S(2)}, u32[]{:S(2)}) collective-permute-start(f32[40,128]{1,0:T(8,128)S(1)} %get-tuple-element.43.refs_5_), channel_id=1, source_target_pairs={{0,64},{32,96},{64,128},{96,160},{128,192},{160,224},{192,0},{224,... | collective-permute-start | bytes 61448 | tf_op jit(solution)/shard_map/ppermute | solution.py:556
  50.8 1.3 %collective-permute-start.15 = (f32[40,128]{1,0:T(8,128)S(1)}, f32[40,128]{1,0:T(8,128)S(1)}, u32[]{:S(2)}, u32[]{:S(2)}) collective-permute-start(f32[40,128]{1,0:T(8,128)S(1)} %get-tuple-element.43.refs_5_), channel_id=1, source_target_pairs={{0,192},{32,224},{64,0},{96,32},{128,64},{160,96},{192,128},{224,1... | collective-permute-start | bytes 61448 | tf_op jit(solution)/shard_map/ppermute | solution.py:556
  52.1 1.9 %edge_part.3 = (f32[2,32,16,256]{3,2,1,0:T(8,128)}, f32[2,32,2,16,128]{4,3,2,1,0:T(8,128)S(1)}) custom-call(f32[784,128]{1,0:T(8,128)S(1)} %collective-permute-done.8.refs_0_.pair, f32[784,128]{1,0:T(8,128)S(1)} %collective-permute-done.9.refs_1_.after_pair, f32[2,32,2,16,128]{4,3,2,1,0:T(8,128)S(1)} %local_part.3.refs_2_.local, ...), custom_call_target="tpu_custom_call" | custom-call | bytes 6000000 | tf_op jit(solution)/shard_map/edge_part/pallas_call | solution.py:591
  54.0 2.4 %collective-permute-done.15.refs_4_ = f32[40,128]{1,0:T(8,128)S(1)} collective-permute-done((f32[40,128]{1,0:T(8,128)S(1)}, f32[40,128]{1,0:T(8,128)S(1)}, u32[]{:S(2)}, u32[]{:S(2)}) %collective-permute-start.15) | collective-permute-done | bytes 20512 | tf_op jit(solution)/shard_map/ppermute | solution.py:556
  56.4 3.3 %last_part.1 = f32[2,32,16,256]{3,2,1,0:T(8,128)} custom-call(f32[2,32,2,16,128]{4,3,2,1,0:T(8,128)S(1)} %get-tuple-element.37.refs_0_, f32[424,128]{1,0:T(8,128)S(1)} %collective-permute-done.12.refs_1_, f32[424,128]{1,0:T(8,128)S(1)} %collective-permute-done.13.refs_2_, f32[40,128]{1,0:T(8,128)S(1)} %collective-permute-done.14.refs_3_, ...), custom_call_target="tpu_custom_call" | custom-call | bytes 18000000 | tf_op jit(solution)/shard_map/last_part/pallas_call | solution.py:651
  (35 shorter events, 0.5 us)
Async XLA Ops:
  0.6 9.1 %copy-start = (f32[2,32,16,256]{3,2,1,0:T(8,128)S(1)}, f32[2,32,16,256]{3,2,1,0:T(8,128)}, u32[]{:S(2)}) copy-start(f32[2,32,16,256]{3,2,1,0:T(8,128)} %refs_2_.1) | copy-start | bytes 3145732
  0.6 9.1 %copy-start.2 = (f32[32,16,256]{2,1,0:T(8,128)S(1)}, f32[32,16,256]{2,1,0:T(8,128)}, u32[]{:S(2)}) copy-start(f32[32,16,256]{2,1,0:T(8,128)} %refs_1_.3) | copy-start | bytes 1572868
  4.1 11.7 %collective-permute-start = (f32[784,128]{1,0:T(8,128)}, f32[784,128]{1,0:T(8,128)S(1)}, u32[]{:S(2)}, u32[]{:S(2)}) collective-permute-start(f32[784,128]{1,0:T(8,128)} %get-tuple-element.23), channel_id=1, source_target_pairs={{0,1},{1,0},{2,3},{3,2},{4,5},{5,4},{6,7},{7,6},{8,9},{9,8},{10,11... | collective-permute-start | bytes 1204232 | tf_op jit(solution)/shard_map/ppermute | solution.py:565
  4.2 11.6 %collective-permute-start.1 = (f32[784,128]{1,0:T(8,128)}, f32[784,128]{1,0:T(8,128)S(1)}, u32[]{:S(2)}, u32[]{:S(2)}) collective-permute-start(f32[784,128]{1,0:T(8,128)} %get-tuple-element.24), channel_id=1, source_target_pairs={{0,31},{1,2},{2,1},{3,4},{4,3},{5,6},{6,5},{7,8},{8,7},{9,10},{10,... | collective-permute-start | bytes 1204232 | tf_op jit(solution)/shard_map/ppermute | solution.py:565
  5.0 10.8 %copy-start.3 = (f32[424,128]{1,0:T(8,128)S(1)}, f32[424,128]{1,0:T(8,128)}, u32[]{:S(2)}) copy-start(f32[424,128]{1,0:T(8,128)} %get-tuple-element.28.x_up_in) | copy-start | bytes 651268
  5.0 10.8 %copy-start.4 = (f32[424,128]{1,0:T(8,128)S(1)}, f32[424,128]{1,0:T(8,128)}, u32[]{:S(2)}) copy-start(f32[424,128]{1,0:T(8,128)} %get-tuple-element.29.x_down_in) | copy-start | bytes 651268
  5.0 10.8 %copy-start.7 = (f32[8,128]{1,0:T(8,128)S(1)}, f32[8,128]{1,0:T(8,128)}, u32[]{:S(2)}) copy-start(f32[8,128]{1,0:T(8,128)} %get-tuple-element.27.part) | copy-start | bytes 12292
  5.0 6.6 %collective-permute-start.2 = (f32[8,128]{1,0:T(8,128)}, f32[8,128]{1,0:T(8,128)S(1)}, u32[]{:S(2)}, u32[]{:S(2)}) collective-permute-start(f32[8,128]{1,0:T(8,128)} %get-tuple-element.27.part), channel_id=1, source_target_pairs={{0,2},{1,3},{2,0},{3,1},{4,6},{5,7},{6,4},{7,5},{8,10},{9,11},{10,... | collective-permute-start | bytes 12296 | tf_op jit(solution)/shard_map/ppermute | solution.py:565
  5.5 10.2 %collective-permute-start.3 = (f32[8,128]{1,0:T(8,128)}, f32[8,128]{1,0:T(8,128)S(1)}, u32[]{:S(2)}, u32[]{:S(2)}) collective-permute-start(f32[8,128]{1,0:T(8,128)} %get-tuple-element.27.part), channel_id=1, source_target_pairs={{0,30},{1,31},{2,4},{3,5},{4,2},{5,3},{6,8},{7,9},{8,6},{9,7},{10,... | collective-permute-start | bytes 12296 | tf_op jit(solution)/shard_map/ppermute | solution.py:565
  16.0 13.0 %collective-permute-start.4 = (f32[424,128]{1,0:T(8,128)S(1)}, f32[424,128]{1,0:T(8,128)S(1)}, u32[]{:S(2)}, u32[]{:S(2)}) collective-permute-start(f32[424,128]{1,0:T(8,128)S(1)} %get-tuple-element.30), channel_id=1, source_target_pairs={{0,32},{32,64},{64,96},{96,128},{128,160},{160,192},{192,224},{224... | collective-permute-start | bytes 651272 | tf_op jit(solution)/shard_map/ppermute | solution.py:556
  18.0 11.1 %collective-permute-start.5 = (f32[424,128]{1,0:T(8,128)S(1)}, f32[424,128]{1,0:T(8,128)S(1)}, u32[]{:S(2)}, u32[]{:S(2)}) collective-permute-start(f32[424,128]{1,0:T(8,128)S(1)} %get-tuple-element.31), channel_id=1, source_target_pairs={{0,224},{32,0},{64,32},{96,64},{128,96},{160,128},{192,160},{224,1... | collective-permute-start | bytes 651272 | tf_op jit(solution)/shard_map/ppermute | solution.py:556
  22.0 7.0 %copy-start.5 = (s32[3,32]{1,0:T(4,128)S(1)}, s32[3,32]{1,0:T(4,128)}, u32[]{:S(2)}) copy-start(s32[3,32]{1,0:T(4,128)} %refs_8_.3) | copy-start | bytes 1156
  22.0 7.0 %copy-start.6 = (s32[32]{0:T(128)S(1)}, s32[32]{0:T(128)}, u32[]{:S(2)}) copy-start(s32[32]{0:T(128)} %refs_9_.3) | copy-start | bytes 388
  22.0 7.0 %copy-start.8 = (f32[9]{0:T(128)S(1)}, f32[9]{0:T(128)}, u32[]{:S(2)}) copy-start(f32[9]{0:T(128)} %refs_7_.3) | copy-start | bytes 112
  22.0 7.0 %collective-permute-start.6 = (f32[40,128]{1,0:T(8,128)S(1)}, f32[40,128]{1,0:T(8,128)S(1)}, u32[]{:S(2)}, u32[]{:S(2)}) collective-permute-start(f32[40,128]{1,0:T(8,128)S(1)} %get-tuple-element.32.refs_5_), channel_id=1, source_target_pairs={{0,64},{32,96},{64,128},{96,160},{128,192},{160,224},{192,0},{224,... | collective-permute-start | bytes 61448 | tf_op jit(solution)/shard_map/ppermute | solution.py:556
  22.1 6.9 %collective-permute-start.7 = (f32[40,128]{1,0:T(8,128)S(1)}, f32[40,128]{1,0:T(8,128)S(1)}, u32[]{:S(2)}, u32[]{:S(2)}) collective-permute-start(f32[40,128]{1,0:T(8,128)S(1)} %get-tuple-element.32.refs_5_), channel_id=1, source_target_pairs={{0,192},{32,224},{64,0},{96,32},{128,64},{160,96},{192,128},{224,1... | collective-permute-start | bytes 61448 | tf_op jit(solution)/shard_map/ppermute | solution.py:556
  32.9 11.5 %collective-permute-start.8 = (f32[784,128]{1,0:T(8,128)S(1)}, f32[784,128]{1,0:T(8,128)S(1)}, u32[]{:S(2)}, u32[]{:S(2)}) collective-permute-start(f32[784,128]{1,0:T(8,128)S(1)} %get-tuple-element.33), channel_id=1, source_target_pairs={{0,1},{1,0},{2,3},{3,2},{4,5},{5,4},{6,7},{7,6},{8,9},{9,8},{10,11... | collective-permute-start | bytes 1204232 | tf_op jit(solution)/shard_map/ppermute | solution.py:565
  33.0 11.4 %collective-permute-start.9 = (f32[784,128]{1,0:T(8,128)S(1)}, f32[784,128]{1,0:T(8,128)S(1)}, u32[]{:S(2)}, u32[]{:S(2)}) collective-permute-start(f32[784,128]{1,0:T(8,128)S(1)} %get-tuple-element.34), channel_id=1, source_target_pairs={{0,31},{1,2},{2,1},{3,4},{4,3},{5,6},{6,5},{7,8},{8,7},{9,10},{10,... | collective-permute-start | bytes 1204232 | tf_op jit(solution)/shard_map/ppermute | solution.py:565
  33.1 7.3 %collective-permute-start.10 = (f32[8,128]{1,0:T(8,128)S(1)}, f32[8,128]{1,0:T(8,128)S(1)}, u32[]{:S(2)}, u32[]{:S(2)}) collective-permute-start(f32[8,128]{1,0:T(8,128)S(1)} %get-tuple-element.38.part), channel_id=1, source_target_pairs={{0,2},{1,3},{2,0},{3,1},{4,6},{5,7},{6,4},{7,5},{8,10},{9,11},{10,... | collective-permute-start | bytes 12296 | tf_op jit(solution)/shard_map/ppermute | solution.py:565
  33.2 11.2 %collective-permute-start.11 = (f32[8,128]{1,0:T(8,128)S(1)}, f32[8,128]{1,0:T(8,128)S(1)}, u32[]{:S(2)}, u32[]{:S(2)}) collective-permute-start(f32[8,128]{1,0:T(8,128)S(1)} %get-tuple-element.38.part), channel_id=1, source_target_pairs={{0,30},{1,31},{2,4},{3,5},{4,2},{5,3},{6,8},{7,9},{8,6},{9,7},{10,... | collective-permute-start | bytes 12296 | tf_op jit(solution)/shard_map/ppermute | solution.py:565
  44.6 11.7 %collective-permute-start.12 = (f32[424,128]{1,0:T(8,128)S(1)}, f32[424,128]{1,0:T(8,128)S(1)}, u32[]{:S(2)}, u32[]{:S(2)}) collective-permute-start(f32[424,128]{1,0:T(8,128)S(1)} %get-tuple-element.41), channel_id=1, source_target_pairs={{0,32},{32,64},{64,96},{96,128},{128,160},{160,192},{192,224},{224... | collective-permute-start | bytes 651272 | tf_op jit(solution)/shard_map/ppermute | solution.py:556
  45.5 10.8 %collective-permute-start.13 = (f32[424,128]{1,0:T(8,128)S(1)}, f32[424,128]{1,0:T(8,128)S(1)}, u32[]{:S(2)}, u32[]{:S(2)}) collective-permute-start(f32[424,128]{1,0:T(8,128)S(1)} %get-tuple-element.42), channel_id=1, source_target_pairs={{0,224},{32,0},{64,32},{96,64},{128,96},{160,128},{192,160},{224,1... | collective-permute-start | bytes 651272 | tf_op jit(solution)/shard_map/ppermute | solution.py:556
  48.0 6.1 %collective-permute-start.14 = (f32[40,128]{1,0:T(8,128)S(1)}, f32[40,128]{1,0:T(8,128)S(1)}, u32[]{:S(2)}, u32[]{:S(2)}) collective-permute-start(f32[40,128]{1,0:T(8,128)S(1)} %get-tuple-element.43.refs_5_), channel_id=1, source_target_pairs={{0,64},{32,96},{64,128},{96,160},{128,192},{160,224},{192,0},{224,... | collective-permute-start | bytes 61448 | tf_op jit(solution)/shard_map/ppermute | solution.py:556
  50.8 5.6 %collective-permute-start.15 = (f32[40,128]{1,0:T(8,128)S(1)}, f32[40,128]{1,0:T(8,128)S(1)}, u32[]{:S(2)}, u32[]{:S(2)}) collective-permute-start(f32[40,128]{1,0:T(8,128)S(1)} %get-tuple-element.43.refs_5_), channel_id=1, source_target_pairs={{0,192},{32,224},{64,0},{96,32},{128,64},{160,96},{192,128},{224,1... | collective-permute-start | bytes 61448 | tf_op jit(solution)/shard_map/ppermute | solution.py:556
  (1 other events, 7.0 us)
